TPU v7x, 32 devices: a whole 2x2x4 slice. The times are simulated.
32 devices in a mesh: seq: 4 (over x, core), fsdp: 8 (over z, y).
Axes of the slice: x: 2, y: 2, z: 4, core: 2. Of those that a mesh axis runs over, the one named last changes fastest.
Arguments:
- latents: bfloat16 [8, 1024, 1152], P('fsdp', 'seq'), may hold values from -6 to 6
- timesteps: int32 [8], P('fsdp'), may hold values from 0 to 999
- labels: int32 [8], P('fsdp'), may hold values from 0 to 999
- upstream: bfloat16 [8, 1024, 1152], P('fsdp', 'seq'), may hold values from -6 to 6
- time_first: float32 [256, 1152], P('fsdp'), may hold values from -0.375 to 0.375
- time_second: float32 [1152, 1152], P('fsdp'), may hold values from -0.1875 to 0.1875
- class_table: float32 [1000, 1152], P(None, 'fsdp'), may hold values from -1.25 to 1.25
- modulation: float32 [1152, 6912], P(None, 'fsdp'), may hold values from -0.1875 to 0.1875
- attend_in: float32 [1152, 3456], P('fsdp'), may hold values from -0.1875 to 0.1875
- attend_out: float32 [1152, 1152], P('fsdp'), may hold values from -2 to 2
- expand: float32 [1152, 4608], P('fsdp'), may hold values from -0.1875 to 0.1875
- contract: float32 [4608, 1152], P('fsdp'), may hold values from -0.09375 to 0.09375
- biases: float32 [18432], P('fsdp'), may hold values from -1.25 to 1.25
- moment_time_first: float32 [256, 1152], P('fsdp'), may hold values from -0.00012207031 to 0.00012207031
- moment_time_second: float32 [1152, 1152], P('fsdp'), may hold values from -0.00012207031 to 0.00012207031
- moment_class_table: float32 [1000, 1152], P(None, 'fsdp'), may hold values from -0.00012207031 to 0.00012207031
- moment_modulation: float32 [1152, 6912], P(None, 'fsdp'), may hold values from -0.00012207031 to 0.00012207031
- moment_attend_in: float32 [1152, 3456], P('fsdp'), may hold values from -0.00012207031 to 0.00012207031
- moment_attend_out: float32 [1152, 1152], P('fsdp'), may hold values from -0.00012207031 to 0.00012207031
- moment_expand: float32 [1152, 4608], P('fsdp'), may hold values from -0.00012207031 to 0.00012207031
- moment_contract: float32 [4608, 1152], P('fsdp'), may hold values from -0.00012207031 to 0.00012207031
- moment_biases: float32 [18432], P('fsdp'), may hold values from -0.00012207031 to 0.00012207031
- square_time_first: float32 [256, 1152], P('fsdp'), may hold values from 1e-12 to 1e-10
- square_time_second: float32 [1152, 1152], P('fsdp'), may hold values from 1e-12 to 1e-10
- square_class_table: float32 [1000, 1152], P(None, 'fsdp'), may hold values from 1e-12 to 1e-10
- square_modulation: float32 [1152, 6912], P(None, 'fsdp'), may hold values from 1e-12 to 1e-10
- square_attend_in: float32 [1152, 3456], P('fsdp'), may hold values from 1e-12 to 1e-10
- square_attend_out: float32 [1152, 1152], P('fsdp'), may hold values from 1e-12 to 1e-10
- square_expand: float32 [1152, 4608], P('fsdp'), may hold values from 1e-12 to 1e-10
- square_contract: float32 [4608, 1152], P('fsdp'), may hold values from 1e-12 to 1e-10
- square_biases: float32 [18432], P('fsdp'), may hold values from 1e-12 to 1e-10
Outputs:
- output: bfloat16 [8, 1024, 1152], P('fsdp', 'seq')
- input_gradient: float32 [8, 1024, 1152], P('fsdp', 'seq')
- condition_gradient: float32 [8, 1152], P('fsdp')
- norm_before: float32 [], replicated
- gradient_time_first: float32 [256, 1152], P('fsdp')
- gradient_time_second: float32 [1152, 1152], P('fsdp')
- gradient_class_table: float32 [1000, 1152], P(None, 'fsdp')
- gradient_modulation: float32 [1152, 6912], P(None, 'fsdp')
- gradient_attend_in: float32 [1152, 3456], P('fsdp')
- gradient_attend_out: float32 [1152, 1152], P('fsdp')
- gradient_expand: float32 [1152, 4608], P('fsdp')
- gradient_contract: float32 [4608, 1152], P('fsdp')
- gradient_biases: float32 [18432], P('fsdp')
- master_time_first: float32 [256, 1152], P('fsdp')
- master_time_second: float32 [1152, 1152], P('fsdp')
- master_class_table: float32 [1000, 1152], P(None, 'fsdp')
- master_modulation: float32 [1152, 6912], P(None, 'fsdp')
- master_attend_in: float32 [1152, 3456], P('fsdp')
- master_attend_out: float32 [1152, 1152], P('fsdp')
- master_expand: float32 [1152, 4608], P('fsdp')
- master_contract: float32 [4608, 1152], P('fsdp')
- master_biases: float32 [18432], P('fsdp')
- moment_next_time_first: float32 [256, 1152], P('fsdp')
- moment_next_time_second: float32 [1152, 1152], P('fsdp')
- moment_next_class_table: float32 [1000, 1152], P(None, 'fsdp')
- moment_next_modulation: float32 [1152, 6912], P(None, 'fsdp')
- moment_next_attend_in: float32 [1152, 3456], P('fsdp')
- moment_next_attend_out: float32 [1152, 1152], P('fsdp')
- moment_next_expand: float32 [1152, 4608], P('fsdp')
- moment_next_contract: float32 [4608, 1152], P('fsdp')
- moment_next_biases: float32 [18432], P('fsdp')
- square_next_time_first: float32 [256, 1152], P('fsdp')
- square_next_time_second: float32 [1152, 1152], P('fsdp')
- square_next_class_table: float32 [1000, 1152], P(None, 'fsdp')
- square_next_modulation: float32 [1152, 6912], P(None, 'fsdp')
- square_next_attend_in: float32 [1152, 3456], P('fsdp')
- square_next_attend_out: float32 [1152, 1152], P('fsdp')
- square_next_expand: float32 [1152, 4608], P('fsdp')
- square_next_contract: float32 [4608, 1152], P('fsdp')
- square_next_biases: float32 [18432], P('fsdp')
All inputs are finite; a program needn't handle non-finite values.
Results may differ from a plain program's by a relative error of at most 0.012.
The roundings to bfloat16 on the way count: a program that leaves them out, or rounds other values in their place, can miss the bound.
Values may be sent and summed in bfloat16 or wider, within the bound.
A program may use at most 384 MiB of HBM per device.

v0:
```python
from functools import partial
import math

import jax
import jax.numpy as jnp
from jax import lax
from jax.sharding import PartitionSpec as P

H = 16
HD = 72
FREQ = 256
NCLS = 1000
STEP = 10


HIGH = lax.Precision.HIGHEST
norm_eps = 1e-06
beta_one = 0.9
beta_two = 0.999
learn_rate = 0.04
weight_decay = 0.01
adam_eps = 1e-08
clip_limit = 1.0


def layer_norm(value):
    centre = value - jnp.mean(value, axis=-1, keepdims=True)
    spread = jnp.mean(centre * centre, axis=-1, keepdims=True)
    return centre * lax.rsqrt(spread + norm_eps)


def time_features(timesteps):
    half = FREQ // 2
    freqs = jnp.exp(-math.log(10000.0) * jnp.arange(half, dtype=jnp.float32) / half)
    angles = timesteps.astype(jnp.float32)[:, None] * freqs[None, :]
    return jnp.concatenate([jnp.cos(angles), jnp.sin(angles)], axis=-1)


def split_biases(biases, width, hidden):
    widths = [width, width, 6 * width, width, width, width, hidden, width]
    pieces = []
    start = 0
    for length in widths:
        pieces.append(biases[start : start + length])
        start = start + length
    return pieces


def high_dot(left, right):
    return jnp.dot(left, right, precision=HIGH, preferred_element_type=jnp.float32)


def mixed_dot(form, left, right):
    return jnp.einsum(form, left, right, preferred_element_type=jnp.float32)


def attend_block(query_block, keys, values):
    score_scale = 1.0 / math.sqrt(keys.shape[-1])
    scores = mixed_dot("qhd,khd->hqk", query_block, keys) * score_scale
    top = jnp.max(scores, axis=-1, keepdims=True)
    expo = jnp.exp(scores - top)
    total = jnp.sum(expo, axis=-1, keepdims=True)
    probs = (expo / total).astype(jnp.bfloat16)
    mixed = mixed_dot("hqk,khd->qhd", probs, values)
    return (mixed, (top + jnp.log(total))[..., 0])


def attend_latent(parts):
    query, keys, values = parts
    length, heads_here, head_dim = query.shape
    block = min(512, length)
    query_blocks = query.reshape(length // block, block, heads_here, head_dim)
    mixed, log_total = lax.map(partial(attend_block, keys=keys, values=values), query_blocks)
    return (mixed.reshape(length, heads_here * head_dim).astype(jnp.bfloat16), log_total)


def attend_back(parts):
    query, keys, values, d_mixed, log_total = parts
    length, heads_here, head_dim = query.shape
    block = min(512, length)
    count = length // block
    score_scale = 1.0 / math.sqrt(head_dim)

    def back_block(carry, pieces):
        d_keys, d_values = carry
        query_block, d_block, log_block = pieces
        scores = mixed_dot("qhd,khd->hqk", query_block, keys) * score_scale
        probs = jnp.exp(scores - log_block[..., None])
        d_probs = mixed_dot("qhd,khd->hqk", d_block, values)
        delta = jnp.sum(probs * d_probs, axis=-1, keepdims=True)
        d_scores = (probs * (d_probs - delta)).astype(jnp.bfloat16)
        d_query = mixed_dot("hqk,khd->qhd", d_scores, keys) * score_scale
        d_keys = d_keys + mixed_dot("hqk,qhd->khd", d_scores, query_block) * score_scale
        d_values = d_values + mixed_dot("hqk,qhd->khd", probs.astype(jnp.bfloat16), d_block)
        return ((d_keys, d_values), d_query)

    empty = jnp.zeros((length, heads_here, head_dim), jnp.float32)
    blocked = (count, block, heads_here, head_dim)
    (d_keys, d_values), d_query = lax.scan(
        back_block, (empty, empty), (query.reshape(blocked), d_mixed.reshape(blocked), log_total)
    )
    flat = (length, heads_here * head_dim)
    return jnp.stack(
        [d_query.reshape(flat), d_keys.reshape(flat), d_values.reshape(flat)], axis=1
    ).astype(jnp.bfloat16)


def adam_step(weight, moment, square, gradient, factor):
    clipped = gradient * factor
    moment_next = beta_one * moment + (1.0 - beta_one) * clipped
    square_next = beta_two * square + (1.0 - beta_two) * clipped * clipped
    moment_hat = moment_next / (1.0 - beta_one**STEP)
    square_hat = square_next / (1.0 - beta_two**STEP)
    master = weight - learn_rate * (
        moment_hat / (jnp.sqrt(square_hat) + adam_eps) + weight_decay * weight
    )
    return (master, moment_next, square_next)


def per_device(
    latents,
    timesteps,
    labels,
    upstream,
    time_first,
    time_second,
    class_table,
    modulation,
    attend_in,
    attend_out,
    expand,
    contract,
    biases,
    moment_time_first,
    moment_time_second,
    moment_class_table,
    moment_modulation,
    moment_attend_in,
    moment_attend_out,
    moment_expand,
    moment_contract,
    moment_biases,
    square_time_first,
    square_time_second,
    square_class_table,
    square_modulation,
    square_attend_in,
    square_attend_out,
    square_expand,
    square_contract,
    square_biases,
):
    low_type = jnp.bfloat16
    lat_dev, tok_rows, width = latents.shape
    hidden = expand.shape[1]
    seq_count = lax.axis_size("seq")
    heads_here = H // seq_count
    w_first, w_second, w_class, w_mod, w_in, w_out, w_up, w_down, all_bias = (
        lax.all_gather(time_first.astype(low_type), "fsdp", axis=0, tiled=True),
        lax.all_gather(time_second.astype(low_type), "fsdp", axis=0, tiled=True),
        lax.all_gather(class_table.astype(low_type), "fsdp", axis=1, tiled=True),
        lax.all_gather(modulation.astype(low_type), "fsdp", axis=1, tiled=True),
        lax.all_gather(attend_in.astype(low_type), "fsdp", axis=0, tiled=True),
        lax.all_gather(attend_out.astype(low_type), "fsdp", axis=0, tiled=True),
        lax.all_gather(expand.astype(low_type), "fsdp", axis=0, tiled=True),
        lax.all_gather(contract.astype(low_type), "fsdp", axis=0, tiled=True),
        lax.all_gather(biases.astype(low_type), "fsdp", axis=0, tiled=True),
    )
    b_t1, b_t2, b_mod, b_q, b_v, b_out, b_up, b_down = split_biases(all_bias, width, hidden)
    features = time_features(timesteps).astype(low_type)
    hidden_time = jnp.dot(features, w_first, preferred_element_type=jnp.float32) + b_t1
    act_time_f, silu_time_pull = jax.vjp(jax.nn.silu, hidden_time)
    act_time = act_time_f.astype(low_type)
    onehot = (labels[:, None] == jnp.arange(NCLS, dtype=jnp.int32)[None, :]).astype(low_type)
    cond = (
        jnp.dot(act_time, w_second, preferred_element_type=jnp.float32)
        + b_t2
        + jnp.dot(onehot, w_class, preferred_element_type=jnp.float32)
    )
    cond_act_f, silu_cond_pull = jax.vjp(jax.nn.silu, cond)
    cond_act = cond_act_f.astype(low_type)
    mod_values = jnp.dot(cond_act, w_mod, preferred_element_type=jnp.float32) + b_mod
    shift1, scale1, gate1, shift2, scale2, gate2 = jnp.split(mod_values[:, None, :], 6, axis=-1)
    inputs = latents.astype(jnp.float32)
    norm_one, norm_one_pull = jax.vjp(layer_norm, inputs)
    h_attn = (norm_one * (1.0 + scale1) + shift1).astype(low_type)
    qkv_bias = jnp.concatenate([b_q, jnp.zeros_like(b_q), b_v])
    qkv = (mixed_dot("btd,de->bte", h_attn, w_in) + qkv_bias).astype(low_type)
    qkv = qkv.reshape(lat_dev, tok_rows, 3, width)
    qkv_grouped = lax.all_to_all(qkv, "seq", split_axis=3, concat_axis=1, tiled=True)
    length = qkv_grouped.shape[1]
    head_shape = (lat_dev, length, heads_here, HD)
    query = qkv_grouped[:, :, 0, :].reshape(head_shape)
    keys = qkv_grouped[:, :, 1, :].reshape(head_shape)
    values = qkv_grouped[:, :, 2, :].reshape(head_shape)
    mixed_heads, log_total = lax.map(attend_latent, (query, keys, values))
    mixed = lax.all_to_all(mixed_heads, "seq", split_axis=1, concat_axis=2, tiled=True)
    attn_out = mixed_dot("btd,de->bte", mixed, w_out) + b_out
    middle = inputs + gate1 * attn_out
    norm_two, norm_two_pull = jax.vjp(layer_norm, middle)
    h_mlp = (norm_two * (1.0 + scale2) + shift2).astype(low_type)
    pre_act = mixed_dot("btd,df->btf", h_mlp, w_up) + b_up
    act_f, gelu_pull = jax.vjp(partial(jax.nn.gelu, approximate=True), pre_act)
    act = act_f.astype(low_type)
    mlp_out = mixed_dot("btf,fd->btd", act, w_down) + b_down
    output = (middle + gate2 * mlp_out).astype(low_type)
    d_out = upstream.astype(jnp.float32)
    d_gate2 = jnp.sum(d_out * mlp_out, axis=1)
    d_mlp = (d_out * gate2).astype(low_type)
    g_down = mixed_dot("btf,btd->fd", act, d_mlp)
    d_act = mixed_dot("btd,fd->btf", d_mlp, w_down)
    d_pre = gelu_pull(d_act)[0].astype(low_type)
    g_up = mixed_dot("btd,btf->df", h_mlp, d_pre)
    d_hmlp = mixed_dot("btf,df->btd", d_pre, w_up)
    d_shift2 = jnp.sum(d_hmlp, axis=1)
    d_scale2 = jnp.sum(d_hmlp * norm_two, axis=1)
    d_middle = d_out + norm_two_pull(d_hmlp * (1.0 + scale2))[0]
    d_gate1 = jnp.sum(d_middle * attn_out, axis=1)
    d_attn = (d_middle * gate1).astype(low_type)
    g_out = mixed_dot("btd,bte->de", mixed, d_attn)
    d_mixed = mixed_dot("bte,de->btd", d_attn, w_out).astype(low_type)
    d_mixed_heads = lax.all_to_all(d_mixed, "seq", split_axis=2, concat_axis=1, tiled=True)
    d_grouped = lax.map(attend_back, (query, keys, values, d_mixed_heads, log_total))
    d_qkv = lax.all_to_all(d_grouped, "seq", split_axis=1, concat_axis=3, tiled=True)
    gb_q = jnp.sum(d_qkv[:, :, 0, :].astype(jnp.float32), axis=(0, 1))
    gb_v = jnp.sum(d_qkv[:, :, 2, :].astype(jnp.float32), axis=(0, 1))
    d_qkv_flat = d_qkv.reshape(lat_dev, tok_rows, 3 * width)
    g_in = mixed_dot("btd,bte->de", h_attn, d_qkv_flat)
    d_hattn = mixed_dot("bte,de->btd", d_qkv_flat, w_in)
    d_shift1 = jnp.sum(d_hattn, axis=1)
    d_scale1 = jnp.sum(d_hattn * norm_one, axis=1)
    input_gradient = d_middle + norm_one_pull(d_hattn * (1.0 + scale1))[0]
    d_mod = jnp.concatenate([d_shift1, d_scale1, d_gate1, d_shift2, d_scale2, d_gate2], axis=-1)
    d_cond_act = high_dot(d_mod, w_mod.astype(jnp.float32).T)
    g_mod = high_dot(cond_act.astype(jnp.float32).T, d_mod)
    gb_mod = jnp.sum(d_mod, axis=0)
    d_cond = silu_cond_pull(d_cond_act)[0]
    g_class = high_dot(onehot.astype(jnp.float32).T, d_cond)
    g_second = high_dot(act_time.astype(jnp.float32).T, d_cond)
    d_hidden_time = silu_time_pull(high_dot(d_cond, w_second.astype(jnp.float32).T))[0]
    g_first = high_dot(features.astype(jnp.float32).T, d_hidden_time)
    g_bias = jnp.concatenate(
        [
            jnp.sum(d_hidden_time, axis=0),
            jnp.sum(d_cond, axis=0),
            gb_mod,
            gb_q,
            gb_v,
            jnp.sum(d_attn.astype(jnp.float32), axis=(0, 1)),
            jnp.sum(d_pre.astype(jnp.float32), axis=(0, 1)),
            jnp.sum(d_mlp.astype(jnp.float32), axis=(0, 1)),
        ]
    )
    s_first, s_second, s_class, s_mod, s_in, s_out, s_up, s_down, s_bias = (
        lax.psum_scatter(g_first, "fsdp", scatter_dimension=0, tiled=True),
        lax.psum_scatter(g_second, "fsdp", scatter_dimension=0, tiled=True),
        lax.psum_scatter(g_class, "fsdp", scatter_dimension=1, tiled=True),
        lax.psum_scatter(g_mod, "fsdp", scatter_dimension=1, tiled=True),
        lax.psum_scatter(g_in, "fsdp", scatter_dimension=0, tiled=True),
        lax.psum_scatter(g_out, "fsdp", scatter_dimension=0, tiled=True),
        lax.psum_scatter(g_up, "fsdp", scatter_dimension=0, tiled=True),
        lax.psum_scatter(g_down, "fsdp", scatter_dimension=0, tiled=True),
        lax.psum_scatter(g_bias, "fsdp", scatter_dimension=0, tiled=True),
    )
    totals = lax.psum(
        (s_first, s_second, s_class, s_mod, s_in, s_out, s_up, s_down, s_bias, d_cond), "seq"
    )
    gradients = totals[:9]
    condition_gradient = totals[9]
    local_sum = jnp.sum(gradients[0] * gradients[0])
    for index in range(1, 9):
        local_sum = local_sum + jnp.sum(gradients[index] * gradients[index])
    norm_before = jnp.sqrt(lax.psum(local_sum, "fsdp"))
    factor = clip_limit / jnp.maximum(norm_before, clip_limit)
    params = (
        time_first,
        time_second,
        class_table,
        modulation,
        attend_in,
        attend_out,
        expand,
        contract,
        biases,
    )
    moments = (
        moment_time_first,
        moment_time_second,
        moment_class_table,
        moment_modulation,
        moment_attend_in,
        moment_attend_out,
        moment_expand,
        moment_contract,
        moment_biases,
    )
    squares = (
        square_time_first,
        square_time_second,
        square_class_table,
        square_modulation,
        square_attend_in,
        square_attend_out,
        square_expand,
        square_contract,
        square_biases,
    )
    results = [
        adam_step(params[index], moments[index], squares[index], gradients[index], factor)
        for index in range(9)
    ]
    return (
        output,
        input_gradient,
        condition_gradient,
        norm_before,
        gradients[0],
        gradients[1],
        gradients[2],
        gradients[3],
        gradients[4],
        gradients[5],
        gradients[6],
        gradients[7],
        gradients[8],
        results[0][0],
        results[1][0],
        results[2][0],
        results[3][0],
        results[4][0],
        results[5][0],
        results[6][0],
        results[7][0],
        results[8][0],
        results[0][1],
        results[1][1],
        results[2][1],
        results[3][1],
        results[4][1],
        results[5][1],
        results[6][1],
        results[7][1],
        results[8][1],
        results[0][2],
        results[1][2],
        results[2][2],
        results[3][2],
        results[4][2],
        results[5][2],
        results[6][2],
        results[7][2],
        results[8][2],
    )


def solution(mesh):
    placed = (
        P("fsdp", "seq", None),
        P("fsdp"),
        P("fsdp"),
        P("fsdp", "seq", None),
        P("fsdp", None),
        P("fsdp", None),
        P(None, "fsdp"),
        P(None, "fsdp"),
        P("fsdp", None),
        P("fsdp", None),
        P("fsdp", None),
        P("fsdp", None),
        P("fsdp"),
        P("fsdp", None),
        P("fsdp", None),
        P(None, "fsdp"),
        P(None, "fsdp"),
        P("fsdp", None),
        P("fsdp", None),
        P("fsdp", None),
        P("fsdp", None),
        P("fsdp"),
        P("fsdp", None),
        P("fsdp", None),
        P(None, "fsdp"),
        P(None, "fsdp"),
        P("fsdp", None),
        P("fsdp", None),
        P("fsdp", None),
        P("fsdp", None),
        P("fsdp"),
    )
    return jax.shard_map(
        per_device,
        mesh=mesh,
        in_specs=placed,
        out_specs=(
            P("fsdp", "seq", None),
            P("fsdp", "seq", None),
            P("fsdp", None),
            P(),
            P("fsdp", None),
            P("fsdp", None),
            P(None, "fsdp"),
            P(None, "fsdp"),
            P("fsdp", None),
            P("fsdp", None),
            P("fsdp", None),
            P("fsdp", None),
            P("fsdp"),
            P("fsdp", None),
            P("fsdp", None),
            P(None, "fsdp"),
            P(None, "fsdp"),
            P("fsdp", None),
            P("fsdp", None),
            P("fsdp", None),
            P("fsdp", None),
            P("fsdp"),
            P("fsdp", None),
            P("fsdp", None),
            P(None, "fsdp"),
            P(None, "fsdp"),
            P("fsdp", None),
            P("fsdp", None),
            P("fsdp", None),
            P("fsdp", None),
            P("fsdp"),
            P("fsdp", None),
            P("fsdp", None),
            P(None, "fsdp"),
            P(None, "fsdp"),
            P("fsdp", None),
            P("fsdp", None),
            P("fsdp", None),
            P("fsdp", None),
            P("fsdp"),
        ),
        check_vma=False,
    )
```

profile of v0, /device:TPU:0, one launch (start us, length us, event | category | flops | bytes accessed | tf_op | source)
XLA Modules:
  0.0 3276.7 jit_solution(9896100669545996430)
XLA Ops:
  25.0 33.1 %all-gather = bf16[8,1,2304]{2,1,0:T(2,128)(2,1)S(1)} all-gather(bf16[1,1,2304]{2,1,0:T(2,128)(2,1)S(1)} %reshape.567), channel_id=1, replica_groups=mesh['seq'=4,'fsdp'=8] {'fsdp'}, dimensions={0}, use_global_device_ids=true | all-gather | bytes 41472 | tf_op jit(solution)/shard_map/all_gather | solution.py:167
  58.4 32.8 %all_gather.27 = bf16[256,1152]{1,0:T(8,128)(2,1)S(1)} all-gather(bf16[32,1152]{1,0:T(8,128)(2,1)S(1)} %convert_element_type.183), channel_id=1, replica_groups=mesh['seq'=4,'fsdp'=8] {'fsdp'}, dimensions={0}, use_global_device_ids=true | all-gather | bytes 663552 | tf_op jit(solution)/shard_map/all_gather | solution.py:159
  95.7 29.5 all-gather.9.cloned.1.call-done
  128.1 215.4 %all-gather.13.cloned.1.call-done = bf16[1152,6912]{0,1:T(8,128)(2,1)} async-done(((bf16[1152,864]{0,1:T(8,128)(2,1)}), bf16[1152,6912]{0,1:T(8,128)(2,1)}) %all-gather.13.cloned.1.call-update) | async-done | bytes 15925264 | tf_op jit(solution)/shard_map/all_gather | solution.py:162
  343.5 9.8 convolution_reduce_fusion
  354.0 109.4 %all-gather.15.cloned.1.call-done = bf16[1152,3456]{1,0:T(8,128)(2,1)} async-done(((bf16[144,3456]{1,0:T(8,128)(2,1)}), bf16[1152,3456]{1,0:T(8,128)(2,1)}) %all-gather.15.cloned.1.call-update) | async-done | bytes 7962640 | tf_op jit(solution)/shard_map/all_gather | solution.py:163
  463.4 7.2 fusion.39
  473.3 10.1 copy.107
  483.4 5.0 all-to-all-start
  488.4 28.5 all-to-all-done
  519.7 10.8 while.45
  537.0 6.6 reduce.48
  545.5 4.3 all-to-all-start.1
  551.2 8.2 all-to-all-done.1
  567.5 4.0 fusion.119
  571.8 100.7 %all-gather.19.cloned.1.call-done = bf16[1152,4608]{1,0:T(8,128)(2,1)} async-done(((bf16[144,4608]{1,0:T(8,128)(2,1)}), bf16[1152,4608]{1,0:T(8,128)(2,1)}) %all-gather.19.cloned.1.call-update) | async-done | bytes 10616848 | tf_op jit(solution)/shard_map/all_gather | solution.py:165
  672.5 9.1 convolution_add_fusion
  681.6 144.0 %all-gather.21.cloned.1.call-done = bf16[4608,1152]{1,0:T(8,128)(2,1)} async-done(((bf16[576,1152]{1,0:T(8,128)(2,1)}), bf16[4608,1152]{1,0:T(8,128)(2,1)}) %all-gather.21.cloned.1.call-update) | async-done | bytes 10616848 | tf_op jit(solution)/shard_map/all_gather | solution.py:166
  825.6 9.2 convert_reduce_fusion
  834.8 8.9 fusion.65
  845.9 9.5 convert_reduce_fusion.2
  859.4 6.3 reduce.49
  866.6 4.6 all-to-all-start.2
  871.2 9.5 all-to-all-done.2
  892.3 34.3 %while.46 = (s32[]{:T(128)}, f32[1024,4,72]{0,2,1:T(8,128)S(1)}, f32[1024,4,72]{0,2,1:T(8,128)S(1)}, bf16[2,512,4,72]{1,3,2,0:T(8,128)(2,1)}, bf16[2,512,4,72]{1...) while((s32[]{:T(128)}, f32[1024,4,72]{0,2,1:T(8,128)S(1)}, ...), condition=%wide.region_12.13_spmd.clone, body=%wide.region_10.12_spmd.clone.sunk | while | flops 1536735232 | bytes 166977968 | solution.py:99
  937.9 35.5 %all-to-all-done.3 = bf16[1,1024,3,288]{3,2,0,1:T(4,128)(2,1)S(1)} async-done(((bf16[1,1024,3,288]{3,2,0,1:T(4,128)(2,1)}), bf16[1,1024,3,288]{3,2,0,1:T(4,128)(2,1)S(1)}, u32[]{:S(2)}, u32[]{:S(2)}) %all-to-all-start.3) | async-done | bytes 1769504 | tf_op jit(solution)/shard_map/all_to_all | solution.py:224
  973.4 4.2 copy.125
  979.5 6.0 fusion.62
  991.5 9.5 convolution_reduce_fusion.2
  1016.8 8.1 fusion.98
  1026.2 12.0 fusion.102
  1039.3 13.6 fusion.77
  1053.7 10.9 broadcast_multiply_fusion
  1069.0 107.0 %reduce-scatter.19.cloned.1.call-done = f32[144,1152]{1,0:T(8,128)} async-done(((f32[1152,1152]{1,0:T(8,128)}), f32[144,1152]{1,0:T(8,128)}) %reduce-scatter.19.cloned.1.call-update) | async-done | bytes 663568 | tf_op jit(solution)/shard_map/reduce_scatter | solution.py:260
  1176.0 98.8 %reduce-scatter.13.cloned.1.call-done = f32[1000,144]{0,1:T(8,128)} async-done(((f32[1000,1152]{0,1:T(8,128)}), f32[1000,144]{0,1:T(8,128)}) %reduce-scatter.13.cloned.1.call-update) | async-done | bytes 576016 | tf_op jit(solution)/shard_map/reduce_scatter | solution.py:257
  1274.9 107.8 %reduce-scatter.11.cloned.1.call-done = f32[144,1152]{1,0:T(8,128)} async-done(((f32[1152,1152]{1,0:T(8,128)}), f32[144,1152]{1,0:T(8,128)}) %reduce-scatter.11.cloned.1.call-update) | async-done | bytes 663568 | tf_op jit(solution)/shard_map/reduce_scatter | solution.py:256
  1382.6 272.0 %reduce-scatter.17.cloned.1.call-done = f32[144,3456]{1,0:T(8,128)} async-done(((f32[1152,3456]{1,0:T(8,128)}), f32[144,3456]{1,0:T(8,128)}) %reduce-scatter.17.cloned.1.call-update) | async-done | bytes 1990672 | tf_op jit(solution)/shard_map/reduce_scatter | solution.py:259
  1654.7 349.6 %reduce-scatter.21.cloned.1.call-done = f32[144,4608]{1,0:T(8,128)} async-done(((f32[1152,4608]{1,0:T(8,128)}), f32[144,4608]{1,0:T(8,128)}) %reduce-scatter.21.cloned.1.call-update) | async-done | bytes 2654224 | tf_op jit(solution)/shard_map/reduce_scatter | solution.py:261
  2004.3 349.3 %reduce-scatter.23.cloned.1.call-done = f32[576,1152]{1,0:T(8,128)} async-done(((f32[4608,1152]{1,0:T(8,128)}), f32[576,1152]{1,0:T(8,128)}) %reduce-scatter.23.cloned.1.call-update) | async-done | bytes 2654224 | tf_op jit(solution)/shard_map/reduce_scatter | solution.py:262
  2353.6 511.5 %reduce-scatter.15.cloned.1.call-done = f32[1152,864]{0,1:T(8,128)} async-done(((f32[1152,6912]{0,1:T(8,128)}), f32[1152,864]{0,1:T(8,128)}) %reduce-scatter.15.cloned.1.call-update) | async-done | bytes 3981328 | tf_op jit(solution)/shard_map/reduce_scatter | solution.py:258
  2867.6 69.8 %all-reduce.6.cloned.1.call-done = f32[18432]{0:T(1024)} async-done(((f32[18432]{0:T(1024)}), f32[18432]{0:T(1024)}) %all-reduce.6.cloned.1.call-update) | async-done | bytes 73744
  2938.2 10.2 all-reduce.1
  2949.0 224.7 %all-reduce.8.cloned.1.call-done = (f32[32,1152]{1,0:T(8,128)}, f32[144,1152]{1,0:T(8,128)}, f32[1000,144]{0,1:T(8,128)}, f32[1152,864]{0,1:T(8,128)}, f32[144,3...) async-done(((f32[32,1152]{1,0:T(8,128)}, f32[144,1152]{1,0:T(8,128)}, f32[1000,144]{0,1:T(8,128)}, f32[1152,864]{0,1:T(8,128)}, ...) | async-done | bytes 13330960 | tf_op jit(solution)/shard_map/psum | solution.py:265
  3179.1 3.9 multiply_reduce_fusion.2
  3196.8 22.1 psum.87
  3227.9 8.8 multiply_subtract_fusion
  3244.0 7.3 multiply_subtract_fusion.2
  3251.4 7.2 multiply_subtract_fusion.1
  (428 shorter events, 195.3 us)
Async XLA Ops:
  7.2 86.1 %all-gather.11.cloned.1.call-start = ((), (), s32[]{:S(2)}) async-start(), calls=%async_computation.13 | async-start | bytes 2654208 | tf_op jit(solution)/shard_map/all_gather | solution.py:161
  9.1 116.1 %all-gather.9.cloned.1.call-start = ((), (), s32[]{:S(2)}) async-start(), calls=%async_computation.12 | async-start | bytes 2985984 | tf_op jit(solution)/shard_map/all_gather | solution.py:160
  11.0 332.4 %all-gather.13.cloned.1.call-start = ((), (), s32[]{:S(2)}) async-start(), calls=%async_computation.14 | async-start | bytes 17915904 | tf_op jit(solution)/shard_map/all_gather | solution.py:162
  14.7 448.7 %all-gather.15.cloned.1.call-start = ((), (), s32[]{:S(2)}) async-start(), calls=%async_computation.15 | async-start | bytes 8957952 | tf_op jit(solution)/shard_map/all_gather | solution.py:163
  17.6 549.9 %all-gather.17.cloned.1.call-start = ((), (), s32[]{:S(2)}) async-start(), calls=%async_computation.16 | async-start | bytes 2985984 | tf_op jit(solution)/shard_map/all_gather | solution.py:164
  18.4 654.1 %all-gather.19.cloned.1.call-start = ((), (), s32[]{:S(2)}) async-start(), calls=%async_computation.17 | async-start | bytes 11943936 | tf_op jit(solution)/shard_map/all_gather | solution.py:165
  19.7 805.9 %all-gather.21.cloned.1.call-start = ((), (), s32[]{:S(2)}) async-start(), calls=%async_computation.18 | async-start | bytes 11943936 | tf_op jit(solution)/shard_map/all_gather | solution.py:166
  22.9 69.9 %copy-start.7 = (bf16[1,256,1152]{2,1,0:T(8,128)(2,1)S(1)}, bf16[1,256,1152]{2,1,0:T(8,128)(2,1)}, u32[]{:S(2)}) copy-start(bf16[1,256,1152]{2,1,0:T(8,128)(2,1)} %param.35) | copy-start | bytes 1769476
  58.3 69.1 %copy-start.60 = (bf16[18432]{0:T(1024)(128)(2,1)}, bf16[18432]{0:T(1024)(128)(2,1)S(1)}, u32[]{:S(2)}) copy-start(bf16[18432]{0:T(1024)(128)(2,1)S(1)} %reshape.568) | copy-start | bytes 110596
  92.9 370.5 %copy-start.74 = (f32[256]{0:T(256)}, f32[256]{0:T(256)S(1)}, u32[]{:S(2)}) copy-start(f32[256]{0:T(256)S(1)} %broadcast_multiply_fusion.5) | copy-start | bytes 3076
  93.2 32.0 copy-start.97
  93.2 370.2 %copy-start.78 = (f32[256]{0:T(256)}, f32[256]{0:T(256)S(1)}, u32[]{:S(2)}) copy-start(f32[256]{0:T(256)S(1)} %fusion.95) | copy-start | bytes 3076
  95.7 257.6 %copy-start.68 = (f32[1152]{0:T(1024)}, f32[1152]{0:T(1024)S(1)}, u32[]{:S(2)}) copy-start(f32[1152]{0:T(1024)S(1)} %convolution_reduce_fusion.3) | copy-start | bytes 13828
  127.4 225.8 %copy-start.70 = (f32[1152]{0:T(1024)}, f32[1152]{0:T(1024)S(1)}, u32[]{:S(2)}) copy-start(f32[1152]{0:T(1024)S(1)} %convolution_reduce_fusion.4) | copy-start | bytes 13828
  354.0 116.7 %copy-start.55 = (f32[1152]{0:T(1024)}, f32[1152]{0:T(1024)S(1)}, u32[]{:S(2)}) copy-start(f32[1152]{0:T(1024)S(1)} %get-tuple-element.269) | copy-start | bytes 13828
  354.0 116.7 %copy-start.62 = (f32[1152]{0:T(1024)}, f32[1152]{0:T(1024)S(1)}, u32[]{:S(2)}) copy-start(f32[1152]{0:T(1024)S(1)} %get-tuple-element.268) | copy-start | bytes 13828
  354.0 318.6 %copy-start.61 = (f32[1152]{0:T(1024)}, f32[1152]{0:T(1024)S(1)}, u32[]{:S(2)}) copy-start(f32[1152]{0:T(1024)S(1)} %get-tuple-element.266) | copy-start | bytes 13828
  354.0 489.8 %copy-start.57 = (f32[1152]{0:T(1024)}, f32[1152]{0:T(1024)S(1)}, u32[]{:S(2)}) copy-start(f32[1152]{0:T(1024)S(1)} %get-tuple-element.267) | copy-start | bytes 13828
  483.4 33.5 %all-to-all-start = ((bf16[1,256,3,1152]{1,2,0,3:T(4,128)(2,1)}), bf16[1,256,3,1152]{1,2,0,3:T(4,128)(2,1)}, u32[]{:S(2)}, u32[]{:S(2)}) async-start(bf16[1,256,3,1152]{1,2,0,3:T(4,128)(2,1)} %copy.107), calls=%async_computation | async-start | bytes 4718592 | tf_op jit(solution)/shard_map/all_to_all | solution.py:190
  532.0 11.5 copy-start.9
  545.5 13.9 all-to-all-start.1
  571.5 272.7 %copy-start.13 = (f32[1,256,1152]{2,1,0:T(8,128)}, f32[1,256,1152]{2,1,0:T(8,128)S(1)}, u32[]{:S(2)}) copy-start(f32[1,256,1152]{2,1,0:T(8,128)S(1)} %get-tuple-element.351) | copy-start | bytes 3538948
  571.5 272.2 %copy-start.86 = (f32[256]{0:T(256)}, f32[256]{0:T(256)S(1)}, u32[]{:S(2)}) copy-start(f32[256]{0:T(256)S(1)} %broadcast_multiply_fusion.4) | copy-start | bytes 3076
  571.8 272.0 %copy-start.92 = (f32[256]{0:T(256)}, f32[256]{0:T(256)S(1)}, u32[]{:S(2)}) copy-start(f32[256]{0:T(256)S(1)} %fusion.96) | copy-start | bytes 3076
  672.5 153.1 %copy-start.36 = (bf16[1,256,1152]{2,1,0:T(8,128)(2,1)S(1)}, bf16[1,256,1152]{2,1,0:T(8,128)(2,1)}, u32[]{:S(2)}) copy-start(bf16[1,256,1152]{2,1,0:T(8,128)(2,1)} %param.38) | copy-start | bytes 1769476
  672.5 153.1 %copy-start.87 = (f32[1152]{0:T(1024)S(1)}, f32[1152]{0:T(1024)}, u32[]{:S(2)}) copy-start(f32[1152]{0:T(1024)} %get-tuple-element.265) | copy-start | bytes 13828
  843.7 11.7 copy-start.30
  844.2 11.2 copy-start.31
  844.2 11.2 copy-start.102
  845.8 10.4 copy-start.32
  866.6 14.1 all-to-all-start.2
  932.8 40.6 %all-to-all-start.3 = ((bf16[1,1024,3,288]{3,2,0,1:T(4,128)(2,1)}), bf16[1,1024,3,288]{3,2,0,1:T(4,128)(2,1)S(1)}, u32[]{:S(2)}, u32[]{:S(2)}) async-start(bf16[1,1024,3,288]{3,2,0,1:T(4,128)(2,1)} %copy.120), calls=%async_computation.3 | async-start | bytes 6291456 | tf_op jit(solution)/shard_map/all_to_all | solution.py:224
  936.5 132.5 %reduce-scatter.9.cloned.1.call-start = ((), (), s32[]{:S(2)}) async-start(), calls=%async_computation.19 | async-start | bytes 1327104 | tf_op jit(solution)/shard_map/reduce_scatter | solution.py:255
  985.4 15.6 copy-start.19
  991.5 10.4 copy-start.18
  1006.6 169.4 %reduce-scatter.19.cloned.1.call-start = ((), (), s32[]{:S(2)}) async-start(), calls=%async_computation.24 | async-start | bytes 5971968 | tf_op jit(solution)/shard_map/reduce_scatter | solution.py:260
  1009.9 264.9 %reduce-scatter.13.cloned.1.call-start = ((), (), s32[]{:S(2)}) async-start(), calls=%async_computation.21 | async-start | bytes 5308416 | tf_op jit(solution)/shard_map/reduce_scatter | solution.py:257
  1012.6 370.0 %reduce-scatter.11.cloned.1.call-start = ((), (), s32[]{:S(2)}) async-start(), calls=%async_computation.20 | async-start | bytes 5971968 | tf_op jit(solution)/shard_map/reduce_scatter | solution.py:256
  1016.1 638.6 %reduce-scatter.17.cloned.1.call-start = ((), (), s32[]{:S(2)}) async-start(), calls=%async_computation.23 | async-start | bytes 17915904 | tf_op jit(solution)/shard_map/reduce_scatter | solution.py:259
  1024.9 979.4 %reduce-scatter.21.cloned.1.call-start = ((), (), s32[]{:S(2)}) async-start(), calls=%async_computation.25 | async-start | bytes 23887872 | tf_op jit(solution)/shard_map/reduce_scatter | solution.py:261
  1038.2 1315.3 %reduce-scatter.23.cloned.1.call-start = ((), (), s32[]{:S(2)}) async-start(), calls=%async_computation.26 | async-start | bytes 23887872 | tf_op jit(solution)/shard_map/reduce_scatter | solution.py:262
  1052.9 1812.2 %reduce-scatter.15.cloned.1.call-start = ((), (), s32[]{:S(2)}) async-start(), calls=%async_computation.22 | async-start | bytes 35831808 | tf_op jit(solution)/shard_map/reduce_scatter | solution.py:258
  1064.7 1872.7 %all-reduce.6.cloned.1.call-start = ((), (), s32[]{:S(2)}) async-start(), calls=%async_computation.27 | async-start | bytes 147456
  1066.7 2107.0 %all-reduce.8.cloned.1.call-start = ((), (), s32[]{:S(2)}) async-start(), calls=%async_computation.28 | async-start | bytes 26689536 | tf_op jit(solution)/shard_map/psum | solution.py:265
  2948.4 234.6 %copy-start.84 = (f32[2304]{0:T(1024)}, f32[2304]{0:T(1024)S(1)}, u32[]{:S(2)}) copy-start(f32[2304]{0:T(1024)S(1)} %get-tuple-element.540) | copy-start | bytes 27652
  3187.5 32.1 copy-start.46
  3187.5 32.1 copy-start.54
  3227.9 9.7 copy-start.45
  (90 other events, 343.0 us)
Sparse Core Ops, SparseCore 0:
  10.8 57.4 all-gather.10
  71.1 54.1 all-gather.8
  128.0 215.4 all-gather.12
  346.1 117.2 all-gather.14
  466.0 53.1 all-gather.16
  521.8 150.6 all-gather.18
  675.3 150.2 all-gather.20
  1006.7 62.2 reduce-scatter.8
  1072.6 103.3 reduce-scatter.18
  1179.5 95.3 reduce-scatter.12
  1278.5 104.1 reduce-scatter.10
  1386.4 268.2 reduce-scatter.16
  1658.6 345.7 reduce-scatter.20
  2008.0 345.4 reduce-scatter.22
  2357.3 507.7 reduce-scatter.14
  2869.0 68.3 all-reduce.5
  2940.4 233.2 all-reduce.7
where the time goes:
time: 3290 us; the launch traced here: 3280 us
  waiting for transfers between devices  2770 us (84%)
  matrix products  148 us (4%)
  other arithmetic  124 us (4%)
  blocking collectives  98.2 us (3%)
  local copies, waits for them, and re-layouts  88.5 us (3%)
    reduce_scatter x1, waiting for transfers between devices, per_device(): lax.psum_scatter(g_mod, 'fsdp', scatter_dimension=1, tiled=True)  512 us
    reduce_scatter x1, waiting for transfers between devices, per_device(): lax.psum_scatter(g_up, 'fsdp', scatter_dimension=0, tiled=True)  350 us
    reduce_scatter x1, waiting for transfers between devices, per_device(): lax.psum_scatter(g_down, 'fsdp', scatter_dimension=0, tiled=True)  349 us
    reduce_scatter x1, waiting for transfers between devices, per_device(): lax.psum_scatter(g_in, 'fsdp', scatter_dimension=0, tiled=True)  272 us
    psum x1, waiting for transfers between devices, per_device(): lax.psum((s_first, s_second, s_class, s_mod, s_in, s_out, s_up, s_down, s...  225 us
    all_gather x1, waiting for transfers between devices, per_device(): lax.all_gather(modulation.astype(low_type), 'fsdp', axis=1, tiled=True)  215 us
    all_gather x1, waiting for transfers between devices, per_device(): lax.all_gather(contract.astype(low_type), 'fsdp', axis=0, tiled=True)  144 us
    dot_general x26, matrix products, mixed_dot(): return jnp.einsum(form, left, right, preferred_element_type=jnp.float32)  122 us
  transfers between devices with their start and end apart: 21, of which 19 were waited for; matrix products, arithmetic and copies ran while one was open for 5% of the time, Pallas kernels for 0%

commit v1 on v0

v1 whole, which is shorter than its diff:
```python
from functools import partial
import math

import jax
import jax.numpy as jnp
from jax import lax
from jax.sharding import PartitionSpec as P

H = 16
HD = 72
FREQ = 256
NCLS = 1000
STEP = 10


HIGH = lax.Precision.HIGHEST
LOW = jnp.bfloat16
norm_eps = 1e-06
beta_one = 0.9
beta_two = 0.999
learn_rate = 0.04
weight_decay = 0.01
adam_eps = 1e-08
clip_limit = 1.0


def layer_norm(value):
    centre = value - jnp.mean(value, axis=-1, keepdims=True)
    spread = jnp.mean(centre * centre, axis=-1, keepdims=True)
    inverse = lax.rsqrt(spread + norm_eps)
    return centre * inverse, inverse


def layer_norm_back(norm, inverse, grad):
    first = jnp.mean(grad, axis=-1, keepdims=True)
    second = jnp.mean(grad * norm, axis=-1, keepdims=True)
    return inverse * (grad - first - norm * second)


def silu_parts(value):
    gate = jax.nn.sigmoid(value)
    return value * gate, gate * (1.0 + value * (1.0 - gate))


def time_features(timesteps):
    half = FREQ // 2
    freqs = jnp.exp(-math.log(10000.0) * jnp.arange(half, dtype=jnp.float32) / half)
    angles = timesteps.astype(jnp.float32)[:, None] * freqs[None, :]
    return jnp.concatenate([jnp.cos(angles), jnp.sin(angles)], axis=-1)


def split_biases(biases, width, hidden):
    widths = [width, width, 6 * width, width, width, width, hidden, width]
    pieces = []
    start = 0
    for length in widths:
        pieces.append(biases[start : start + length])
        start = start + length
    return pieces


def high_dot(left, right):
    return jnp.dot(left, right, precision=HIGH, preferred_element_type=jnp.float32)


def mixed_dot(form, left, right):
    return jnp.einsum(form, left, right, preferred_element_type=jnp.float32)


SWAP_Y = [(i, i ^ 1) for i in range(8)]
SWAP_Z1 = [(i, i ^ 2) for i in range(8)]
SWAP_Z2 = [(i, i ^ 4) for i in range(8)]
Z_UP = [(i, i + 2) for i in range(6)]
Z_DOWN = [(i + 2, i) for i in range(6)]
SWAP_CORE = [(i, i ^ 1) for i in range(4)]
SWAP_X = [(i, i ^ 2) for i in range(4)]


def pick(array, index, axis=0):
    return lax.dynamic_index_in_dim(array, index, axis, keepdims=False)


def place(array, block, *index):
    starts = tuple(index) + (0,) * (array.ndim - len(index))
    return lax.dynamic_update_slice(array, block[(None,) * len(index)], starts)


def gather_rows(block):
    count = lax.axis_size("fsdp")
    if count != 8:
        return lax.all_gather(block, "fsdp", axis=0, tiled=True)
    me = lax.axis_index("fsdp")
    z, y = me // 2, me % 2
    hop = partial(lax.ppermute, axis_name="fsdp")
    up1, down1 = hop(block, perm=Z_UP), hop(block, perm=Z_DOWN)
    mate0 = hop(block, perm=SWAP_Y)
    one = jnp.where(z == 0, down1, up1)
    mate1 = hop(one, perm=SWAP_Y)
    up2, down2 = hop(up1, perm=Z_UP), hop(down1, perm=Z_DOWN)
    two = jnp.where(z < 2, down2, up2)
    mate2 = hop(two, perm=SWAP_Y)
    up3, down3 = hop(up2, perm=Z_UP), hop(down2, perm=Z_DOWN)
    three = jnp.where(z == 0, down3, jnp.where(z == 3, up3, down1))
    mate3 = hop(three, perm=SWAP_Y)
    at1 = jnp.where(z == 0, 1, z - 1)
    at2 = jnp.where(z < 2, z + 2, z - 2)
    at3 = jnp.where(z == 0, 3, jnp.where(z == 3, 0, z + 1))
    whole = jnp.zeros((4, 2) + block.shape, block.dtype)
    for at, own, mate in ((z, block, mate0), (at1, one, mate1), (at2, two, mate2), (at3, three, mate3)):
        whole = place(whole, own, at, y)
        whole = place(whole, mate, at, 1 - y)
    return whole.reshape((8 * block.shape[0],) + block.shape[1:])


def scatter_rows(whole):
    count = lax.axis_size("fsdp")
    if count != 8:
        return lax.psum_scatter(whole, "fsdp", scatter_dimension=0, tiled=True)
    me = lax.axis_index("fsdp")
    z, y = me // 2, me % 2
    hop = partial(lax.ppermute, axis_name="fsdp")
    parts = whole.reshape((4, 2, whole.shape[0] // 8) + whole.shape[1:])
    got = hop(pick(parts, 1 - y, 1).astype(LOW), perm=SWAP_Y)
    acc = pick(parts, y, 1) + got.astype(jnp.float32)
    rise = pick(acc, jnp.minimum(z + 3, 3))
    fall = pick(acc, jnp.maximum(z - 3, 0))
    for step in (2, 1, 0):
        rise_in = hop(rise.astype(LOW), perm=Z_UP).astype(jnp.float32)
        fall_in = hop(fall.astype(LOW), perm=Z_DOWN).astype(jnp.float32)
        if step:
            rise = pick(acc, jnp.minimum(z + step, 3)) + rise_in
            fall = pick(acc, jnp.maximum(z - step, 0)) + fall_in
    return pick(acc, z) + (rise_in + fall_in)


def small_gather(block):
    count = lax.axis_size("fsdp")
    if count != 8:
        return lax.all_gather(block, "fsdp", axis=0)
    me = lax.axis_index("fsdp")
    whole = block[None]
    for bit, perm in ((1, SWAP_Y), (2, SWAP_Z1), (4, SWAP_Z2)):
        other = lax.ppermute(whole, "fsdp", perm)
        low = (me & bit) == 0
        whole = jnp.concatenate([jnp.where(low, whole, other), jnp.where(low, other, whole)], axis=0)
    return whole


def small_sum(block):
    count = lax.axis_size("fsdp")
    if count != 8:
        return lax.psum(block, "fsdp")
    for perm in (SWAP_Y, SWAP_Z1, SWAP_Z2):
        block = block + lax.ppermute(block, "fsdp", perm)
    return block


def seq_sum(block):
    count = lax.axis_size("seq")
    if count != 4:
        return lax.psum(block, "seq")
    for perm in (SWAP_CORE, SWAP_X):
        block = block + lax.ppermute(block, "seq", perm)
    return block


def seq_gather(block):
    count = lax.axis_size("seq")
    if count != 4:
        return lax.all_gather(block, "seq", axis=0)
    me = lax.axis_index("seq")
    hop = partial(lax.ppermute, axis_name="seq")
    across = hop(block, perm=SWAP_X)
    mate = hop(block, perm=SWAP_CORE)
    last = hop(across, perm=SWAP_CORE)
    whole = jnp.zeros((4,) + block.shape, block.dtype)
    for at, part in ((me, block), (me ^ 1, mate), (me ^ 2, across), (me ^ 3, last)):
        whole = place(whole, part, at)
    return whole


def seq_scatter(parts):
    count = lax.axis_size("seq")
    if count != 4:
        return lax.psum_scatter(parts, "seq", scatter_dimension=0, tiled=False)
    me = lax.axis_index("seq")
    x, core = me // 2, me % 2
    hop = partial(lax.ppermute, axis_name="seq")
    parts = parts.reshape((2, 2) + parts.shape[1:])
    got = hop(pick(parts, 1 - core, 1).astype(LOW), perm=SWAP_CORE)
    acc = pick(parts, core, 1) + got.astype(jnp.float32)
    got = hop(pick(acc, 1 - x).astype(LOW), perm=SWAP_X)
    return pick(acc, x) + got.astype(jnp.float32)


def attend(query, keys, values):
    score_scale = 1.0 / math.sqrt(keys.shape[-1])
    scores = mixed_dot("qhd,khd->hqk", query, keys) * score_scale
    top = jnp.max(scores, axis=-1, keepdims=True)
    expo = jnp.exp(scores - top)
    total = jnp.sum(expo, axis=-1, keepdims=True)
    probs = (expo / total).astype(LOW)
    mixed = mixed_dot("hqk,khd->qhd", probs, values)
    return mixed.astype(LOW), (top + jnp.log(total))[..., 0]


def attend_back(query, keys, values, d_mixed, log_total):
    length, heads_here, head_dim = query.shape
    block = min(512, length)
    count = length // block
    score_scale = 1.0 / math.sqrt(head_dim)

    def back_block(carry, pieces):
        d_keys, d_values = carry
        query_block, d_block, log_block = pieces
        scores = mixed_dot("qhd,khd->hqk", query_block, keys) * score_scale
        probs = jnp.exp(scores - log_block[..., None])
        d_probs = mixed_dot("qhd,khd->hqk", d_block, values)
        delta = jnp.sum(probs * d_probs, axis=-1, keepdims=True)
        d_scores = (probs * (d_probs - delta)).astype(LOW)
        d_query = mixed_dot("hqk,khd->qhd", d_scores, keys) * score_scale
        d_keys = d_keys + mixed_dot("hqk,qhd->khd", d_scores, query_block) * score_scale
        d_values = d_values + mixed_dot("hqk,qhd->khd", probs.astype(LOW), d_block)
        return ((d_keys, d_values), d_query)

    empty = jnp.zeros((length, heads_here, head_dim), jnp.float32)
    blocked = (count, block, heads_here, head_dim)
    logs = log_total.reshape(heads_here, count, block).transpose(1, 0, 2)
    (d_keys, d_values), d_query = lax.scan(
        back_block, (empty, empty), (query.reshape(blocked), d_mixed.reshape(blocked), logs)
    )
    flat = (length, heads_here * head_dim)
    return jnp.concatenate(
        [d_query.reshape(flat), d_keys.reshape(flat), d_values.reshape(flat)], axis=1
    ).astype(LOW)


def adam_step(weight, moment, square, gradient, factor):
    clipped = gradient * factor
    moment_next = beta_one * moment + (1.0 - beta_one) * clipped
    square_next = beta_two * square + (1.0 - beta_two) * clipped * clipped
    moment_hat = moment_next / (1.0 - beta_one**STEP)
    square_hat = square_next / (1.0 - beta_two**STEP)
    master = weight - learn_rate * (
        moment_hat / (jnp.sqrt(square_hat) + adam_eps) + weight_decay * weight
    )
    return (master, moment_next, square_next)


def per_device(latents, timesteps, labels, upstream, *state):
    params, moments, squares = state[:9], state[9:18], state[18:]
    time_first, time_second, class_table, modulation, attend_in, attend_out, expand, contract, biases = params
    lat_dev, tok_rows, width = latents.shape
    assert lat_dev == 1
    hidden = expand.shape[1]
    ranks = lax.axis_size("seq")
    owners = lax.axis_size("fsdp")
    rank = lax.axis_index("seq")
    owner = lax.axis_index("fsdp")
    heads_here = H // ranks
    span = heads_here * HD
    length = ranks * tok_rows
    rows = width // owners
    unit = hidden // (owners * ranks)
    hid_here = owners * unit
    mod_here = 6 * width // owners
    first_rows = FREQ // owners

    def mine(array, axis, parts, index):
        size = array.shape[axis] // parts
        return lax.dynamic_slice_in_dim(array, index * size, size, axis)

    w_in = gather_rows(pick(attend_in.reshape(rows, 3, ranks, span), rank, 2).astype(LOW).reshape(rows, 3 * span))
    w_out_part = gather_rows(mine(attend_out, 1, ranks, rank).astype(LOW))
    w_up = gather_rows(
        pick(expand.reshape(rows, owners, ranks, unit), rank, 2).astype(LOW).reshape(rows, hid_here)
    )
    w_down = gather_rows(mine(contract, 0, ranks, rank).astype(LOW))
    inputs_low = seq_gather(latents[0]).reshape(length, width)
    d_out_low = seq_gather(upstream[0]).reshape(length, width)
    w_out = seq_gather(w_out_part).transpose(1, 0, 2).reshape(width, width)

    note = jnp.concatenate(
        [biases.astype(LOW).astype(jnp.float32), timesteps.astype(jnp.float32), labels.astype(jnp.float32)]
    )
    notes = small_gather(note)
    share = biases.shape[0]
    all_bias = notes[:, :share].reshape(owners * share)
    all_steps = notes[:, share]
    all_labels = notes[:, share + 1].astype(jnp.int32)
    b_t1, b_t2, b_mod, b_q, b_v, b_out, b_up, b_down = split_biases(all_bias, width, hidden)
    features = time_features(all_steps).astype(LOW)
    my_features = mine(features, 1, owners, owner)
    hidden_time = small_sum(mixed_dot("bf,fd->bd", my_features, time_first.astype(LOW))) + b_t1
    act_time_f, silu_time_slope = silu_parts(hidden_time)
    act_time = act_time_f.astype(LOW)
    my_act_time = mine(act_time, 1, owners, owner)
    onehot = (all_labels[:, None] == jnp.arange(NCLS, dtype=jnp.int32)[None, :]).astype(LOW)
    class_part = mixed_dot("bc,cd->bd", onehot, class_table.astype(LOW))
    cond_part = mixed_dot("bd,de->be", my_act_time, time_second.astype(LOW))
    class_wide = lax.dynamic_update_slice(jnp.zeros_like(cond_part), class_part, (0, owner * rows))
    cond = small_sum(cond_part + class_wide) + b_t2
    cond_act_f, silu_cond_slope = silu_parts(cond)
    cond_act = cond_act_f.astype(LOW)
    modulation_low = modulation.astype(LOW)
    mod_part = mixed_dot("bd,de->be", cond_act, modulation_low) + mine(b_mod, 0, owners, owner)
    mod_values = pick(small_gather(mod_part), owner, 1).reshape(6, 1, width)
    shift1, scale1, gate1, shift2, scale2, gate2 = [mod_values[index] for index in range(6)]

    inputs = inputs_low.astype(jnp.float32)
    norm_one, _ = layer_norm(inputs)
    h_attn = (norm_one * (1.0 + scale1) + shift1).astype(LOW)
    my_b_q, my_b_v = mine(b_q, 0, ranks, rank), mine(b_v, 0, ranks, rank)
    qkv_bias = jnp.concatenate([my_b_q, jnp.zeros_like(my_b_q), my_b_v])
    qkv = (mixed_dot("td,de->te", h_attn, w_in) + qkv_bias).astype(LOW)
    head_shape = (length, heads_here, HD)
    query, keys, values = [qkv[:, part * span : (part + 1) * span].reshape(head_shape) for part in range(3)]
    mixed_heads, log_total = attend(query, keys, values)
    mixed = seq_gather(mixed_heads.reshape(length, span)).transpose(1, 0, 2).reshape(length, width)
    attn_out = mixed_dot("td,de->te", mixed, w_out) + b_out
    middle = inputs + gate1 * attn_out
    norm_two, inverse_two = layer_norm(middle)
    h_mlp = (norm_two * (1.0 + scale2) + shift2).astype(LOW)

    my_b_up = pick(b_up.reshape(owners, ranks, unit), rank, 1).reshape(hid_here)
    pre_act = mixed_dot("td,df->tf", h_mlp, w_up) + my_b_up
    act_f, gelu_pull = jax.vjp(partial(jax.nn.gelu, approximate=True), pre_act)
    act = act_f.astype(LOW)
    mlp_part = mixed_dot("tf,fd->td", act, w_down)
    d_out = d_out_low.astype(jnp.float32)
    d_mlp = (d_out * gate2).astype(LOW)
    d_act = mixed_dot("td,fd->tf", d_mlp, w_down)
    d_pre = gelu_pull(d_act)[0].astype(LOW)
    d_hmlp_part = mixed_dot("tf,df->td", d_pre, w_up)
    d_hmlp = seq_scatter(d_hmlp_part.reshape(ranks, tok_rows, width))
    g_down = scatter_rows(mixed_dot("tf,td->fd", act, d_mlp))
    g_up = scatter_rows(mixed_dot("td,tf->df", h_mlp, d_pre))
    gb_up = jnp.sum(d_pre.astype(jnp.float32), axis=0)
    gb_down = jnp.sum(d_mlp.astype(jnp.float32), axis=0)

    own = lambda array: mine(array, 0, ranks, rank)
    my_attn_out, my_middle, my_norm_two, my_inverse_two = own(attn_out), own(middle), own(norm_two), own(inverse_two)
    my_d_out = upstream[0].astype(jnp.float32)
    mlp_out = seq_scatter(mlp_part.reshape(ranks, tok_rows, width)) + b_down
    output = (my_middle + gate2 * mlp_out).astype(LOW)
    d_gate2 = jnp.sum(my_d_out * mlp_out, axis=0)
    d_shift2 = jnp.sum(d_hmlp, axis=0)
    d_scale2 = jnp.sum(d_hmlp * my_norm_two, axis=0)
    d_middle = my_d_out + layer_norm_back(my_norm_two, my_inverse_two, d_hmlp * (1.0 + scale2))
    d_gate1 = jnp.sum(d_middle * my_attn_out, axis=0)
    my_d_attn = (d_middle * gate1).astype(LOW)
    d_attn = seq_gather(my_d_attn).reshape(length, width)
    d_mixed = mixed_dot("te,de->td", d_attn, mine(w_out, 0, ranks, rank)).astype(LOW)
    g_out = scatter_rows(mixed_dot("td,te->de", mixed, mine(d_attn, 1, ranks, rank)))
    d_qkv = attend_back(query, keys, values, d_mixed.reshape(head_shape), log_total)
    g_in = scatter_rows(mixed_dot("td,te->de", h_attn, d_qkv))
    d_hattn = seq_scatter(mixed_dot("te,de->td", d_qkv, w_in).reshape(ranks, tok_rows, width))
    my_inputs = latents[0].astype(jnp.float32)
    my_norm_one, my_inverse_one = layer_norm(my_inputs)
    d_shift1 = jnp.sum(d_hattn, axis=0)
    d_scale1 = jnp.sum(d_hattn * my_norm_one, axis=0)
    input_gradient = d_middle + layer_norm_back(my_norm_one, my_inverse_one, d_hattn * (1.0 + scale1))

    my_d_mod = jnp.concatenate([d_shift1, d_scale1, d_gate1, d_shift2, d_scale2, d_gate2])
    d_mod = small_gather(seq_sum(my_d_mod))
    gb_qv = jnp.sum(d_qkv.astype(jnp.float32), axis=0)
    wide = lambda part, size: lax.dynamic_update_slice(jnp.zeros((size,), jnp.float32), part, (rank * part.shape[0],))
    gb_up_wide = lax.dynamic_update_slice(
        jnp.zeros((owners, ranks, unit), jnp.float32), gb_up.reshape(owners, 1, unit), (0, rank, 0)
    ).reshape(hidden)
    gb_tail = jnp.concatenate(
        [
            wide(gb_qv[:span], width),
            wide(gb_qv[2 * span :], width),
            jnp.sum(my_d_attn.astype(jnp.float32), axis=0),
            gb_up_wide,
            jnp.where(rank == 0, gb_down, 0.0),
        ]
    )
    gb_tail = small_sum(seq_sum(gb_tail))
    my_d_mod_all = mine(d_mod, 1, owners, owner)
    d_cond_act = small_sum(high_dot(my_d_mod_all, modulation_low.astype(jnp.float32).T))
    d_cond = d_cond_act * silu_cond_slope
    my_d_cond = mine(d_cond, 1, owners, owner)
    d_time_part = high_dot(d_cond, time_second.astype(LOW).astype(jnp.float32).T)
    d_time_part = d_time_part * mine(silu_time_slope, 1, owners, owner)
    d_hidden_time = small_gather(d_time_part).transpose(1, 0, 2).reshape(owners, width)
    grad_mod = high_dot(cond_act.astype(jnp.float32).T, my_d_mod_all)
    grad_class = high_dot(onehot.astype(jnp.float32).T, my_d_cond)
    grad_second = high_dot(my_act_time.astype(jnp.float32).T, d_cond)
    grad_first = high_dot(my_features.astype(jnp.float32).T, d_hidden_time)
    all_grad_bias = jnp.concatenate(
        [jnp.sum(d_hidden_time, axis=0), jnp.sum(d_cond, axis=0), jnp.sum(d_mod, axis=0), gb_tail]
    )
    grad_bias = mine(all_grad_bias, 0, owners, owner)
    condition_gradient = lax.dynamic_slice_in_dim(d_cond, owner, 1, 0)

    grad_in = seq_gather(g_in.astype(LOW)).astype(jnp.float32).reshape(ranks, rows, 3, span)
    grad_in = grad_in.transpose(1, 2, 0, 3).reshape(rows, 3 * width)
    grad_out = seq_gather(g_out.astype(LOW)).astype(jnp.float32).transpose(1, 0, 2).reshape(rows, width)
    grad_up = seq_gather(g_up.astype(LOW)).astype(jnp.float32).reshape(ranks, rows, owners, unit)
    grad_up = grad_up.transpose(1, 2, 0, 3).reshape(rows, hidden)
    grad_down = seq_gather(g_down.astype(LOW)).astype(jnp.float32).reshape(contract.shape)
    gradients = (grad_first, grad_second, grad_class, grad_mod, grad_in, grad_out, grad_up, grad_down, grad_bias)
    local_sum = sum(jnp.sum(gradient * gradient) for gradient in gradients)
    norm_before = jnp.sqrt(small_sum(local_sum))
    factor = clip_limit / jnp.maximum(norm_before, clip_limit)
    results = [
        adam_step(params[index], moments[index], squares[index], gradients[index], factor)
        for index in range(9)
    ]
    return (
        (output[None], input_gradient[None], condition_gradient, norm_before)
        + gradients
        + tuple(result[0] for result in results)
        + tuple(result[1] for result in results)
        + tuple(result[2] for result in results)
    )


def solution(mesh):
    tokens = P("fsdp", "seq", None)
    rows, columns = P("fsdp", None), P(None, "fsdp")
    weights = (rows, rows, columns, columns, rows, rows, rows, rows, P("fsdp"))
    return jax.shard_map(
        per_device,
        mesh=mesh,
        in_specs=(tokens, P("fsdp"), P("fsdp"), tokens) + weights * 3,
        out_specs=(tokens, tokens, rows, P()) + weights * 4,
        check_vma=False,
    )
```

time: 3290 us -> 829 us (0.25)
  waiting for transfers between devices: 2770 us -> 158 us
  starting transfers between devices: 18.5 us -> 207 us
  local copies, waits for them, and re-layouts: 88.5 us -> 187 us
  blocking collectives: 98.2 us -> 0 us
    reduce_scatter x8 -> x0, waiting for transfers between devices: 1800 us -> none  [the longest x1 512 us: per_device(): lax.psum_scatter(g_mod, 'fsdp', scatter_dimension=1, tiled=True)]
    all_gather x7 -> x0, waiting for transfers between devices: 599 us -> none  [the longest x1 215 us: per_device(): lax.all_gather(modulation.astype(low_type), 'fsdp', axis=1, tiled=True)]
    psum x1 -> x0, waiting for transfers between devices: 225 us -> none  [per_device(): lax.psum((s_first, s_second, s_class, s_mod, s_in, s_out, s_up, s_down, s...]
    ppermute x0 -> x132, starting transfers between devices: none -> 207 us  [the longest x12 48.2 us: scatter_rows(): rise_in = hop(rise.astype(LOW), perm=Z_UP).astype(jnp.float32)]
    ppermute x0 -> x132, waiting for transfers between devices: none -> 158 us  [the longest x4 47.2 us: scatter_rows(): got = hop(pick(parts, 1 - y, 1).astype(LOW), perm=SWAP_Y)]
    all_to_all x4 -> x0, waiting for transfers between devices: 81.8 us -> none  [the longest x1 35.5 us: per_device(): lax.all_to_all(d_grouped, 'seq', split_axis=1, concat_axis=3, tiled=True)]
    unnamed x18 -> x0, waiting for transfers between devices: 70.1 us -> none
    all_gather x2 -> x0, blocking collectives: 65.9 us -> none  [the longest x1 33.1 us: per_device(): lax.all_gather(biases.astype(low_type), 'fsdp', axis=0, tiled=True)]
  transfers between devices with their start and end apart: 21 -> 132, of which waited for: 19 -> 47; matrix products, arithmetic and copies ran while one was open for 5% -> 41% of each run, Pallas kernels for 0% -> 0%
where the time goes in v1:
time: 829 us; the launch traced here: 816 us
  starting transfers between devices  207 us (25%)
  local copies, waits for them, and re-layouts  187 us (23%)
  waiting for transfers between devices  158 us (19%)
  other arithmetic  125 us (15%)
  matrix products  125 us (15%)
  between operations  14.4 us (2%)
    dot_general x28, matrix products, mixed_dot(): return jnp.einsum(form, left, right, preferred_element_type=jnp.float32)  113 us
    dynamic_update_slice x52, local copies, waits for them, and re-layouts, place(): return lax.dynamic_update_slice(array, block[(None,) * len(index)], starts)  57.2 us
    ppermute x12, starting transfers between devices, scatter_rows(): rise_in = hop(rise.astype(LOW), perm=Z_UP).astype(jnp.float32)  48.2 us
    ppermute x4, waiting for transfers between devices, scatter_rows(): got = hop(pick(parts, 1 - y, 1).astype(LOW), perm=SWAP_Y)  47.2 us
    sub x9, other arithmetic, adam_step(): weight - learn_rate * (moment_hat / (jnp.sqrt(square_hat) + adam_eps) + w...  31.3 us
    ppermute x12, waiting for transfers between devices, scatter_rows(): fall_in = hop(fall.astype(LOW), perm=Z_DOWN).astype(jnp.float32)  25.8 us
    unnamed x312, local copies, waits for them, and re-layouts  23 us
    ppermute x8, starting transfers between devices, gather_rows(): up3, down3 = (hop(up2, perm=Z_UP), hop(down2, perm=Z_DOWN))  22.6 us
  transfers between devices with their start and end apart: 132, of which 47 were waited for; matrix products, arithmetic and copies ran while one was open for 41% of the time, Pallas kernels for 0%

profile of v1, /device:TPU:0, one launch (start us, length us, event | category | flops | bytes accessed | tf_op | source)
XLA Modules:
  0.0 816.4 jit_solution(14666831210921264680)
XLA Ops:
  0.7 4.7 reshape.427
  75.6 4.6 collective-permute-start.33
  96.0 4.5 collective-permute-start.36
  112.1 4.6 collective-permute-start.11
  136.9 5.2 collective-permute-start.53
  157.5 4.7 collective-permute-start.14
  185.6 7.0 collective-permute-done.64
  195.8 4.8 collective-permute-start.46
  207.0 4.4 collective-permute-start.56
  217.0 4.4 collective-permute-start.23
  229.3 4.2 collective-permute-start.49
  247.0 4.4 collective-permute-start.59
  269.6 8.1 multiply_reduce_fusion.1
  277.7 8.5 %fusion.30 = f32[4,1024]{1,0:T(4,128)S(1)} fusion(f32[4,1024,1024]{1,2,0:T(8,128)} %get-tuple-element.349, f32[4,1024]{1,0:T(4,128)S(1)} %get-tuple-element.348), kind=kLoop, calls=%fused_computation.34 | loop fusion | flops 12578816 | bytes 16809984 | tf_op jit(solution)/shard_map/reduce_sum | solution.py:201
  286.8 8.6 %fusion.76 = bf16[4,72,1024]{2,1,0:T(8,128)(2,1)} fusion(bf16[1024,4,72]{0,2,1:T(8,128)(2,1)S(1)} %bitcast.518, f32[4,1024,1024]{1,2,0:T(8,128)} %get-tuple-element.349, f32[4,1024]{1,0:T(4,128)S(1)} %fusion.30, f32[4,1024]{1,0:T(4,128)S(1)} %get-tuple-element.348), kind=kOutput, calls=%fused_computation.133 | convolution fusion | flops 621051904 | bytes 17989632 | tf_op jit(solution)/shard_map/hqk,khd->qhd/dot_general | solution.py:67
  312.7 5.7 collective-permute-done.26
  320.6 9.1 %fusion.193 = (f32[1024]{0:T(1024)S(1)}, f32[1024,1152]{1,0:T(8,128)S(1)}, bf16[1024,1152]{1,0:T(8,128)(2,1)}, f32[1024,1152]{1,0:T(8,128)}) fusion(f32[1152]{0:T(1024)S(1)} %copy-done.124, bf16[4,256,1152]{2,1,0:T(8,128)(2,1)S(1)} %bitcast_dynamic-update-slice_fusion.13, f32[1152]{0:T(1024)S(1)} %copy-done.126, f32[1152]{0:T(1024)S(1)} %copy-done.102, ...), kind=kOutput, calls=%fused_computation.478 | convolution fusion | flops 2729704448 | bytes 19200000 | tf_op jit(solution)/shard_map/td,de->te/dot_general | solution.py:67
  332.0 8.7 %fusion.46 = (bf16[1152,1024]{0,1:T(8,128)(2,1)}, f32[1024,1152]{1,0:T(8,128)S(1)}) fusion(f32[1152]{0:T(1024)S(1)} %copy-done.145, bf16[1152,1152]{1,0:T(8,128)(2,1)} %bitcast.49, f32[1024,1152]{1,0:T(8,128)S(1)} %subtract_multiply_fusion, f32[1152]{0:T(1024)S(1)} %copy-done.144, f32[1152]{0:T(1024)S(1)} %copy-done.112), kind=kOutput, calls=%fused_computation.54 | convolution fusion | flops 2733244416 | bytes 14464512 | tf_op jit(solution)/shard_map/td,df->tf/dot_general | solution.py:67
  340.6 8.2 %convert_reduce_fusion.2 = (f32[1152]{0:T(1024)}, bf16[1024,1152]{1,0:T(8,128)(2,1)S(1)}, bf16[1024,1152]{1,0:T(8,128)(2,1)S(1)}) fusion(f32[1024,1152]{1,0:T(8,128)S(1)} %get-tuple-element.360, bf16[1024,1152]{1,0:T(8,128)(2,1)S(1)} %bitcast.545, bf16[1152,1152]{1,0:T(8,128)(2,1)} %bitcast.59), kind=kOutput, calls=%fused_computation.71 | convolution fusion | flops 2746219520 | bytes 14455296 | tf_op jit(solution)/shard_map/td,fd->tf/dot_general | solution.py:67
  348.8 5.2 fusion.196
  355.9 5.7 fusion.111
  361.6 5.3 fusion.197
  370.2 4.8 copy.203
  375.1 4.9 fusion.198
  400.4 19.3 %collective-permute-done.114 = bf16[4,144,1152]{2,1,0:T(8,128)(2,1)} collective-permute-done((bf16[4,144,1152]{2,1,0:T(8,128)(2,1)}, bf16[4,144,1152]{2,1,0:T(8,128)(2,1)}, u32[]{:S(2)}, u32[]{:S(2)}) %collective-permute-start.114) | collective-permute-done | bytes 1327136 | tf_op jit(solution)/shard_map/ppermute | solution.py:123
  427.1 20.6 %collective-permute-done.104 = bf16[4,144,1152]{2,1,0:T(8,128)(2,1)} collective-permute-done((bf16[4,144,1152]{2,1,0:T(8,128)(2,1)}, bf16[4,144,1152]{2,1,0:T(8,128)(2,1)}, u32[]{:S(2)}, u32[]{:S(2)}) %collective-permute-start.104) | collective-permute-done | bytes 1327136 | tf_op jit(solution)/shard_map/ppermute | solution.py:123
  449.4 4.1 collective-permute-start.105
  454.9 5.5 collective-permute-done.105
  460.4 4.4 collective-permute-start.116
  475.4 4.6 collective-permute-start.117
  481.5 5.2 collective-permute-done.119
  496.0 9.6 %collective-permute-done.120 = bf16[144,1152]{1,0:T(8,128)(2,1)S(1)} collective-permute-done((bf16[144,1152]{1,0:T(8,128)(2,1)S(1)}, bf16[144,1152]{1,0:T(8,128)(2,1)S(1)}, u32[]{:S(2)}, u32[]{:S(2)}) %collective-permute-start.120) | collective-permute-done | bytes 331808 | tf_op jit(solution)/shard_map/ppermute | solution.py:129
  523.1 36.8 %while.15 = (s32[]{:T(128)}, f32[1024,4,72]{0,2,1:T(8,128)S(1)}, f32[1024,4,72]{0,2,1:T(8,128)S(1)}, bf16[2,512,4,72]{1,3,2,0:T(8,128)(2,1)}, bf16[2,512,4,72]{1...) while((s32[]{:T(128)}, f32[1024,4,72]{0,2,1:T(8,128)S(1)}, ...), condition=%wide.region_12.13_spmd.clone, body=%wide.region_10.12_spmd.clone.sunk | while | flops 1536735232 | bytes 164618640 | solution.py:229
  576.0 4.5 fusion.61
  586.9 7.3 collective-permute-done.94
  601.2 5.0 collective-permute-start.96
  616.7 4.1 collective-permute-start.97
  622.9 4.7 reshape.446
  641.3 5.2 copy.230
  646.5 7.2 reshape.442
  684.5 4.4 collective-permute-start.86
  690.4 4.3 collective-permute-done.86
  696.8 5.7 collective-permute-start.87
  706.8 4.8 collective-permute-done.77
  727.3 4.5 multiply_reduce_fusion.4
  780.7 9.2 %multiply_subtract_fusion.1 = (f32[576,1152]{1,0:T(8,128)}, f32[576,1152]{1,0:T(8,128)}, f32[576,1152]{1,0:T(8,128)}, f32[576,1152]{1,0:T(8,128)}) fusion(f32[576,1152]{1,0:T(8,128)} %param.44, f32[]{:T(128)S(6)} %div.225, f32[576,1152]{1,0:T(8,128)} %param.53, f32[576,1152]{1,0:T(8,128)} %param.62, bf16[4,144,1152]{2,1,0:T(8,128)(2,1)S(1)} %copy-done.17), kind=kLoop, calls=%fused_computation.94 | loop fusion | flops 11280384 | bytes 19906564 | tf_op jit(solution)/shard_map/sub | solution.py:244
  795.5 6.1 multiply_subtract_fusion
  809.5 4.7 multiply_subtract_fusion.2
  (876 shorter events, 506.7 us)
Async XLA Ops:
  8.1 124.7 %collective-permute-start.41 = (bf16[144,1152]{1,0:T(8,128)(2,1)}, bf16[144,1152]{1,0:T(8,128)(2,1)}, u32[]{:S(2)}, u32[]{:S(2)}) collective-permute-start(bf16[144,1152]{1,0:T(8,128)(2,1)} %convert_element_type.479), channel_id=1, source_target_pairs={{0,1},{1,0},{2,3},{3,2},{4,5},{5,4},{6,7},{7,6},{8,9},{9,8},{10,11... | collective-permute-start | bytes 995336 | tf_op jit(solution)/shard_map/ppermute | solution.py:96
  11.1 124.2 %collective-permute-start.42 = (bf16[144,1152]{1,0:T(8,128)(2,1)}, bf16[144,1152]{1,0:T(8,128)(2,1)}, u32[]{:S(2)}, u32[]{:S(2)}) collective-permute-start(bf16[144,1152]{1,0:T(8,128)(2,1)} %convert_element_type.479), channel_id=1, source_target_pairs={{2,0},{3,1},{4,2},{5,3},{6,4},{7,5},{10,8},{11,9},{12,10},{13,11},... | collective-permute-start | bytes 995336 | tf_op jit(solution)/shard_map/ppermute | solution.py:95
  15.1 44.5 %collective-permute-start.28 = (bf16[144,288]{1,0:T(8,128)(2,1)}, bf16[144,288]{1,0:T(8,128)(2,1)}, u32[]{:S(2)}, u32[]{:S(2)}) collective-permute-start(bf16[144,288]{1,0:T(8,128)(2,1)} %get-tuple-element.267), channel_id=1, source_target_pairs={{0,1},{1,0},{2,3},{3,2},{4,5},{5,4},{6,7},{7,6},{8,9},{9,8},{10,11... | collective-permute-start | bytes 248840 | tf_op jit(solution)/shard_map/ppermute | solution.py:96
  15.1 46.6 %collective-permute-start.29 = (bf16[144,288]{1,0:T(8,128)(2,1)}, bf16[144,288]{1,0:T(8,128)(2,1)}, u32[]{:S(2)}, u32[]{:S(2)}) collective-permute-start(bf16[144,288]{1,0:T(8,128)(2,1)} %get-tuple-element.267), channel_id=1, source_target_pairs={{2,0},{3,1},{4,2},{5,3},{6,4},{7,5},{10,8},{11,9},{12,10},{13,11},... | collective-permute-start | bytes 248840 | tf_op jit(solution)/shard_map/ppermute | solution.py:95
  17.8 19.2 %collective-permute-start.3 = (f32[1,2306]{1,0:T(1,128)S(1)}, f32[1,2306]{1,0:T(1,128)S(1)}, u32[]{:S(2)}, u32[]{:S(2)}) collective-permute-start(f32[1,2306]{1,0:T(1,128)S(1)} %broadcast_in_dim.267), channel_id=1, source_target_pairs={{0,1},{1,0},{2,3},{3,2},{4,5},{5,4},{6,7},{7,6},{8,9},{9,8},{10,11... | collective-permute-start | bytes 27680 | tf_op jit(solution)/shard_map/ppermute | solution.py:143
  59.6 52.5 %collective-permute-start.15 = (bf16[144,864]{1,0:T(8,128)(2,1)}, bf16[144,864]{1,0:T(8,128)(2,1)}, u32[]{:S(2)}, u32[]{:S(2)}) collective-permute-start(bf16[144,864]{1,0:T(8,128)(2,1)} %convert_element_type.470), channel_id=1, source_target_pairs={{0,1},{1,0},{2,3},{3,2},{4,5},{5,4},{6,7},{7,6},{8,9},{9,8},{10,11... | collective-permute-start | bytes 746504 | tf_op jit(solution)/shard_map/ppermute | solution.py:96
  102.1 34.8 %collective-permute-start.43 = (bf16[144,1152]{1,0:T(8,128)(2,1)}, bf16[144,1152]{1,0:T(8,128)(2,1)S(1)}, u32[]{:S(2)}, u32[]{:S(2)}) collective-permute-start(bf16[144,1152]{1,0:T(8,128)(2,1)} %convert_element_type.479), channel_id=1, source_target_pairs={{0,2},{1,3},{2,4},{3,5},{4,6},{5,7},{8,10},{9,11},{10,12},{11,13},... | collective-permute-start | bytes 995336 | tf_op jit(solution)/shard_map/ppermute | solution.py:95
  126.1 52.6 %collective-permute-start = (bf16[256,1152]{1,0:T(8,128)(2,1)S(1)}, bf16[256,1152]{1,0:T(8,128)(2,1)}, u32[]{:S(2)}, u32[]{:S(2)}) collective-permute-start(bf16[256,1152]{1,0:T(8,128)(2,1)S(1)} %bitcast.521), channel_id=1, source_target_pairs={{0,8},{8,0},{16,24},{24,16},{1,9},{9,1},{17,25},{25,17},{2,10},{10... | collective-permute-start | bytes 1769480 | tf_op jit(solution)/shard_map/ppermute | solution.py:174
  131.2 52.3 %collective-permute-start.1 = (bf16[256,1152]{1,0:T(8,128)(2,1)S(1)}, bf16[256,1152]{1,0:T(8,128)(2,1)}, u32[]{:S(2)}, u32[]{:S(2)}) collective-permute-start(bf16[256,1152]{1,0:T(8,128)(2,1)S(1)} %bitcast.522), channel_id=1, source_target_pairs={{0,16},{8,24},{16,0},{24,8},{1,17},{9,25},{17,1},{25,9},{2,18},{10... | collective-permute-start | bytes 1769480 | tf_op jit(solution)/shard_map/ppermute | solution.py:173
  146.2 28.4 %collective-permute-start.18 = (bf16[144,864]{1,0:T(8,128)(2,1)}, bf16[144,864]{1,0:T(8,128)(2,1)}, u32[]{:S(2)}, u32[]{:S(2)}) collective-permute-start(bf16[144,864]{1,0:T(8,128)(2,1)} %get-tuple-element.273), channel_id=1, source_target_pairs={{0,1},{1,0},{2,3},{3,2},{4,5},{5,4},{6,7},{7,6},{8,9},{9,8},{10,11... | collective-permute-start | bytes 746504 | tf_op jit(solution)/shard_map/ppermute | solution.py:98
  146.8 29.5 %collective-permute-start.19 = (bf16[144,864]{1,0:T(8,128)(2,1)}, bf16[144,864]{1,0:T(8,128)(2,1)}, u32[]{:S(2)}, u32[]{:S(2)}) collective-permute-start(bf16[144,864]{1,0:T(8,128)(2,1)} %collective-permute-done.16), channel_id=1, source_target_pairs={{2,0},{3,1},{4,2},{5,3},{6,4},{7,5},{10,8},{11,9},{12,10},{13,11},... | collective-permute-start | bytes 746504 | tf_op jit(solution)/shard_map/ppermute | solution.py:99
  176.3 16.3 %collective-permute-start.64 = (bf16[256,1152]{1,0:T(8,128)(2,1)S(1)}, bf16[256,1152]{1,0:T(8,128)(2,1)}, u32[]{:S(2)}, u32[]{:S(2)}) collective-permute-start(bf16[256,1152]{1,0:T(8,128)(2,1)S(1)} %bitcast.537), channel_id=1, source_target_pairs={{0,16},{8,24},{16,0},{24,8},{1,17},{9,25},{17,1},{25,9},{2,18},{10... | collective-permute-start | bytes 1769480 | tf_op jit(solution)/shard_map/ppermute | solution.py:173
  176.8 65.1 %collective-permute-start.38 = (bf16[1152,288]{0,1:T(8,128)(2,1)}, bf16[1152,288]{0,1:T(8,128)(2,1)S(1)}, u32[]{:S(2)}, u32[]{:S(2)}) collective-permute-start(bf16[1152,288]{0,1:T(8,128)(2,1)} %copy.182), channel_id=1, source_target_pairs={{0,8},{8,0},{16,24},{24,16},{1,9},{9,1},{17,25},{25,17},{2,10},{10... | collective-permute-start | bytes 1990664 | tf_op jit(solution)/shard_map/ppermute | solution.py:174
  178.8 78.5 %collective-permute-start.39 = (bf16[1152,288]{0,1:T(8,128)(2,1)}, bf16[1152,288]{0,1:T(8,128)(2,1)}, u32[]{:S(2)}, u32[]{:S(2)}) collective-permute-start(bf16[1152,288]{0,1:T(8,128)(2,1)} %copy.182), channel_id=1, source_target_pairs={{0,16},{8,24},{16,0},{24,8},{1,17},{9,25},{17,1},{25,9},{2,18},{10... | collective-permute-start | bytes 1990664 | tf_op jit(solution)/shard_map/ppermute | solution.py:173
  183.6 28.6 %collective-permute-start.54 = (bf16[144,1152]{1,0:T(8,128)(2,1)S(1)}, bf16[144,1152]{1,0:T(8,128)(2,1)S(1)}, u32[]{:S(2)}, u32[]{:S(2)}) collective-permute-start(bf16[144,1152]{1,0:T(8,128)(2,1)S(1)} %copy-done.87), channel_id=1, source_target_pairs={{0,1},{1,0},{2,3},{3,2},{4,5},{5,4},{6,7},{7,6},{8,9},{9,8},{10,11... | collective-permute-start | bytes 995336 | tf_op jit(solution)/shard_map/ppermute | solution.py:98
  224.4 37.6 %collective-permute-start.2 = (bf16[256,1152]{1,0:T(8,128)(2,1)}, bf16[256,1152]{1,0:T(8,128)(2,1)S(1)}, u32[]{:S(2)}, u32[]{:S(2)}) collective-permute-start(bf16[256,1152]{1,0:T(8,128)(2,1)} %collective-permute-done.1), channel_id=1, source_target_pairs={{0,8},{8,0},{16,24},{24,16},{1,9},{9,1},{17,25},{25,17},{2,10},{10... | collective-permute-start | bytes 1769480 | tf_op jit(solution)/shard_map/ppermute | solution.py:175
  236.5 66.7 %collective-permute-start.65 = (bf16[256,1152]{1,0:T(8,128)(2,1)}, bf16[256,1152]{1,0:T(8,128)(2,1)}, u32[]{:S(2)}, u32[]{:S(2)}) collective-permute-start(bf16[256,1152]{1,0:T(8,128)(2,1)} %collective-permute-done.64), channel_id=1, source_target_pairs={{0,8},{8,0},{16,24},{24,16},{1,9},{9,1},{17,25},{25,17},{2,10},{10... | collective-permute-start | bytes 1769480 | tf_op jit(solution)/shard_map/ppermute | solution.py:175
  256.0 53.0 %collective-permute-start.50 = (bf16[144,1152]{1,0:T(8,128)(2,1)}, bf16[144,1152]{1,0:T(8,128)(2,1)}, u32[]{:S(2)}, u32[]{:S(2)}) collective-permute-start(bf16[144,1152]{1,0:T(8,128)(2,1)} %get-tuple-element.277), channel_id=1, source_target_pairs={{0,1},{1,0},{2,3},{3,2},{4,5},{5,4},{6,7},{7,6},{8,9},{9,8},{10,11... | collective-permute-start | bytes 995336 | tf_op jit(solution)/shard_map/ppermute | solution.py:104
  257.2 53.7 %collective-permute-start.60 = (bf16[144,1152]{1,0:T(8,128)(2,1)}, bf16[144,1152]{1,0:T(8,128)(2,1)}, u32[]{:S(2)}, u32[]{:S(2)}) collective-permute-start(bf16[144,1152]{1,0:T(8,128)(2,1)} %get-tuple-element.251), channel_id=1, source_target_pairs={{0,1},{1,0},{2,3},{3,2},{4,5},{5,4},{6,7},{7,6},{8,9},{9,8},{10,11... | collective-permute-start | bytes 995336 | tf_op jit(solution)/shard_map/ppermute | solution.py:104
  261.2 57.2 %collective-permute-start.40 = (bf16[1152,288]{0,1:T(8,128)(2,1)}, bf16[1152,288]{0,1:T(8,128)(2,1)}, u32[]{:S(2)}, u32[]{:S(2)}) collective-permute-start(bf16[1152,288]{0,1:T(8,128)(2,1)} %collective-permute-done.39), channel_id=1, source_target_pairs={{0,8},{8,0},{16,24},{24,16},{1,9},{9,1},{17,25},{25,17},{2,10},{10... | collective-permute-start | bytes 1990664 | tf_op jit(solution)/shard_map/ppermute | solution.py:175
  299.7 20.7 %collective-permute-start.25 = (bf16[1024,288]{0,1:T(8,128)(2,1)}, bf16[1024,288]{0,1:T(8,128)(2,1)S(1)}, u32[]{:S(2)}, u32[]{:S(2)}) collective-permute-start(bf16[1024,288]{0,1:T(8,128)(2,1)} %bitcast.551), channel_id=1, source_target_pairs={{0,8},{8,0},{16,24},{24,16},{1,9},{9,1},{17,25},{25,17},{2,10},{10... | collective-permute-start | bytes 1769480 | tf_op jit(solution)/shard_map/ppermute | solution.py:174
  355.4 37.9 %collective-permute-start.61 = (bf16[2,256,1152]{2,1,0:T(8,128)(2,1)}, bf16[2,256,1152]{2,1,0:T(8,128)(2,1)}, u32[]{:S(2)}, u32[]{:S(2)}) collective-permute-start(bf16[2,256,1152]{2,1,0:T(8,128)(2,1)} %fusion.86), channel_id=1, source_target_pairs={{0,8},{8,0},{16,24},{24,16},{1,9},{9,1},{17,25},{25,17},{2,10},{10... | collective-permute-start | bytes 3538952 | tf_op jit(solution)/shard_map/ppermute | solution.py:190
  370.2 26.6 %collective-permute-start.66 = (bf16[2,256,1152]{2,1,0:T(8,128)(2,1)}, bf16[2,256,1152]{2,1,0:T(8,128)(2,1)}, u32[]{:S(2)}, u32[]{:S(2)}) collective-permute-start(bf16[2,256,1152]{2,1,0:T(8,128)(2,1)} %fusion.85), channel_id=1, source_target_pairs={{0,8},{8,0},{16,24},{24,16},{1,9},{9,1},{17,25},{25,17},{2,10},{10... | collective-permute-start | bytes 3538952 | tf_op jit(solution)/shard_map/ppermute | solution.py:190
  387.4 32.3 %collective-permute-start.114 = (bf16[4,144,1152]{2,1,0:T(8,128)(2,1)}, bf16[4,144,1152]{2,1,0:T(8,128)(2,1)}, u32[]{:S(2)}, u32[]{:S(2)}) collective-permute-start(bf16[4,144,1152]{2,1,0:T(8,128)(2,1)} %fusion.75), channel_id=1, source_target_pairs={{0,1},{1,0},{2,3},{3,2},{4,5},{5,4},{6,7},{7,6},{8,9},{9,8},{10,11... | collective-permute-start | bytes 3981320 | tf_op jit(solution)/shard_map/ppermute | solution.py:123
  391.6 56.2 %collective-permute-start.104 = (bf16[4,144,1152]{2,1,0:T(8,128)(2,1)}, bf16[4,144,1152]{2,1,0:T(8,128)(2,1)}, u32[]{:S(2)}, u32[]{:S(2)}) collective-permute-start(bf16[4,144,1152]{2,1,0:T(8,128)(2,1)} %fusion.74), channel_id=1, source_target_pairs={{0,1},{1,0},{2,3},{3,2},{4,5},{5,4},{6,7},{7,6},{8,9},{9,8},{10,11... | collective-permute-start | bytes 3981320 | tf_op jit(solution)/shard_map/ppermute | solution.py:123
  395.8 72.9 %collective-permute-start.62 = (bf16[256,1152]{1,0:T(8,128)(2,1)S(1)}, bf16[256,1152]{1,0:T(8,128)(2,1)S(1)}, u32[]{:S(2)}, u32[]{:S(2)}) collective-permute-start(bf16[256,1152]{1,0:T(8,128)(2,1)S(1)} %fusion.113), channel_id=1, source_target_pairs={{0,16},{8,24},{16,0},{24,8},{1,17},{9,25},{17,1},{25,9},{2,18},{10... | collective-permute-start | bytes 1769480 | tf_op jit(solution)/shard_map/ppermute | solution.py:192
  399.3 65.6 %collective-permute-start.67 = (bf16[256,1152]{1,0:T(8,128)(2,1)S(1)}, bf16[256,1152]{1,0:T(8,128)(2,1)S(1)}, u32[]{:S(2)}, u32[]{:S(2)}) collective-permute-start(bf16[256,1152]{1,0:T(8,128)(2,1)S(1)} %fusion.115), channel_id=1, source_target_pairs={{0,16},{8,24},{16,0},{24,8},{1,17},{9,25},{17,1},{25,9},{2,18},{10... | collective-permute-start | bytes 1769480 | tf_op jit(solution)/shard_map/ppermute | solution.py:192
  421.3 32.2 %collective-permute-start.115 = (bf16[144,1152]{1,0:T(8,128)(2,1)S(1)}, bf16[144,1152]{1,0:T(8,128)(2,1)S(1)}, u32[]{:S(2)}, u32[]{:S(2)}) collective-permute-start(bf16[144,1152]{1,0:T(8,128)(2,1)S(1)} %get-tuple-element.289), channel_id=1, source_target_pairs={{0,2},{1,3},{2,4},{3,5},{4,6},{5,7},{8,10},{9,11},{10,12},{11,13},... | collective-permute-start | bytes 995336 | tf_op jit(solution)/shard_map/ppermute | solution.py:128
  425.5 47.4 %collective-permute-start.118 = (bf16[144,1152]{1,0:T(8,128)(2,1)S(1)}, bf16[144,1152]{1,0:T(8,128)(2,1)S(1)}, u32[]{:S(2)}, u32[]{:S(2)}) collective-permute-start(bf16[144,1152]{1,0:T(8,128)(2,1)S(1)} %get-tuple-element.290), channel_id=1, source_target_pairs={{2,0},{3,1},{4,2},{5,3},{6,4},{7,5},{10,8},{11,9},{12,10},{13,11},... | collective-permute-start | bytes 995336 | tf_op jit(solution)/shard_map/ppermute | solution.py:129
  453.5 21.9 %collective-permute-start.108 = (bf16[144,1152]{1,0:T(8,128)(2,1)S(1)}, bf16[144,1152]{1,0:T(8,128)(2,1)S(1)}, u32[]{:S(2)}, u32[]{:S(2)}) collective-permute-start(bf16[144,1152]{1,0:T(8,128)(2,1)S(1)} %get-tuple-element.294), channel_id=1, source_target_pairs={{2,0},{3,1},{4,2},{5,3},{6,4},{7,5},{10,8},{11,9},{12,10},{13,11},... | collective-permute-start | bytes 995336 | tf_op jit(solution)/shard_map/ppermute | solution.py:129
  472.6 21.8 %collective-permute-start.68 = (bf16[256,1152]{1,0:T(8,128)(2,1)S(1)}, bf16[256,1152]{1,0:T(8,128)(2,1)S(1)}, u32[]{:S(2)}, u32[]{:S(2)}) collective-permute-start(bf16[256,1152]{1,0:T(8,128)(2,1)S(1)} %get-tuple-element.310), channel_id=1, source_target_pairs={{0,8},{8,0},{16,24},{24,16},{1,9},{9,1},{17,25},{25,17},{2,10},{10... | collective-permute-start | bytes 1769480 | tf_op jit(solution)/shard_map/ppermute | solution.py:174
  472.9 22.8 %collective-permute-start.69 = (bf16[256,1152]{1,0:T(8,128)(2,1)S(1)}, bf16[256,1152]{1,0:T(8,128)(2,1)S(1)}, u32[]{:S(2)}, u32[]{:S(2)}) collective-permute-start(bf16[256,1152]{1,0:T(8,128)(2,1)S(1)} %get-tuple-element.310), channel_id=1, source_target_pairs={{0,16},{8,24},{16,0},{24,8},{1,17},{9,25},{17,1},{25,9},{2,18},{10... | collective-permute-start | bytes 1769480 | tf_op jit(solution)/shard_map/ppermute | solution.py:173
  475.4 20.6 %collective-permute-start.117 = (bf16[144,1152]{1,0:T(8,128)(2,1)S(1)}, bf16[144,1152]{1,0:T(8,128)(2,1)S(1)}, u32[]{:S(2)}, u32[]{:S(2)}) collective-permute-start(bf16[144,1152]{1,0:T(8,128)(2,1)S(1)} %get-tuple-element.287), channel_id=1, source_target_pairs={{0,2},{1,3},{2,4},{3,5},{4,6},{5,7},{8,10},{9,11},{10,12},{11,13},... | collective-permute-start | bytes 995336 | tf_op jit(solution)/shard_map/ppermute | solution.py:128
  486.7 20.9 %collective-permute-start.107 = (bf16[144,1152]{1,0:T(8,128)(2,1)S(1)}, bf16[144,1152]{1,0:T(8,128)(2,1)S(1)}, u32[]{:S(2)}, u32[]{:S(2)}) collective-permute-start(bf16[144,1152]{1,0:T(8,128)(2,1)S(1)} %get-tuple-element.291), channel_id=1, source_target_pairs={{0,2},{1,3},{2,4},{3,5},{4,6},{5,7},{8,10},{9,11},{10,12},{11,13},... | collective-permute-start | bytes 995336 | tf_op jit(solution)/shard_map/ppermute | solution.py:128
  494.4 16.7 %collective-permute-start.110 = (bf16[144,1152]{1,0:T(8,128)(2,1)S(1)}, bf16[144,1152]{1,0:T(8,128)(2,1)S(1)}, u32[]{:S(2)}, u32[]{:S(2)}) collective-permute-start(bf16[144,1152]{1,0:T(8,128)(2,1)S(1)} %fusion.107), channel_id=1, source_target_pairs={{2,0},{3,1},{4,2},{5,3},{6,4},{7,5},{10,8},{11,9},{12,10},{13,11},... | collective-permute-start | bytes 995336 | tf_op jit(solution)/shard_map/ppermute | solution.py:129
  495.7 17.4 %collective-permute-start.70 = (bf16[256,1152]{1,0:T(8,128)(2,1)S(1)}, bf16[256,1152]{1,0:T(8,128)(2,1)S(1)}, u32[]{:S(2)}, u32[]{:S(2)}) collective-permute-start(bf16[256,1152]{1,0:T(8,128)(2,1)S(1)} %collective-permute-done.69), channel_id=1, source_target_pairs={{0,8},{8,0},{16,24},{24,16},{1,9},{9,1},{17,25},{25,17},{2,10},{10... | collective-permute-start | bytes 1769480 | tf_op jit(solution)/shard_map/ppermute | solution.py:175
  506.6 76.3 %collective-permute-start.121 = (bf16[144,1152]{1,0:T(8,128)(2,1)}, bf16[144,1152]{1,0:T(8,128)(2,1)}, u32[]{:S(2)}, u32[]{:S(2)}) collective-permute-start(bf16[144,1152]{1,0:T(8,128)(2,1)} %get-tuple-element.243), channel_id=1, source_target_pairs={{0,8},{8,0},{16,24},{24,16},{1,9},{9,1},{17,25},{25,17},{2,10},{10... | collective-permute-start | bytes 995336 | tf_op jit(solution)/shard_map/ppermute | solution.py:174
  506.6 88.8 %collective-permute-start.122 = (bf16[144,1152]{1,0:T(8,128)(2,1)}, bf16[144,1152]{1,0:T(8,128)(2,1)}, u32[]{:S(2)}, u32[]{:S(2)}) collective-permute-start(bf16[144,1152]{1,0:T(8,128)(2,1)} %get-tuple-element.243), channel_id=1, source_target_pairs={{0,16},{8,24},{16,0},{24,8},{1,17},{9,25},{17,1},{25,9},{2,18},{10... | collective-permute-start | bytes 995336 | tf_op jit(solution)/shard_map/ppermute | solution.py:173
  512.1 89.1 %collective-permute-start.111 = (bf16[144,1152]{1,0:T(8,128)(2,1)}, bf16[144,1152]{1,0:T(8,128)(2,1)}, u32[]{:S(2)}, u32[]{:S(2)}) collective-permute-start(bf16[144,1152]{1,0:T(8,128)(2,1)} %get-tuple-element.245), channel_id=1, source_target_pairs={{0,8},{8,0},{16,24},{24,16},{1,9},{9,1},{17,25},{25,17},{2,10},{10... | collective-permute-start | bytes 995336 | tf_op jit(solution)/shard_map/ppermute | solution.py:174
  512.1 95.1 %collective-permute-start.112 = (bf16[144,1152]{1,0:T(8,128)(2,1)}, bf16[144,1152]{1,0:T(8,128)(2,1)}, u32[]{:S(2)}, u32[]{:S(2)}) collective-permute-start(bf16[144,1152]{1,0:T(8,128)(2,1)} %get-tuple-element.245), channel_id=1, source_target_pairs={{0,16},{8,24},{16,0},{24,8},{1,17},{9,25},{17,1},{25,9},{2,18},{10... | collective-permute-start | bytes 995336 | tf_op jit(solution)/shard_map/ppermute | solution.py:173
  586.9 43.6 %collective-permute-start.71 = (bf16[2,256,1152]{2,1,0:T(8,128)(2,1)}, bf16[2,256,1152]{2,1,0:T(8,128)(2,1)}, u32[]{:S(2)}, u32[]{:S(2)}) collective-permute-start(bf16[2,256,1152]{2,1,0:T(8,128)(2,1)} %fusion.87), channel_id=1, source_target_pairs={{0,8},{8,0},{16,24},{24,16},{1,9},{9,1},{17,25},{25,17},{2,10},{10... | collective-permute-start | bytes 3538952 | tf_op jit(solution)/shard_map/ppermute | solution.py:190
  612.7 54.1 %collective-permute-start.84 = (bf16[4,144,864]{2,1,0:T(8,128)(2,1)}, bf16[4,144,864]{2,1,0:T(8,128)(2,1)}, u32[]{:S(2)}, u32[]{:S(2)}) collective-permute-start(bf16[4,144,864]{2,1,0:T(8,128)(2,1)} %fusion.91), channel_id=1, source_target_pairs={{0,1},{1,0},{2,3},{3,2},{4,5},{5,4},{6,7},{7,6},{8,9},{9,8},{10,11... | collective-permute-start | bytes 2985992 | tf_op jit(solution)/shard_map/ppermute | solution.py:123
  634.6 34.5 %collective-permute-start.72 = (bf16[256,1152]{1,0:T(8,128)(2,1)S(1)}, bf16[256,1152]{1,0:T(8,128)(2,1)}, u32[]{:S(2)}, u32[]{:S(2)}) collective-permute-start(bf16[256,1152]{1,0:T(8,128)(2,1)S(1)} %fusion.116), channel_id=1, source_target_pairs={{0,16},{8,24},{16,0},{24,8},{1,17},{9,25},{17,1},{25,9},{2,18},{10... | collective-permute-start | bytes 1769480 | tf_op jit(solution)/shard_map/ppermute | solution.py:192
  639.5 17.5 %collective-permute-start.101 = (bf16[144,288]{1,0:T(8,128)(2,1)S(1)}, bf16[144,288]{1,0:T(8,128)(2,1)S(1)}, u32[]{:S(2)}, u32[]{:S(2)}) collective-permute-start(bf16[144,288]{1,0:T(8,128)(2,1)S(1)} %fusion.134), channel_id=1, source_target_pairs={{0,8},{8,0},{16,24},{24,16},{1,9},{9,1},{17,25},{25,17},{2,10},{10... | collective-permute-start | bytes 248840 | tf_op jit(solution)/shard_map/ppermute | solution.py:174
  639.5 23.9 %collective-permute-start.103 = (bf16[144,288]{1,0:T(8,128)(2,1)S(1)}, bf16[144,288]{1,0:T(8,128)(2,1)S(1)}, u32[]{:S(2)}, u32[]{:S(2)}) collective-permute-start(bf16[144,288]{1,0:T(8,128)(2,1)S(1)} %collective-permute-done.102), channel_id=1, source_target_pairs={{0,8},{8,0},{16,24},{24,16},{1,9},{9,1},{17,25},{25,17},{2,10},{10... | collective-permute-start | bytes 248840 | tf_op jit(solution)/shard_map/ppermute | solution.py:175
  696.8 22.9 %collective-permute-start.87 = (bf16[144,864]{1,0:T(8,128)(2,1)}, bf16[144,864]{1,0:T(8,128)(2,1)}, u32[]{:S(2)}, u32[]{:S(2)}) collective-permute-start(bf16[144,864]{1,0:T(8,128)(2,1)} %get-tuple-element.296), channel_id=1, source_target_pairs={{0,2},{1,3},{2,4},{3,5},{4,6},{5,7},{8,10},{9,11},{10,12},{11,13},... | collective-permute-start | bytes 746504 | tf_op jit(solution)/shard_map/ppermute | solution.py:128
  722.7 28.0 %collective-permute-start.91 = (bf16[144,864]{1,0:T(8,128)(2,1)S(1)}, bf16[144,864]{1,0:T(8,128)(2,1)S(1)}, u32[]{:S(2)}, u32[]{:S(2)}) collective-permute-start(bf16[144,864]{1,0:T(8,128)(2,1)S(1)} %get-tuple-element.247), channel_id=1, source_target_pairs={{0,8},{8,0},{16,24},{24,16},{1,9},{9,1},{17,25},{25,17},{2,10},{10... | collective-permute-start | bytes 746504 | tf_op jit(solution)/shard_map/ppermute | solution.py:174
  722.7 28.0 %collective-permute-start.92 = (bf16[144,864]{1,0:T(8,128)(2,1)S(1)}, bf16[144,864]{1,0:T(8,128)(2,1)S(1)}, u32[]{:S(2)}, u32[]{:S(2)}) collective-permute-start(bf16[144,864]{1,0:T(8,128)(2,1)S(1)} %get-tuple-element.247), channel_id=1, source_target_pairs={{0,16},{8,24},{16,0},{24,8},{1,17},{9,25},{17,1},{25,9},{2,18},{10... | collective-permute-start | bytes 746504 | tf_op jit(solution)/shard_map/ppermute | solution.py:173
  (248 other events, 2403.5 us)

commit v2 on v1

v2 whole, which is shorter than its diff:
```python
from functools import partial
import math

import jax
import jax.numpy as jnp
from jax import lax
from jax.experimental import pallas as pl
from jax.experimental.pallas import tpu as pltpu
from jax.sharding import PartitionSpec as P

H = 16
HD = 72
FREQ = 256
NCLS = 1000
STEP = 10


HIGH = lax.Precision.HIGHEST
LOW = jnp.bfloat16
norm_eps = 1e-06
beta_one = 0.9
beta_two = 0.999
learn_rate = 0.04
weight_decay = 0.01
adam_eps = 1e-08
clip_limit = 1.0


def layer_norm(value):
    centre = value - jnp.mean(value, axis=-1, keepdims=True)
    spread = jnp.mean(centre * centre, axis=-1, keepdims=True)
    inverse = lax.rsqrt(spread + norm_eps)
    return centre * inverse, inverse


def layer_norm_back(norm, inverse, grad):
    first = jnp.mean(grad, axis=-1, keepdims=True)
    second = jnp.mean(grad * norm, axis=-1, keepdims=True)
    return inverse * (grad - first - norm * second)


def silu_parts(value):
    gate = jax.nn.sigmoid(value)
    return value * gate, gate * (1.0 + value * (1.0 - gate))


def time_features(timesteps):
    half = FREQ // 2
    freqs = jnp.exp(-math.log(10000.0) * jnp.arange(half, dtype=jnp.float32) / half)
    angles = timesteps.astype(jnp.float32)[:, None] * freqs[None, :]
    return jnp.concatenate([jnp.cos(angles), jnp.sin(angles)], axis=-1)


def split_biases(biases, width, hidden):
    widths = [width, width, 6 * width, width, width, width, hidden, width]
    pieces = []
    start = 0
    for length in widths:
        pieces.append(biases[start : start + length])
        start = start + length
    return pieces


def high_dot(left, right):
    return jnp.dot(left, right, precision=HIGH, preferred_element_type=jnp.float32)


def mixed_dot(form, left, right):
    return jnp.einsum(form, left, right, preferred_element_type=jnp.float32)


def pick(array, index, axis=0):
    return lax.dynamic_index_in_dim(array, index, axis, keepdims=False)


def mine(array, axis, parts, index):
    size = array.shape[axis] // parts
    return lax.dynamic_slice_in_dim(array, index * size, size, axis)


HBM = pl.BlockSpec(memory_space=pl.ANY)
VMEM = pl.BlockSpec(memory_space=pltpu.VMEM)
DMA = pltpu.SemaphoreType.DMA
F32 = jnp.float32


def fast():
    return lax.axis_size("fsdp") == 8 and lax.axis_size("seq") == 4


def places():
    owner, rank = lax.axis_index("fsdp"), lax.axis_index("seq")
    return owner, rank, lax.div(owner, 2), lax.rem(owner, 2), lax.div(rank, 2), lax.rem(rank, 2)


def remote(src, dst, sent, landed, **where):
    return pltpu.make_async_remote_copy(
        src_ref=src, dst_ref=dst, send_sem=sent, recv_sem=landed, device_id=where, device_id_type=pl.DeviceIdType.MESH
    )


def arrived(dst, landed, **where):
    remote(dst, dst, landed, landed, **where).wait_recv()


def greet(over_owners, over_ranks):
    owner, rank, *_ = places()
    barrier = pltpu.get_barrier_semaphore()
    count = 0
    if over_owners:
        for step in range(1, 8):
            pl.semaphore_signal(
                barrier, inc=1, device_id={"fsdp": lax.rem(owner + step, 8)}, device_id_type=pl.DeviceIdType.MESH
            )
        count += 7
    if over_ranks:
        for step in range(1, 4):
            pl.semaphore_signal(
                barrier, inc=1, device_id={"seq": lax.rem(rank + step, 4)}, device_id_type=pl.DeviceIdType.MESH
            )
        count += 3
    pl.semaphore_wait(barrier, count)


def run_all(parts):
    parts = list(parts)
    while parts:
        for part in list(parts):
            try:
                next(part)
            except StopIteration:
                parts.remove(part)


class Sends:
    def __init__(self):
        self.live = []

    def start(self, copy, when=None):
        self.live.append((copy, when))
        if when is None:
            copy.start()
        else:
            pl.when(when)(copy.start)

    def finish(self):
        for copy, when in self.live:
            wait = copy.wait_send if hasattr(copy, "wait_send") else copy.wait
            if when is None:
                wait()
            else:
                pl.when(when)(wait)


def gather_owners(src, out, sems):
    own_sem, sent, landed = sems
    owner, rank, z, y, x, core = places()
    mate = owner + 1 - 2 * y
    sends = Sends()
    local = pltpu.make_async_copy(src, out.at[owner], own_sem)
    local.start()
    sends.start(remote(src, out.at[owner], sent.at[0, 0], landed.at[owner], fsdp=owner + 2), z < 3)
    sends.start(remote(src, out.at[owner], sent.at[0, 1], landed.at[owner], fsdp=owner - 2), z > 0)
    sends.start(remote(src, out.at[owner], sent.at[0, 2], landed.at[owner], fsdp=mate))
    yield
    for far in (1, 2, 3):
        for sign in (-1, 1):
            block = owner + sign * 2 * far
            here = (z >= far) if sign < 0 else (z + far <= 3)
            on = (z < 3) if sign < 0 else (z > 0)
            at = far if sign < 0 else 3 + far
            pl.when(here)(lambda: arrived(out.at[block], landed.at[block], fsdp=mate))
            sends.start(
                remote(out.at[block], out.at[block], sent.at[at, 0], landed.at[block], fsdp=owner - sign * 2), here & on
            )
            sends.start(remote(out.at[block], out.at[block], sent.at[at, 2], landed.at[block], fsdp=mate), here)
            yield
    for step in range(4):
        block = step * 2 + 1 - y
        arrived(out.at[block], landed.at[block], fsdp=mate)
    local.wait()
    sends.finish()


GATHER_OWNERS_SEMS = [DMA(()), DMA((7, 3)), DMA((8,))]


def gather_ranks(src, out, sems, local_copy=True):
    own_sem, sent, landed = sems
    owner, rank, z, y, x, core = places()
    mate, across, last = x * 2 + 1 - core, (1 - x) * 2 + core, (1 - x) * 2 + 1 - core
    sends = Sends()
    local = None
    if local_copy:
        local = pltpu.make_async_copy(src, out.at[rank], own_sem)
        local.start()
    sends.start(remote(src, out.at[rank], sent.at[0], landed.at[rank], seq=across))
    sends.start(remote(src, out.at[rank], sent.at[1], landed.at[rank], seq=mate))
    yield
    yield
    arrived(out.at[across], landed.at[across], seq=across)
    sends.start(remote(out.at[across], out.at[across], sent.at[2], landed.at[across], seq=mate))
    yield
    arrived(out.at[mate], landed.at[mate], seq=mate)
    arrived(out.at[last], landed.at[last], seq=mate)
    if local is not None:
        local.wait()
    sends.finish()


GATHER_RANKS_SEMS = [DMA(()), DMA((3,)), DMA((4,))]


def gather_both(src, out, sems):
    rank = lax.axis_index("seq")
    yield from gather_owners(src, out.at[rank], sems[:3])
    yield from gather_ranks(out.at[rank], out, sems[3:], local_copy=False)


def by_rows(count, body, step=16):
    def one(index, carry):
        body(pl.ds(pl.multiple_of(index * step, step), step))
        return carry

    lax.fori_loop(0, count // step, one, 0)


def scatter_ranks(parts, out, own, mail, leave, enter, sems):
    own_sem, sent, landed = sems
    owner, rank, z, y, x, core = places()
    mate, across = x * 2 + 1 - core, (1 - x) * 2 + core
    sends = Sends()
    loads = []
    for step in (1, 0):
        to = lax.rem(x + step, 2)
        loads.append(pltpu.make_async_copy(parts.at[to * 2 + core], own.at[step], own_sem.at[step]))
        loads[-1].start()
        sends.start(remote(parts.at[to * 2 + 1 - core], mail.at[step], sent.at[step], landed.at[step], seq=mate))
    yield
    loads[0].wait()
    arrived(mail.at[1], landed.at[1], seq=mate)

    def first(rows):
        leave[rows] = (own[1, rows].astype(F32) + mail[1, rows].astype(F32)).astype(LOW)

    by_rows(out.shape[0], first)
    sends.start(remote(leave, enter, sent.at[2], landed.at[2], seq=across))
    yield
    loads[1].wait()
    arrived(mail.at[0], landed.at[0], seq=mate)
    yield
    arrived(enter, landed.at[2], seq=across)

    def last(rows):
        out[rows] = own[0, rows].astype(F32) + mail[0, rows].astype(F32) + enter[rows].astype(F32)

    by_rows(out.shape[0], last)
    sends.finish()


def scatter_ranks_scratch(rows, columns):
    return [
        pltpu.VMEM((2, rows, columns), LOW),
        pltpu.VMEM((2, rows, columns), LOW),
        pltpu.VMEM((rows, columns), LOW),
        pltpu.VMEM((rows, columns), LOW),
        DMA((2,)),
        DMA((3,)),
        DMA((3,)),
    ]


def scatter_owners(parts, out, own, mail, rise, fall, leave, sems):
    own_sem, y_sent, y_landed, z_sent, up_landed, down_landed = sems[:6]
    owner, rank, z, y, x, core = places()
    mate = owner + 1 - 2 * y
    rows_here = own.shape[1]
    sends = Sends()
    loads = {}
    for to in (3, 0, 2, 1):
        sends.start(remote(parts.at[to * 2 + 1 - y], mail.at[to], y_sent.at[to], y_landed.at[to], fsdp=mate))
        loads[to] = pltpu.make_async_copy(parts.at[to * 2 + y], own.at[to], own_sem.at[to])
        loads[to].start()
    yield
    for to, up in ((3, True), (0, False), (2, True), (1, False), (1, True), (2, False)):
        here = (z < to) if up else (z > to)
        more = (z > 0) if up else (z < 3)
        box, box_landed = (rise, up_landed) if up else (fall, down_landed)

        def total(to=to, more=more, box=box, box_landed=box_landed):
            loads[to].wait()
            arrived(mail.at[to], y_landed.at[to], fsdp=mate)

            def start(rows):
                leave[to, rows] = (own[to, rows].astype(F32) + mail[to, rows].astype(F32)).astype(LOW)

            def add(rows):
                leave[to, rows] = (
                    own[to, rows].astype(F32) + mail[to, rows].astype(F32) + box[to, rows].astype(F32)
                ).astype(LOW)

            @pl.when(more)
            def _():
                arrived(box.at[to], box_landed.at[to], fsdp=mate)
                by_rows(rows_here, add)

            @pl.when(jnp.logical_not(more))
            def _():
                by_rows(rows_here, start)

        pl.when(here)(total)
        sends.start(
            remote(
                leave.at[to], box.at[to], z_sent.at[to], box_landed.at[to], fsdp=owner + 2 if up else owner - 2
            ),
            here,
        )
        yield
    for to in range(4):
        at_home = z == to

        @pl.when(at_home)
        def _(to=to):
            loads[to].wait()
            arrived(mail.at[to], y_landed.at[to], fsdp=mate)
            if to > 0:
                arrived(rise.at[to], up_landed.at[to], fsdp=mate)
            if to < 3:
                arrived(fall.at[to], down_landed.at[to], fsdp=mate)

            def end(rows):
                value = own[to, rows].astype(F32) + mail[to, rows].astype(F32)
                if to > 0:
                    value = value + rise[to, rows].astype(F32)
                if to < 3:
                    value = value + fall[to, rows].astype(F32)
                leave[to, rows] = value.astype(LOW)

            by_rows(rows_here, end)

    yield from gather_ranks(leave.at[z], out, sems[6:])
    sends.finish()


def scatter_owners_scratch(rows, columns):
    return [pltpu.VMEM((4, rows, columns), LOW)] * 5 + [DMA((4,))] * 6 + GATHER_RANKS_SEMS


def swap_start(sends, src_of, dst, sent, landed):
    owner = lax.axis_index("fsdp")
    for step in range(1, 8):
        to = lax.rem(owner + step, 8)
        sends.start(remote(src_of(to), dst.at[owner], sent.at[step - 1], landed.at[owner], fsdp=to))


def swap_wait(dst, landed):
    owner = lax.axis_index("fsdp")
    for step in range(1, 8):
        of = lax.rem(owner + step, 8)
        arrived(dst.at[of], landed.at[of], fsdp=of)


SWAP_SEMS = [DMA((7,)), DMA((8,))]


def low_dot(left, right, contract):
    return lax.dot_general(left, right, ((contract[:1], contract[1:]), ((), ())), preferred_element_type=F32)


def fine_dot(left, right, contract):
    high = left.astype(LOW)
    rest = left - high.astype(F32)
    return low_dot(high, right, contract) + low_dot(rest.astype(LOW), right, contract)


def stack_rows(ref):
    return jnp.concatenate([ref[index] for index in range(8)], axis=0)


def condition_forward(note, first, second, table, modulation, outs, scratch, sems):
    notes, act_out, slope_out, cond_cut, cond_out, mod = outs
    send_cut, hid_in, cond_in, bias_cut, mod_cut = scratch
    owner = lax.axis_index("fsdp")
    cut = second.shape[0]
    share = note.shape[2] - 128
    sends = Sends()
    notes[owner] = note[owner]
    swap_start(sends, lambda to: note.at[to], notes, *sems[0:2])
    yield
    swap_wait(notes, sems[1])
    rows = stack_rows(notes)
    feats = rows[:, share : share + first.shape[0]].astype(LOW)
    label = rows[:, share + first.shape[0] : share + first.shape[0] + 1]
    hidden = low_dot(feats, first[...], (1, 0))
    for to in range(8):
        send_cut[0, to] = hidden[:, to * cut : (to + 1) * cut]
        bias_cut[0, to] = rows[0:1, to * cut : (to + 1) * cut]
        bias_cut[1, to] = rows[0:1, (8 + to) * cut : (9 + to) * cut]
    hid_in[owner] = send_cut[0, owner]
    swap_start(sends, lambda to: send_cut.at[0, to], hid_in, *sems[2:4])
    yield
    classes = lax.broadcasted_iota(jnp.int32, (8, table.shape[0]), 1).astype(F32)
    onehot = (label == classes).astype(F32).astype(LOW)
    from_class = low_dot(onehot, table[...], (1, 0))
    swap_wait(hid_in, sems[3])
    hidden_cut = bias_cut[0, owner] + jnp.zeros((8, cut), F32)
    for of in range(8):
        hidden_cut = hidden_cut + hid_in[of]
    act, slope = silu_parts(hidden_cut)
    act = act.astype(LOW)
    act_out[...] = act.astype(F32)
    slope_out[...] = slope
    part = low_dot(act, second[...], (1, 0))
    for to in range(8):
        send_cut[1, to] = part[:, to * cut : (to + 1) * cut]
    cond_in[owner] = send_cut[1, owner]
    swap_start(sends, lambda to: send_cut.at[1, to], cond_in, *sems[4:6])
    yield
    swap_wait(cond_in, sems[5])
    mine_cond = bias_cut[1, owner] + from_class
    for of in range(8):
        mine_cond = mine_cond + cond_in[of]
    cond_cut[owner] = mine_cond
    swap_start(sends, lambda to: cond_cut.at[owner], cond_cut, *sems[6:8])
    yield
    swap_wait(cond_cut, sems[7])
    for of in range(8):
        cond_out[:, of * cut : (of + 1) * cut] = cond_cut[of]
    cond_act = silu_parts(cond_out[...])[0].astype(LOW)
    values = low_dot(cond_act, modulation[...], (1, 0))
    for to in range(8):
        mod_cut[to] = values[to : to + 1]
    mod[owner] = mod_cut[owner]
    swap_start(sends, lambda to: mod_cut.at[to], mod, *sems[8:10])
    yield
    swap_wait(mod, sems[9])
    sends.finish()


def condition_backward(news, second, modulation, cond_cut, time_slope, outs, scratch, sems):
    by_latent, d_cond_out, d_hid_cut, sums = outs
    rank_news, owner_news, d_cut, d_in, d_cond_cut = scratch
    owner, rank, *_ = places()
    cut = second.shape[0]
    wide = modulation.shape[1]
    sends = Sends()
    for step in range(1, 4):
        to = lax.rem(rank + step, 4)
        sends.start(remote(news, rank_news.at[rank], sems[0].at[step - 1], sems[1].at[rank], seq=to))
    yield
    for step in range(1, 4):
        of = lax.rem(rank + step, 4)
        arrived(rank_news.at[of], sems[1].at[of], seq=of)
    rank_news[rank] = news[...]
    for to in range(8):
        owner_news[to] = rank_news[0, to] + rank_news[1, to] + rank_news[2, to] + rank_news[3, to]
    by_latent[owner] = owner_news[owner]
    swap_start(sends, lambda to: owner_news.at[to], by_latent, *sems[2:4])
    yield
    swap_wait(by_latent, sems[3])
    d_mod = stack_rows(by_latent)[:, :wide]
    part = fine_dot(d_mod, modulation[...], (1, 1))
    for to in range(8):
        d_cut[to] = part[:, to * cut : (to + 1) * cut]
    d_in[owner] = d_cut[owner]
    swap_start(sends, lambda to: d_cut.at[to], d_in, *sems[4:6])
    sums[owner] = jnp.sum(d_mod, axis=0, keepdims=True)
    swap_start(sends, lambda to: sums.at[owner], sums, *sems[6:8])
    yield
    swap_wait(d_in, sems[5])
    total = d_in[0]
    for of in range(1, 8):
        total = total + d_in[of]
    d_cond_cut[owner] = total * silu_parts(cond_cut[owner])[1]
    swap_start(sends, lambda to: d_cond_cut.at[owner], d_cond_cut, *sems[8:10])
    yield
    swap_wait(d_cond_cut, sems[9])
    for of in range(8):
        d_cond_out[:, of * cut : (of + 1) * cut] = d_cond_cut[of]
    d_hid_cut[owner] = fine_dot(d_cond_out[...], second[...], (1, 1)) * time_slope[...]
    swap_start(sends, lambda to: d_hid_cut.at[owner], d_hid_cut, *sems[10:12])
    yield
    swap_wait(d_hid_cut, sems[11])
    swap_wait(sums, sems[7])
    sends.finish()


def takes(refs, *counts):
    refs = list(refs)
    groups = []
    for count in counts:
        groups.append(refs[:count])
        refs = refs[count:]
    assert not refs
    return groups


def call(kernel, number, args, in_specs, outs, out_specs, scratch, name):
    return pl.pallas_call(
        kernel,
        out_shape=outs,
        in_specs=in_specs,
        out_specs=out_specs,
        scratch_shapes=scratch,
        compiler_params=pltpu.CompilerParams(
            collective_id=number, has_side_effects=True, vmem_limit_bytes=60 * 1024 * 1024
        ),
        name=name,
    )(*args)


def shape(dims, kind):
    return jax.ShapeDtypeStruct(tuple(dims), kind)


def forward_first(w_in, w_out, tokens, note, first, second, table, modulation):
    rows, width = second.shape
    wide = modulation.shape[1]

    def kernel(*refs):
        args, outs, scratch, cond_sems, in_sems, out_sems, token_sems = takes(refs, 8, 9, 5, 10, 3, 6, 3)
        greet(True, True)
        run_all(
            [
                condition_forward(args[3], *args[4:8], outs[3:9], scratch, cond_sems),
                gather_both(args[1], outs[1], out_sems),
                gather_ranks(args[2], outs[2], token_sems),
                gather_owners(args[0], outs[0], in_sems),
            ]
        )

    return call(
        kernel,
        1,
        (w_in, w_out, tokens, note, first, second, table, modulation),
        [VMEM] * 8,
        [
            shape((8,) + w_in.shape, LOW),
            shape((4, 8) + w_out.shape, LOW),
            shape((4,) + tokens.shape, LOW),
            shape(note.shape, F32),
            shape((8, rows), F32),
            shape((8, rows), F32),
            shape((8, 8, rows), F32),
            shape((8, width), F32),
            shape((8, 1, wide), F32),
        ],
        [HBM] * 3 + [VMEM] * 6,
        [
            pltpu.VMEM((2, 8, 8, rows), F32),
            pltpu.VMEM((8, 8, rows), F32),
            pltpu.VMEM((8, 8, rows), F32),
            pltpu.VMEM((2, 8, 1, rows), F32),
            pltpu.VMEM((8, 1, wide), F32),
        ]
        + SWAP_SEMS * 5
        + GATHER_OWNERS_SEMS
        + GATHER_OWNERS_SEMS
        + GATHER_RANKS_SEMS
        + GATHER_RANKS_SEMS,
        "forward_first",
    )


def gathers(number, by_owner, by_rank, name):
    if not fast():
        return [lax.all_gather(block, "fsdp", axis=0) for block in by_owner] + [
            lax.all_gather(block, "seq", axis=0) for block in by_rank
        ]
    many, few = len(by_owner), len(by_rank)

    def kernel(*refs):
        groups = takes(refs, many + few, many + few, *[3] * (many + few))
        args, outs, sems = groups[0], groups[1], groups[2:]
        greet(many > 0, few > 0)
        run_all(
            [gather_owners(args[at], outs[at], sems[at]) for at in range(many)]
            + [gather_ranks(args[at], outs[at], sems[at]) for at in range(many, many + few)]
        )

    blocks = list(by_owner) + list(by_rank)
    return call(
        kernel,
        number,
        blocks,
        [VMEM] * len(blocks),
        [shape((8 if at < many else 4,) + block.shape, block.dtype) for at, block in enumerate(blocks)],
        [HBM] * len(blocks),
        GATHER_OWNERS_SEMS * many + GATHER_RANKS_SEMS * few,
        name,
    )


def rank_sums(number, blocks, name):
    if not fast():
        return [lax.psum_scatter(block.astype(F32), "seq", scatter_dimension=0, tiled=False) for block in blocks]
    many = len(blocks)

    def kernel(*refs):
        groups = takes(refs, many, many, *[7] * many)
        greet(False, True)
        run_all(
            [
                scatter_ranks(groups[0][at], groups[1][at], *groups[2 + at][:4], groups[2 + at][4:])
                for at in range(many)
            ]
        )

    scratch = []
    for block in blocks:
        scratch += scatter_ranks_scratch(*block.shape[1:])
    return call(
        kernel,
        number,
        blocks,
        [HBM] * many,
        [shape(block.shape[1:], F32) for block in blocks],
        [VMEM] * many,
        scratch,
        name,
    )


def backward_last(blocks, news, second, modulation, cond_cut, time_slope):
    many = len(blocks)
    rows, width = second.shape

    def kernel(*refs):
        groups = takes(refs, many + 5, many + 4, 5, 12, *[14] * many)
        args, outs, scratch, sems = groups[:4]
        greet(True, True)
        run_all(
            [condition_backward(*args[many:], outs[many:], scratch, sems)]
            + [
                scatter_owners(args[at], outs[at], *groups[4 + at][:5], groups[4 + at][5:])
                for at in range(many)
            ]
        )

    scratch = [
        pltpu.VMEM((4,) + news.shape, F32),
        pltpu.VMEM(news.shape, F32),
        pltpu.VMEM((8, 8, rows), F32),
        pltpu.VMEM((8, 8, rows), F32),
        pltpu.VMEM((8, 8, rows), F32),
        DMA((3,)),
        DMA((4,)),
    ] + SWAP_SEMS * 5
    for block in blocks:
        scratch += scatter_owners_scratch(*block.shape[1:])
    return call(
        kernel,
        8,
        tuple(blocks) + (news, second, modulation, cond_cut, time_slope),
        [HBM] * many + [VMEM] * 5,
        [shape((4,) + block.shape[1:], LOW) for block in blocks]
        + [
            shape(news.shape, F32),
            shape((8, width), F32),
            shape((8, 8, rows), F32),
            shape((8, 1, modulation.shape[1]), F32),
        ],
        [HBM] * many + [VMEM] * 4,
        scratch,
        "backward_last",
    )


def sum_owners(number, value, name):
    if not fast():
        return lax.psum(value, "fsdp")

    def kernel(src, out, boxes, *sems):
        owner = lax.axis_index("fsdp")
        greet(True, False)
        sends = Sends()
        boxes[owner] = src[...]
        swap_start(sends, lambda to: src, boxes, *sems)
        swap_wait(boxes, sems[1])
        total = boxes[0]
        for of in range(1, 8):
            total = total + boxes[of]
        out[...] = total
        sends.finish()

    block = jnp.full((8, 128), value, F32)
    total = call(
        kernel, number, (block,), [VMEM], shape((8, 128), F32), VMEM, [pltpu.VMEM((8, 8, 128), F32)] + SWAP_SEMS, name
    )
    return total[0, 0]


def attend(query, keys, values):
    score_scale = 1.0 / math.sqrt(keys.shape[-1])
    scores = mixed_dot("qhd,khd->hqk", query, keys) * score_scale
    top = jnp.max(scores, axis=-1, keepdims=True)
    expo = jnp.exp(scores - top)
    total = jnp.sum(expo, axis=-1, keepdims=True)
    probs = (expo / total).astype(LOW)
    mixed = mixed_dot("hqk,khd->qhd", probs, values)
    return mixed.astype(LOW), (top + jnp.log(total))[..., 0]


def attend_back(query, keys, values, d_mixed, log_total):
    length, heads_here, head_dim = query.shape
    block = min(512, length)
    count = length // block
    score_scale = 1.0 / math.sqrt(head_dim)

    def back_block(carry, pieces):
        d_keys, d_values = carry
        query_block, d_block, log_block = pieces
        scores = mixed_dot("qhd,khd->hqk", query_block, keys) * score_scale
        probs = jnp.exp(scores - log_block[..., None])
        d_probs = mixed_dot("qhd,khd->hqk", d_block, values)
        delta = jnp.sum(probs * d_probs, axis=-1, keepdims=True)
        d_scores = (probs * (d_probs - delta)).astype(LOW)
        d_query = mixed_dot("hqk,khd->qhd", d_scores, keys) * score_scale
        d_keys = d_keys + mixed_dot("hqk,qhd->khd", d_scores, query_block) * score_scale
        d_values = d_values + mixed_dot("hqk,qhd->khd", probs.astype(LOW), d_block)
        return ((d_keys, d_values), d_query)

    empty = jnp.zeros((length, heads_here, head_dim), jnp.float32)
    blocked = (count, block, heads_here, head_dim)
    logs = log_total.reshape(heads_here, count, block).transpose(1, 0, 2)
    (d_keys, d_values), d_query = lax.scan(
        back_block, (empty, empty), (query.reshape(blocked), d_mixed.reshape(blocked), logs)
    )
    flat = (length, heads_here * head_dim)
    return jnp.concatenate(
        [d_query.reshape(flat), d_keys.reshape(flat), d_values.reshape(flat)], axis=1
    ).astype(LOW)


def adam_step(weight, moment, square, gradient, factor):
    clipped = gradient * factor
    moment_next = beta_one * moment + (1.0 - beta_one) * clipped
    square_next = beta_two * square + (1.0 - beta_two) * clipped * clipped
    moment_hat = moment_next / (1.0 - beta_one**STEP)
    square_hat = square_next / (1.0 - beta_two**STEP)
    master = weight - learn_rate * (
        moment_hat / (jnp.sqrt(square_hat) + adam_eps) + weight_decay * weight
    )
    return (master, moment_next, square_next)


def condition_start(latent_tokens, w_in, w_out, biases, timesteps, labels, time_first, time_second, class_table, modulation):
    owners, owner = lax.axis_size("fsdp"), lax.axis_index("fsdp")
    share = biases.shape[0]
    width = time_first.shape[1]
    first, second = time_first.astype(LOW), time_second.astype(LOW)
    table, modulation_low = class_table.astype(LOW), modulation.astype(LOW)
    units = first.shape[0]
    bias_low = biases.astype(LOW).astype(F32)
    features = time_features(timesteps).astype(LOW)
    if fast():
        note = jnp.concatenate(
            [
                jnp.broadcast_to(bias_low, (owners, share)),
                features.astype(F32).reshape(owners, units),
                jnp.broadcast_to(labels.astype(F32), (owners, 1)),
                jnp.zeros((owners, 127 - units), F32),
            ],
            axis=1,
        )[:, None]
        w_in_all, w_out_all, tokens, notes, act, slope, cond_cut, cond, mod = forward_first(
            w_in, w_out, latent_tokens, note, first, second, table, modulation_low
        )
        notes = notes[:, 0]
        all_bias = notes[:, :share].reshape(owners * share)
        my_features = notes[:, share : share + units]
        all_labels = notes[:, share + units]
        mod_values = mod.reshape(owners * mod.shape[2])
        state = (first, second, modulation_low, my_features, all_labels, act, slope, cond_cut, cond)
        return w_in_all, w_out_all, tokens, all_bias, mod_values, state
    w_in_all, w_out_part = lax.all_gather(w_in, "fsdp", axis=0), lax.all_gather(w_out, "fsdp", axis=0)
    w_out_all = lax.all_gather(w_out_part, "seq", axis=0)
    tokens = lax.all_gather(latent_tokens, "seq", axis=0)
    note = jnp.concatenate([bias_low, features[0].astype(F32), labels.astype(F32)])
    notes = lax.all_gather(note, "fsdp", axis=0)
    all_bias = notes[:, :share].reshape(owners * share)
    my_features = mine(notes[:, share:-1], 1, owners, owner)
    all_labels = notes[:, -1]
    hidden_time = lax.psum(mixed_dot("bf,fd->bd", my_features.astype(LOW), first), "fsdp") + all_bias[:width]
    act, slope = silu_parts(mine(hidden_time, 1, owners, owner))
    act = act.astype(LOW)
    onehot = (all_labels[:, None] == jnp.arange(NCLS, dtype=F32)[None, :]).astype(LOW)
    cond_part = mixed_dot("bd,de->be", act, second)
    class_part = mixed_dot("bc,cd->bd", onehot, table)
    class_wide = lax.dynamic_update_slice(jnp.zeros_like(cond_part), class_part, (0, owner * class_part.shape[1]))
    cond = lax.psum(cond_part + class_wide, "fsdp") + all_bias[width : 2 * width]
    mod_part = mixed_dot("bd,de->be", silu_parts(cond)[0].astype(LOW), modulation_low)
    mod_values = pick(lax.all_gather(mod_part, "fsdp", axis=0), owner, 1).reshape(owners * mod_part.shape[1])
    state = (first, second, modulation_low, my_features, all_labels, act.astype(F32), slope, None, cond)
    return w_in_all, w_out_all, tokens, all_bias, mod_values, state


def condition_end(state, blocks, my_d_mod, tail, share):
    first, second, modulation_low, my_features, all_labels, act, slope, cond_cut, cond = state
    owners, owner, rank = lax.axis_size("fsdp"), lax.axis_index("fsdp"), lax.axis_index("seq")
    wide, width = modulation_low.shape[1], cond.shape[1]
    if fast():
        pad = -wide % 128
        tails = jnp.concatenate([jnp.zeros((owners * share - tail.shape[0],), F32), tail]).reshape(owners, share)
        news = jnp.concatenate(
            [my_d_mod.reshape(owners, wide), jnp.zeros((owners, pad), F32), tails], axis=1
        )[:, None]
        *grads, by_latent, d_cond, d_hid, sums = backward_last(blocks, news, second, modulation_low, cond_cut, slope)
        d_mod = by_latent[:, 0, :wide]
        my_tail = jnp.sum(by_latent[:, 0, wide + pad :], axis=0)
        d_hidden = d_hid.transpose(1, 0, 2).reshape(owners, width)
        front = jnp.concatenate([jnp.sum(d_hidden, axis=0), jnp.sum(d_cond, axis=0), sums.reshape(owners * wide)])
        count = front.shape[0] // share
        grad_bias = jnp.where(
            owner < count, pick(front.reshape(count, share), jnp.minimum(owner, count - 1)), my_tail
        )
    else:
        summed = [lax.psum_scatter(block.astype(F32), "fsdp", scatter_dimension=0, tiled=False) for block in blocks]
        grads = [lax.all_gather(block.astype(LOW), "seq", axis=0) for block in summed]
        all_d_mod = lax.all_gather(lax.psum(my_d_mod, "seq"), "fsdp", axis=0)
        d_mod = mine(all_d_mod, 1, owners, owner)
        part = high_dot(d_mod, modulation_low.astype(F32).T)
        d_cond = lax.psum(part, "fsdp") * silu_parts(cond)[1]
        d_time = high_dot(d_cond, second.astype(F32).T) * slope
        d_hidden = lax.all_gather(d_time, "fsdp", axis=0).transpose(1, 0, 2).reshape(owners, width)
        tail = lax.psum(tail, ("seq", "fsdp"))
        all_bias = jnp.concatenate(
            [jnp.sum(d_hidden, axis=0), jnp.sum(d_cond, axis=0), jnp.sum(all_d_mod, axis=0), tail]
        )
        grad_bias = mine(all_bias, 0, owners, owner)
    onehot = (all_labels[:, None] == jnp.arange(NCLS, dtype=F32)[None, :]).astype(F32)
    cond_act = silu_parts(cond)[0].astype(LOW).astype(F32)
    grad_mod = high_dot(cond_act.T, d_mod)
    grad_class = high_dot(onehot.T, mine(d_cond, 1, owners, owner))
    grad_second = high_dot(act.T, d_cond)
    grad_first = high_dot(my_features.T, d_hidden)
    condition_gradient = lax.dynamic_slice_in_dim(d_cond, owner, 1, 0)
    return grads, (grad_first, grad_second, grad_class, grad_mod), grad_bias, condition_gradient


def per_device(latents, timesteps, labels, upstream, *state):
    params, moments, squares = state[:9], state[9:18], state[18:]
    time_first, time_second, class_table, modulation, attend_in, attend_out, expand, contract, biases = params
    lat_dev, tok_rows, width = latents.shape
    assert lat_dev == 1
    hidden = expand.shape[1]
    ranks = lax.axis_size("seq")
    owners = lax.axis_size("fsdp")
    rank = lax.axis_index("seq")
    heads_here = H // ranks
    span = heads_here * HD
    length = ranks * tok_rows
    rows = width // owners
    unit = hidden // (owners * ranks)
    hid_here = owners * unit

    my_in = pick(attend_in.reshape(rows, 3, ranks, span), rank, 2).astype(LOW).reshape(rows, 3 * span)
    my_out = mine(attend_out, 1, ranks, rank).astype(LOW)
    my_up = pick(expand.reshape(rows, owners, ranks, unit), rank, 2).astype(LOW).reshape(rows, hid_here)
    my_down = mine(contract, 0, ranks, rank).astype(LOW)
    w_in, w_out, tokens, all_bias, mod_values, kept = condition_start(
        latents[0], my_in, my_out, biases, timesteps, labels, time_first, time_second, class_table, modulation
    )
    w_in = w_in.reshape(width, 3 * span)
    w_out = w_out.transpose(1, 2, 0, 3).reshape(width, width)
    inputs_low = tokens.reshape(length, width)
    w_up, w_down, d_out_low = gathers(2, [my_up, my_down], [upstream[0]], "forward_second")
    w_up, w_down = w_up.reshape(width, hid_here), w_down.reshape(hid_here, width)
    d_out_low = d_out_low.reshape(length, width)

    b_t1, b_t2, b_mod, b_q, b_v, b_out, b_up, b_down = split_biases(all_bias, width, hidden)
    mod_values = (mod_values + b_mod).reshape(6, 1, width)
    shift1, scale1, gate1, shift2, scale2, gate2 = [mod_values[index] for index in range(6)]

    inputs = inputs_low.astype(F32)
    norm_one, _ = layer_norm(inputs)
    h_attn = (norm_one * (1.0 + scale1) + shift1).astype(LOW)
    my_b_q, my_b_v = mine(b_q, 0, ranks, rank), mine(b_v, 0, ranks, rank)
    qkv_bias = jnp.concatenate([my_b_q, jnp.zeros_like(my_b_q), my_b_v])
    qkv = (mixed_dot("td,de->te", h_attn, w_in) + qkv_bias).astype(LOW)
    head_shape = (length, heads_here, HD)
    query, keys, values = [qkv[:, part * span : (part + 1) * span].reshape(head_shape) for part in range(3)]
    mixed_heads, log_total = attend(query, keys, values)
    (mixed,) = gathers(3, [], [mixed_heads.reshape(length, span)], "gather_mixed")
    mixed = mixed.transpose(1, 0, 2).reshape(length, width)
    attn_out = mixed_dot("td,de->te", mixed, w_out) + b_out
    middle = inputs + gate1 * attn_out
    norm_two, inverse_two = layer_norm(middle)
    h_mlp = (norm_two * (1.0 + scale2) + shift2).astype(LOW)

    my_b_up = pick(b_up.reshape(owners, ranks, unit), rank, 1).reshape(hid_here)
    pre_act = mixed_dot("td,df->tf", h_mlp, w_up) + my_b_up
    act_f, gelu_pull = jax.vjp(partial(jax.nn.gelu, approximate=True), pre_act)
    act = act_f.astype(LOW)
    by_rank = (ranks, tok_rows, width)
    by_owner = lambda block: block.astype(LOW).reshape((owners, -1) + block.shape[1:])
    mlp_part = mixed_dot("tf,fd->td", act, w_down).astype(LOW).reshape(by_rank)
    d_out = d_out_low.astype(F32)
    d_mlp = (d_out * gate2).astype(LOW)
    d_act = mixed_dot("td,fd->tf", d_mlp, w_down)
    d_pre = gelu_pull(d_act)[0].astype(LOW)
    d_hmlp_part = mixed_dot("tf,df->td", d_pre, w_up).astype(LOW).reshape(by_rank)
    d_hmlp, mlp_sum = rank_sums(4, [d_hmlp_part, mlp_part], "sum_feed")
    g_down = by_owner(mixed_dot("tf,td->fd", act, d_mlp))
    g_up = by_owner(mixed_dot("td,tf->df", h_mlp, d_pre))
    gb_up = jnp.sum(d_pre.astype(F32), axis=0)
    gb_down = jnp.sum(d_mlp.astype(F32), axis=0)

    own = lambda array: mine(array, 0, ranks, rank)
    my_attn_out, my_middle, my_norm_two, my_inverse_two = own(attn_out), own(middle), own(norm_two), own(inverse_two)
    my_d_out = upstream[0].astype(F32)
    mlp_out = mlp_sum + b_down
    output = (my_middle + gate2 * mlp_out).astype(LOW)
    d_gate2 = jnp.sum(my_d_out * mlp_out, axis=0)
    d_shift2 = jnp.sum(d_hmlp, axis=0)
    d_scale2 = jnp.sum(d_hmlp * my_norm_two, axis=0)
    d_middle = my_d_out + layer_norm_back(my_norm_two, my_inverse_two, d_hmlp * (1.0 + scale2))
    d_gate1 = jnp.sum(d_middle * my_attn_out, axis=0)
    my_d_attn = (d_middle * gate1).astype(LOW)
    (d_attn,) = gathers(5, [], [my_d_attn], "gather_d_attn")
    d_attn = d_attn.reshape(length, width)
    d_mixed = mixed_dot("te,de->td", d_attn, mine(w_out, 0, ranks, rank)).astype(LOW)
    g_out = by_owner(mixed_dot("td,te->de", mixed, mine(d_attn, 1, ranks, rank)))
    d_qkv = attend_back(query, keys, values, d_mixed.reshape(head_shape), log_total)
    g_in = by_owner(mixed_dot("td,te->de", h_attn, d_qkv))
    d_hattn_part = mixed_dot("te,de->td", d_qkv, w_in).astype(LOW).reshape(by_rank)
    (d_hattn,) = rank_sums(6, [d_hattn_part], "sum_attend")
    my_inputs = latents[0].astype(F32)
    my_norm_one, my_inverse_one = layer_norm(my_inputs)
    d_shift1 = jnp.sum(d_hattn, axis=0)
    d_scale1 = jnp.sum(d_hattn * my_norm_one, axis=0)
    input_gradient = d_middle + layer_norm_back(my_norm_one, my_inverse_one, d_hattn * (1.0 + scale1))

    my_d_mod = jnp.concatenate([d_shift1, d_scale1, d_gate1, d_shift2, d_scale2, d_gate2])
    gb_qv = jnp.sum(d_qkv.astype(F32), axis=0)
    wide = lambda part, size: lax.dynamic_update_slice(jnp.zeros((size,), F32), part, (rank * part.shape[0],))
    gb_up_wide = lax.dynamic_update_slice(
        jnp.zeros((owners, ranks, unit), F32), gb_up.reshape(owners, 1, unit), (0, rank, 0)
    ).reshape(hidden)
    gb_tail = jnp.concatenate(
        [
            wide(gb_qv[:span], width),
            wide(gb_qv[2 * span :], width),
            jnp.sum(my_d_attn.astype(F32), axis=0),
            gb_up_wide,
            jnp.where(rank == 0, gb_down, 0.0),
        ]
    )
    grads, small_grads, grad_bias, condition_gradient = condition_end(
        kept, [g_down, g_up, g_out, g_in], my_d_mod, gb_tail, biases.shape[0]
    )
    grad_down, grad_up, grad_out, grad_in = [grad.astype(F32) for grad in grads]
    grad_in = grad_in.reshape(ranks, rows, 3, span).transpose(1, 2, 0, 3).reshape(rows, 3 * width)
    grad_out = grad_out.transpose(1, 0, 2).reshape(rows, width)
    grad_up = grad_up.reshape(ranks, rows, owners, unit).transpose(1, 2, 0, 3).reshape(rows, hidden)
    grad_down = grad_down.reshape(contract.shape)
    gradients = small_grads + (grad_in, grad_out, grad_up, grad_down, grad_bias)
    local_sum = sum(jnp.sum(gradient * gradient) for gradient in gradients)
    norm_before = jnp.sqrt(sum_owners(7, local_sum, "sum_squares"))
    factor = clip_limit / jnp.maximum(norm_before, clip_limit)
    results = [
        adam_step(params[index], moments[index], squares[index], gradients[index], factor)
        for index in range(9)
    ]
    return (
        (output[None], input_gradient[None], condition_gradient, norm_before)
        + gradients
        + tuple(result[0] for result in results)
        + tuple(result[1] for result in results)
        + tuple(result[2] for result in results)
    )


def solution(mesh):
    tokens = P("fsdp", "seq", None)
    rows, columns = P("fsdp", None), P(None, "fsdp")
    weights = (rows, rows, columns, columns, rows, rows, rows, rows, P("fsdp"))
    return jax.shard_map(
        per_device,
        mesh=mesh,
        in_specs=(tokens, P("fsdp"), P("fsdp"), tokens) + weights * 3,
        out_specs=(tokens, tokens, rows, P()) + weights * 4,
        check_vma=False,
    )
```

time: 829 us -> 773 us (0.932)
  Pallas kernels: 0 us -> 425 us
  starting transfers between devices: 207 us -> 0 us
  waiting for transfers between devices: 158 us -> 0 us
  local copies, waits for them, and re-layouts: 187 us -> 119 us
  other arithmetic: 125 us -> 98.1 us
  matrix products: 125 us -> 112 us
    pallas_call x0 -> x8, Pallas kernels: none -> 425 us  [call(): pl.pallas_call(kernel, out_shape=outs, in_specs=in_specs, out_specs=out_s...]
    ppermute x132 -> x0, starting transfers between devices: 207 us -> none  [the longest x12 48.2 us: scatter_rows(): rise_in = hop(rise.astype(LOW), perm=Z_UP).astype(jnp.float32)]
    ppermute x132 -> x0, waiting for transfers between devices: 158 us -> none  [the longest x4 47.2 us: scatter_rows(): got = hop(pick(parts, 1 - y, 1).astype(LOW), perm=SWAP_Y)]
    dynamic_update_slice x55 -> x3, local copies, waits for them, and re-layouts: 57.6 us -> 1.7 us  [the longest x1 1.41 us: per_device(): lax.dynamic_update_slice(jnp.zeros((owners, ranks, unit), F32), gb_up.res...]
    dynamic_update_slice x15 -> x0, other arithmetic: 20.2 us -> none  [place(): return lax.dynamic_update_slice(array, block[(None,) * len(index)], starts)]
    add x20 -> x1, other arithmetic: 15.8 us -> 0.01 us  [per_device(): mod_values = (mod_values + b_mod).reshape(6, 1, width)]
    transpose x5 -> x8, local copies, waits for them, and re-layouts: 17.2 us -> 29 us  [the longest x2 11.7 us: per_device(): grad_up.reshape(ranks, rows, owners, unit).transpose(1, 2, 0, 3)]
    dot_general x28 -> x24, matrix products: 113 us -> 102 us  [mixed_dot(): return jnp.einsum(form, left, right, preferred_element_type=jnp.float32)]
  transfers between devices with their start and end apart: 132 -> 0, of which waited for: 47 -> 0; matrix products, arithmetic and copies ran while one was open for 41% -> 0% of each run, Pallas kernels for 0% -> 0%
where the time goes in v2:
time: 773 us; the launch traced here: 766 us
  Pallas kernels  425 us (55%)
  local copies, waits for them, and re-layouts  119 us (15%)
  matrix products  112 us (14%)
  other arithmetic  98.1 us (13%)
  between operations  11 us (1%)
    pallas_call x8, Pallas kernels, call(): pl.pallas_call(kernel, out_shape=outs, in_specs=in_specs, out_specs=out_s...  425 us
    dot_general x24, matrix products, mixed_dot(): return jnp.einsum(form, left, right, preferred_element_type=jnp.float32)  102 us
    sub x9, other arithmetic, adam_step(): weight - learn_rate * (moment_hat / (jnp.sqrt(square_hat) + adam_eps) + w...  36.1 us
    unnamed x183, local copies, waits for them, and re-layouts  18.9 us

profile of v2, /device:TPU:0, one launch (start us, length us, event | category | flops | bytes accessed | tf_op | source)
XLA Modules:
  0.0 766.4 jit_solution(16021039216600537566)
XLA Ops:
  16.1 2.9 reshape.404
  22.2 4.6 copy.117.refs_7_.refs_6_
  26.7 6.3 reshape.414
  33.0 2.9 constant_dynamic-slice_fusion.1
  37.3 65.9 %forward_second.1 = (bf16[8,144,1152]{2,1,0:T(8,128)(2,1)}, bf16[8,144,1152]{2,1,0:T(8,128)(2,1)}, bf16[4,256,1152]{2,1,0:T(8,128)(2,1)}) custom-call(bf16[144,1152]{1,0:T(8,128)(2,1)} %convert_element_type.210.refs_0_, bf16[144,1152]{1,0:T(8,128)(2,1)} %dynamic-slice_convert_fusion.refs_1_, bf16[256,1152]{1,0:T(8,128)(2,1)} %bitcast.199), custom_call_target="tpu_custom_call" | custom-call | tf_op jit(solution)/shard_map/forward_second/pallas_call | solution.py:499
  103.2 66.1 %forward_first.1 = (bf16[8,144,864]{2,1,0:T(8,128)(2,1)}, bf16[4,8,144,288]{3,2,1,0:T(8,128)(2,1)}, bf16[4,256,1152]{2,1,0:T(8,128)(2,1)}, f32[8,1,2432]{2,1,0:T...) custom-call(bf16[144,864]{1,0:T(8,128)(2,1)} %convert_element_type.1, ...), custom_call_target="tpu_custom_call" | custom-call | tf_op jit(solution)/shard_map/forward_first/pallas_call | solution.py:499
  188.7 3.7 fusion.39
  194.1 5.3 fusion.107
  199.4 4.5 copy.122
  204.0 6.4 reshape.413
  210.3 9.2 %multiply_reduce_fusion.1 = (f32[4,1024]{1,0:T(4,128)S(1)}, f32[4,1024,1024]{1,2,0:T(8,128)}) fusion(bf16[1024,4,72]{0,2,1:T(8,128)(2,1)} %bitcast.194, bf16[1024,4,72]{0,2,1:T(8,128)(2,1)S(1)} %bitcast.183), kind=kOutput, calls=%fused_computation.33 | convolution fusion | flops 612364288 | bytes 17973248 | tf_op jit(solution)/shard_map/qhd,khd->hqk/dot_general | solution.py:69
  219.5 8.5 %fusion.30 = f32[4,1024]{1,0:T(4,128)S(1)} fusion(f32[4,1024,1024]{1,2,0:T(8,128)} %get-tuple-element.295, f32[4,1024]{1,0:T(4,128)S(1)} %get-tuple-element.294), kind=kLoop, calls=%fused_computation.34 | loop fusion | flops 12578816 | bytes 16809984 | tf_op jit(solution)/shard_map/reduce_sum | solution.py:698
  228.0 8.7 %fusion.59 = bf16[4,72,1024]{2,1,0:T(8,128)(2,1)} fusion(bf16[1024,4,72]{0,2,1:T(8,128)(2,1)S(1)} %bitcast.187, f32[4,1024,1024]{1,2,0:T(8,128)} %get-tuple-element.295, f32[4,1024]{1,0:T(4,128)S(1)} %fusion.30, f32[4,1024]{1,0:T(4,128)S(1)} %get-tuple-element.294), kind=kOutput, calls=%fused_computation.110 | convolution fusion | flops 621051904 | bytes 17989632 | tf_op jit(solution)/shard_map/hqk,khd->qhd/dot_general | solution.py:69
  239.0 23.4 %gather_mixed.1 = bf16[4,1024,288]{2,1,0:T(8,128)(2,1)} custom-call(bf16[1024,288]{1,0:T(8,128)(2,1)} %copy.120.refs_0_), custom_call_target="tpu_custom_call" | custom-call | tf_op jit(solution)/shard_map/gather_mixed/pallas_call | solution.py:499
  262.4 4.5 copy.121
  266.8 11.2 %fusion.103 = (f32[1024]{0:T(1024)S(1)}, f32[1024,1152]{1,0:T(8,128)S(1)}, bf16[1024,1152]{1,0:T(8,128)(2,1)}, f32[1024,1152]{1,0:T(8,128)}) fusion(f32[1152]{0:T(1024)} %get-tuple-element.289, bf16[4,256,1152]{2,1,0:T(8,128)(2,1)} %get-tuple-element.111, f32[1152]{0:T(1024)} %copy-done.56, f32[1152]{0:T(1024)} %copy-done.44, f32[1024]{0:T(1024)} %bitcast.227, ...), kind=kOutput, calls=%fused_computation.223 | convolution fusion | flops 2729704448 | bytes 19200000 | tf_op jit(solution)/shard_map/td,de->te/dot_general | solution.py:69
  281.5 9.6 %convert_reduce_fusion.2 = (f32[1152]{0:T(1024)}, bf16[1024,1152]{1,0:T(8,128)(2,1)S(1)}, f32[1024,1152]{1,0:T(8,128)S(1)}) fusion(f32[1024,1152]{1,0:T(8,128)} %fusion.107, f32[1152]{0:T(1024)S(1)} %copy-done.70, bf16[1152,1152]{1,0:T(8,128)(2,1)S(1)} %bitcast.228, f32[1024,1152]{1,0:T(8,128)S(1)} %subtract_multiply_fusion, f32[1152]{0:T(1024)S(1)} %copy-done.68, ...), kind=kOutput, calls=%fused_computation.66 | convolution fusion | flops 2748578816 | bytes 19187712 | tf_op jit(solution)/shard_map/td,df->tf/dot_general | solution.py:69
  291.2 5.4 convolution_convert_fusion.3
  296.6 4.8 convolution_convert_fusion.4
  306.3 32.9 %sum_feed.1 = (f32[256,1152]{1,0:T(8,128)}, f32[256,1152]{1,0:T(8,128)}) custom-call(bf16[4,256,1152]{2,1,0:T(8,128)(2,1)} %bitcast.210, bf16[4,256,1152]{2,1,0:T(8,128)(2,1)} %bitcast.209), custom_call_target="tpu_custom_call" | custom-call | tf_op jit(solution)/shard_map/sum_feed/pallas_call | solution.py:499
  342.1 5.0 fusion.67
  347.2 4.8 convolution_convert_fusion
  352.0 5.2 convolution_convert_fusion.1
  357.1 18.8 %gather_d_attn.1 = bf16[4,256,1152]{2,1,0:T(8,128)(2,1)} custom-call(bf16[256,1152]{1,0:T(8,128)(2,1)} %get-tuple-element.278.refs_0_), custom_call_target="tpu_custom_call" | custom-call | tf_op jit(solution)/shard_map/gather_d_attn/pallas_call | solution.py:499
  376.0 3.7 convolution_convert_fusion.7
  379.7 3.3 convolution_convert_fusion.6
  387.8 24.4 %while.15 = (s32[]{:T(128)}, f32[1024,4,72]{0,2,1:T(8,128)S(1)}, f32[1024,4,72]{0,2,1:T(8,128)S(1)}, bf16[2,512,4,72]{1,3,2,0:T(8,128)(2,1)}, bf16[2,512,4,72]{1...) while((s32[]{:T(128)}, f32[1024,4,72]{0,2,1:T(8,128)S(1)}, ...), condition=%wide.region_12.13_spmd.clone, body=%wide.region_10.12_spmd.clone.sunk | while | flops 1536735232 | bytes 80666888 | solution.py:726
  392.7 2.9 multiply_reduce_fusion.18
  404.8 2.9 multiply_reduce_fusion.18
  418.0 3.7 convolution_convert_fusion.5
  422.1 4.2 convolution_convert_fusion.2
  426.3 19.4 %sum_attend.1 = f32[256,1152]{1,0:T(8,128)} custom-call(bf16[4,256,1152]{2,1,0:T(8,128)(2,1)} %bitcast.213), custom_call_target="tpu_custom_call" | custom-call | tf_op jit(solution)/shard_map/sum_attend/pallas_call | solution.py:499
  452.0 4.5 copy.128
  456.4 168.4 %backward_last.1 = (bf16[4,144,1152]{2,1,0:T(8,128)(2,1)}, bf16[4,144,1152]{2,1,0:T(8,128)(2,1)}, bf16[4,144,288]{2,1,0:T(8,128)(2,1)}, bf16[4,144,864]{2,1,0:T(...) custom-call(bf16[8,144,1152]{2,1,0:T(8,128)(2,1)} %bitcast.198, ...), custom_call_target="tpu_custom_call" | custom-call | tf_op jit(solution)/shard_map/backward_last/pallas_call | solution.py:499
  647.9 3.9 reshape.444
  654.3 3.2 copy.130
  657.5 3.6 reshape.437
  661.1 4.3 multiply_reduce_fusion.4
  667.3 4.2 reshape.445
  671.5 4.2 multiply_reduce_fusion.2
  677.6 7.5 copy.132
  685.2 6.6 reshape.439
  692.4 30.5 %sum_squares.1 = f32[8,128]{1,0:T(8,128)} custom-call(f32[8,128]{1,0:T(8,128)} %broadcast_in_dim.81.src), custom_call_target="tpu_custom_call" | custom-call | tf_op jit(solution)/shard_map/sum_squares/pallas_call | solution.py:499
  728.2 3.1 multiply_subtract_fusion.6
  737.2 3.8 multiply_subtract_fusion.3
  742.6 4.7 multiply_subtract_fusion.2
  747.4 9.4 %multiply_subtract_fusion.1 = (f32[576,1152]{1,0:T(8,128)}, f32[576,1152]{1,0:T(8,128)}, f32[576,1152]{1,0:T(8,128)}, f32[576,1152]{1,0:T(8,128)}) fusion(f32[576,1152]{1,0:T(8,128)} %param.44, f32[]{:T(128)S(6)} %div.191, f32[576,1152]{1,0:T(8,128)} %param.53, f32[576,1152]{1,0:T(8,128)} %param.62, bf16[4,144,1152]{2,1,0:T(8,128)(2,1)S(1)} %copy-done.14), kind=kLoop, calls=%fused_computation.90 | loop fusion | flops 11280384 | bytes 19906564 | tf_op jit(solution)/shard_map/sub | solution.py:741
  757.8 7.3 multiply_subtract_fusion
  (329 shorter events, 125.3 us)
Async XLA Ops:
  0.7 14.6 %copy-start.20 = (f32[144,1152]{1,0:T(8,128)S(1)}, f32[144,1152]{1,0:T(8,128)}, u32[]{:S(2)}) copy-start(f32[144,1152]{1,0:T(8,128)} %param.38) | copy-start | bytes 1990660
  169.3 5.2 copy-start.50
  174.4 5.9 copy-start.41
  175.8 16.5 %copy-start.46 = (f32[1152]{0:T(1024)}, f32[1152]{0:T(1024)S(1)}, u32[]{:S(2)}) copy-start(f32[1152]{0:T(1024)S(1)} %get-tuple-element.284) | copy-start | bytes 13828
  194.1 5.3 copy-start.18
  281.5 9.6 %copy-start.7 = (f32[1024,1152]{1,0:T(8,128)}, f32[1024,1152]{1,0:T(8,128)S(1)}, u32[]{:S(2)}) copy-start(f32[1024,1152]{1,0:T(8,128)S(1)} %subtract_multiply_fusion) | copy-start | bytes 14155780
  281.5 9.6 %copy-start.75 = (bf16[8,144,1152]{2,1,0:T(8,128)(2,1)S(1)}, bf16[8,144,1152]{2,1,0:T(8,128)(2,1)}, u32[]{:S(2)}) copy-start(bf16[8,144,1152]{2,1,0:T(8,128)(2,1)} %get-tuple-element.117) | copy-start | bytes 7962628
  291.2 5.4 copy-start.78
  291.2 5.4 copy-start.80
  306.2 33.0 %copy-start.52 = (f32[1152]{0:T(1024)S(1)}, f32[1152]{0:T(1024)}, u32[]{:S(2)}) copy-start(f32[1152]{0:T(1024)} %get-tuple-element.286) | copy-start | bytes 13828
  306.2 35.8 %copy-start.47 = (f32[1152]{0:T(1024)S(1)}, f32[1152]{0:T(1024)}, u32[]{:S(2)}) copy-start(f32[1152]{0:T(1024)} %copy-done.46) | copy-start | bytes 13828
  306.2 35.8 %copy-start.55 = (f32[1152]{0:T(1024)S(1)}, f32[1152]{0:T(1024)}, u32[]{:S(2)}) copy-start(f32[1152]{0:T(1024)} %get-tuple-element.289) | copy-start | bytes 13828
  306.2 35.8 %copy-start.62 = (f32[1152]{0:T(1024)S(1)}, f32[1152]{0:T(1024)}, u32[]{:S(2)}) copy-start(f32[1152]{0:T(1024)} %get-tuple-element.280) | copy-start | bytes 13828
  306.3 35.8 %copy-start.71 = (f32[256]{0:T(256)S(1)}, f32[256]{0:T(256)}, u32[]{:S(2)}) copy-start(f32[256]{0:T(256)} %dynamic-slice.3) | copy-start | bytes 3076
  339.2 7.9 %slice-start = ((s8[4718592]{0:T(1024)(128)(4,1)}), s8[4194304]{0:T(1024)(128)(4,1)S(1)}, s32[]{:S(2)}) async-start(s8[4718592]{0:T(1024)(128)(4,1)} %bitcast.191), calls=%async_computation | async-start | bytes 8388608
  339.3 7.9 %copy-start.81 = (bf16[1024,1152]{1,0:T(8,128)(2,1)S(1)}, bf16[1024,1152]{1,0:T(8,128)(2,1)}, u32[]{:S(2)}) copy-start(bf16[1024,1152]{1,0:T(8,128)(2,1)} %copy-done.80) | copy-start | bytes 7077892
  342.1 5.0 slice-start.1
  342.1 5.0 copy-start.69
  342.1 9.8 %slice-start.2 = ((s8[4718592]{0:T(1024)(128)(4,1)}), s8[4194304]{0:T(1024)(128)(4,1)S(1)}, s32[]{:S(2)}) async-start(s8[4718592]{0:T(1024)(128)(4,1)} %bitcast.234), calls=%async_computation.2 | async-start | bytes 8388608
  426.3 19.8 %copy-start.43 = (f32[18432]{0:T(1024)S(1)}, f32[18432]{0:T(1024)}, u32[]{:S(2)}) copy-start(f32[18432]{0:T(1024)} %broadcast_dynamic-update-slice_fusion) | copy-start | bytes 221188
  426.3 19.8 %copy-start.61 = (f32[1152]{0:T(1024)S(1)}, f32[1152]{0:T(1024)}, u32[]{:S(2)}) copy-start(f32[1152]{0:T(1024)} %get-tuple-element.277) | copy-start | bytes 13828
  426.3 19.9 %copy-start.49 = (f32[4608]{0:T(1024)S(1)}, f32[4608]{0:T(1024)}, u32[]{:S(2)}) copy-start(f32[4608]{0:T(1024)} %reshape.430) | copy-start | bytes 55300
  426.3 19.9 %copy-start.57 = (f32[1152]{0:T(1024)S(1)}, f32[1152]{0:T(1024)}, u32[]{:S(2)}) copy-start(f32[1152]{0:T(1024)} %get-tuple-element.258) | copy-start | bytes 13828
  426.3 19.9 %copy-start.6 = (bf16[1,256,1152]{2,1,0:T(8,128)(2,1)S(1)}, bf16[1,256,1152]{2,1,0:T(8,128)(2,1)}, u32[]{:S(2)}) copy-start(bf16[1,256,1152]{2,1,0:T(8,128)(2,1)} %param.33) | copy-start | bytes 1769476
  426.3 19.9 %copy-start.45 = (f32[1152]{0:T(1024)S(1)}, f32[1152]{0:T(1024)}, u32[]{:S(2)}) copy-start(f32[1152]{0:T(1024)} %copy-done.44) | copy-start | bytes 13828
  426.3 19.9 %copy-start.65 = (f32[256]{0:T(256)S(1)}, f32[256]{0:T(256)}, u32[]{:S(2)}) copy-start(f32[256]{0:T(256)} %copy-done.64) | copy-start | bytes 3076
  426.3 19.9 %copy-start.66 = (f32[256]{0:T(256)S(1)}, f32[256]{0:T(256)}, u32[]{:S(2)}) copy-start(f32[256]{0:T(256)} %add_rsqrt_fusion.2) | copy-start | bytes 3076
  426.3 21.8 %copy-start.63 = (f32[6912]{0:T(1024)S(1)}, f32[6912]{0:T(1024)}, u32[]{:S(2)}) copy-start(f32[6912]{0:T(1024)} %custom-call.3) | copy-start | bytes 82948
  426.3 21.8 %copy-start.16 = (f32[256,1152]{1,0:T(8,128)S(1)}, f32[256,1152]{1,0:T(8,128)}, u32[]{:S(2)}) copy-start(f32[256,1152]{1,0:T(8,128)} %get-tuple-element.279) | copy-start | bytes 3538948
  624.8 15.4 %copy-start.42 = (f32[8,1152]{1,0:T(8,128)S(1)}, f32[8,1152]{1,0:T(8,128)}, u32[]{:S(2)}) copy-start(f32[8,1152]{1,0:T(8,128)} %get-tuple-element.126) | copy-start | bytes 110596
  624.8 15.4 %copy-start.72 = (f32[8]{0:T(128)S(1)}, f32[8]{0:T(128)}, u32[]{:S(2)}) copy-start(f32[8]{0:T(128)} %slice_reduce_fusion.1) | copy-start | bytes 100
  624.8 17.3 %copy-start.67 = (f32[8,144]{1,0:T(8,128)S(1)}, f32[8,144]{1,0:T(8,128)}, u32[]{:S(2)}) copy-start(f32[8,144]{1,0:T(8,128)} %get-tuple-element.128) | copy-start | bytes 13828
  624.8 21.4 %copy-start.30 = (bf16[4,144,288]{2,1,0:T(8,128)(2,1)S(1)}, bf16[4,144,288]{2,1,0:T(8,128)(2,1)}, u32[]{:S(2)}) copy-start(bf16[4,144,288]{2,1,0:T(8,128)(2,1)} %get-tuple-element.132) | copy-start | bytes 995332
  661.1 6.3 copy-start.31
  685.2 39.6 %copy-start.53 = (f32[2304]{0:T(1024)S(1)}, f32[2304]{0:T(1024)}, u32[]{:S(2)}) copy-start(f32[2304]{0:T(1024)} %param.45) | copy-start | bytes 27652
  685.2 41.2 %copy-start.37 = (f32[32,1152]{1,0:T(8,128)S(1)}, f32[32,1152]{1,0:T(8,128)}, u32[]{:S(2)}) copy-start(f32[32,1152]{1,0:T(8,128)} %param.37) | copy-start | bytes 442372
  685.2 41.2 %copy-start.38 = (f32[32,1152]{1,0:T(8,128)S(1)}, f32[32,1152]{1,0:T(8,128)}, u32[]{:S(2)}) copy-start(f32[32,1152]{1,0:T(8,128)} %get-tuple-element.299) | copy-start | bytes 442372
  685.2 43.0 %copy-start.25 = (f32[1000,144]{0,1:T(8,128)S(1)}, f32[1000,144]{0,1:T(8,128)}, u32[]{:S(2)}) copy-start(f32[1000,144]{0,1:T(8,128)} %param.39) | copy-start | bytes 1728004
  691.7 49.3 %copy-start.10 = (f32[144,4608]{1,0:T(8,128)}, f32[144,4608]{1,0:T(8,128)S(1)}, u32[]{:S(2)}) copy-start(f32[144,4608]{1,0:T(8,128)S(1)} %reshape.439) | copy-start | bytes 7962628
  724.8 6.4 copy-start.32
  724.8 6.4 copy-start.33
  724.8 6.4 copy-start.34
  728.2 6.0 copy-start.35
  728.2 6.0 copy-start.36
  737.1 5.5 copy-start.23
  747.4 9.4 %copy-start.4 = (f32[1152,864]{0,1:T(8,128)S(1)}, f32[1152,864]{0,1:T(8,128)}, u32[]{:S(2)}) copy-start(f32[1152,864]{0,1:T(8,128)} %param.40) | copy-start | bytes 11943940
  747.4 9.4 %copy-start.5 = (f32[1152,864]{0,1:T(8,128)S(1)}, f32[1152,864]{0,1:T(8,128)}, u32[]{:S(2)}) copy-start(f32[1152,864]{0,1:T(8,128)} %get-tuple-element.305) | copy-start | bytes 11943940
  747.4 10.5 %copy-start.17 = (f32[1152,864]{0,1:T(8,128)S(1)}, f32[1152,864]{0,1:T(8,128)}, u32[]{:S(2)}) copy-start(f32[1152,864]{0,1:T(8,128)} %param.49) | copy-start | bytes 11943940
  (42 other events, 117.0 us)

commit v3 on v2

--- a/solution.py
+++ b/solution.py
@@ -211,12 +211,6 @@
 GATHER_RANKS_SEMS = [DMA(()), DMA((3,)), DMA((4,))]
 
 
-def gather_both(src, out, sems):
-    rank = lax.axis_index("seq")
-    yield from gather_owners(src, out.at[rank], sems[:3])
-    yield from gather_ranks(out.at[rank], out, sems[3:], local_copy=False)
-
-
 def by_rows(count, body, step=16):
     def one(index, carry):
         body(pl.ds(pl.multiple_of(index * step, step), step))
@@ -281,7 +275,7 @@
         sends.start(remote(parts.at[to * 2 + 1 - y], mail.at[to], y_sent.at[to], y_landed.at[to], fsdp=mate))
         loads[to] = pltpu.make_async_copy(parts.at[to * 2 + y], own.at[to], own_sem.at[to])
         loads[to].start()
-    yield
+        yield
     for to, up in ((3, True), (0, False), (2, True), (1, False), (1, True), (2, False)):
         here = (z < to) if up else (z > to)
         more = (z > 0) if up else (z < 3)
@@ -513,30 +507,28 @@
     return jax.ShapeDtypeStruct(tuple(dims), kind)
 
 
-def forward_first(w_in, w_out, tokens, note, first, second, table, modulation):
+def forward_first(w_io, tokens, note, first, second, table, modulation):
     rows, width = second.shape
     wide = modulation.shape[1]
 
     def kernel(*refs):
-        args, outs, scratch, cond_sems, in_sems, out_sems, token_sems = takes(refs, 8, 9, 5, 10, 3, 6, 3)
+        args, outs, scratch, cond_sems, io_sems, token_sems = takes(refs, 7, 8, 5, 10, 3, 3)
         greet(True, True)
         run_all(
             [
-                condition_forward(args[3], *args[4:8], outs[3:9], scratch, cond_sems),
-                gather_both(args[1], outs[1], out_sems),
-                gather_ranks(args[2], outs[2], token_sems),
-                gather_owners(args[0], outs[0], in_sems),
+                condition_forward(args[2], *args[3:7], outs[2:8], scratch, cond_sems),
+                gather_ranks(args[1], outs[1], token_sems),
+                gather_owners(args[0], outs[0], io_sems),
             ]
         )
 
     return call(
         kernel,
         1,
-        (w_in, w_out, tokens, note, first, second, table, modulation),
-        [VMEM] * 8,
+        (w_io, tokens, note, first, second, table, modulation),
+        [VMEM] * 7,
         [
-            shape((8,) + w_in.shape, LOW),
-            shape((4, 8) + w_out.shape, LOW),
+            shape((8,) + w_io.shape, LOW),
             shape((4,) + tokens.shape, LOW),
             shape(note.shape, F32),
             shape((8, rows), F32),
@@ -545,7 +537,7 @@
             shape((8, width), F32),
             shape((8, 1, wide), F32),
         ],
-        [HBM] * 3 + [VMEM] * 6,
+        [HBM] * 2 + [VMEM] * 6,
         [
             pltpu.VMEM((2, 8, 8, rows), F32),
             pltpu.VMEM((8, 8, rows), F32),
@@ -555,10 +547,116 @@
         ]
         + SWAP_SEMS * 5
         + GATHER_OWNERS_SEMS
-        + GATHER_OWNERS_SEMS
-        + GATHER_RANKS_SEMS
         + GATHER_RANKS_SEMS,
         "forward_first",
+    )
+
+
+QUERIES = 256
+
+
+def block_of(index, size=QUERIES):
+    return pl.ds(pl.multiple_of(index * size, size), size)
+
+
+def attend_heads(qkv, mixed, logs, head_rows, heads):
+    length = qkv.shape[0]
+    span = heads * HD
+    scale = 1.0 / math.sqrt(HD)
+    for head in range(heads):
+        for part in range(3):
+            start = part * span + head * HD
+            head_rows[part] = qkv[:, start : start + HD]
+
+        def block(index, carry):
+            query = head_rows[0, block_of(index)]
+            scores = low_dot(head_rows[1], query, (1, 1)) * scale
+            top = jnp.max(scores, axis=0, keepdims=True)
+            expo = jnp.exp(scores - top)
+            total = jnp.sum(expo, axis=0, keepdims=True)
+            probs = (expo * (1.0 / total)).astype(LOW)
+            mixed[block_of(index), head * HD : (head + 1) * HD] = low_dot(head_rows[2], probs, (0, 0)).T.astype(LOW)
+            logs[head, index] = top + jnp.log(total)
+            return carry
+
+        lax.fori_loop(0, length // QUERIES, block, 0)
+        yield
+
+
+def attend_heads_back(qkv, logs, d_mixed, d_qkv, head_rows, d_head, d_keys, d_values, heads):
+    length = qkv.shape[0]
+    span = heads * HD
+    scale = 1.0 / math.sqrt(HD)
+    for head in range(heads):
+        lanes = slice(head * HD, (head + 1) * HD)
+        for part in range(3):
+            start = part * span + head * HD
+            head_rows[part] = qkv[:, start : start + HD]
+        d_head[...] = d_mixed[:, lanes]
+        d_keys[...] = jnp.zeros_like(d_keys)
+        d_values[...] = jnp.zeros_like(d_values)
+
+        def block(index, carry):
+            query, d_block = head_rows[0, block_of(index)], d_head[block_of(index)]
+            scores = low_dot(head_rows[1], query, (1, 1)) * scale
+            probs = jnp.exp(scores - logs[head, index])
+            d_probs = low_dot(head_rows[2], d_block, (1, 1))
+            delta = jnp.sum(probs * d_probs, axis=0, keepdims=True)
+            d_scores = (probs * (d_probs - delta)).astype(LOW)
+            d_keys[...] += low_dot(d_scores, query, (1, 0))
+            d_values[...] += low_dot(probs.astype(LOW), d_block, (1, 0))
+            d_query = low_dot(head_rows[1], d_scores, (0, 0)).T * scale
+            d_qkv[block_of(index), lanes] = d_query.astype(LOW)
+            return carry
+
+        lax.fori_loop(0, length // QUERIES, block, 0)
+        d_qkv[:, span + head * HD : span + (head + 1) * HD] = (d_keys[...] * scale).astype(LOW)
+        d_qkv[:, 2 * span + head * HD : 2 * span + (head + 1) * HD] = d_values[...].astype(LOW)
+        yield
+
+
+def forward_attention(qkv, w_up, w_down, upstream, w_out):
+    length = qkv.shape[0]
+    heads = qkv.shape[1] // (3 * HD)
+    span = heads * HD
+
+    def kernel(*refs):
+        args, outs, scratch, up_sems, down_sems, token_sems, out_sems, mixed_sems = takes(refs, 5, 6, 2, 3, 3, 3, 3, 3)
+        mixed_here, head_rows = scratch
+        greet(True, True)
+
+        def attention():
+            yield from attend_heads(args[0], mixed_here, outs[5], head_rows, heads)
+            yield from gather_ranks(mixed_here, outs[4], mixed_sems)
+
+        run_all(
+            [
+                gather_owners(args[1], outs[0], up_sems),
+                gather_owners(args[2], outs[1], down_sems),
+                gather_ranks(args[4], outs[3], out_sems),
+                attention(),
+                gather_ranks(args[3], outs[2], token_sems),
+            ]
+        )
+
+    return call(
+        kernel,
+        2,
+        (qkv, w_up, w_down, upstream, w_out),
+        [VMEM] * 5,
+        [
+            shape((8,) + w_up.shape, LOW),
+            shape((8,) + w_down.shape, LOW),
+            shape((4,) + upstream.shape, LOW),
+            shape((4,) + w_out.shape, LOW),
+            shape((4, length, span), LOW),
+            shape((heads, length // QUERIES, 1, QUERIES), F32),
+        ],
+        [HBM] * 5 + [VMEM],
+        [pltpu.VMEM((length, span), LOW), pltpu.VMEM((3, length, HD), LOW)]
+        + GATHER_OWNERS_SEMS * 2
+        + GATHER_RANKS_SEMS * 3,
+        "forward_attention",
     )
 
 
@@ -621,49 +719,178 @@
     )
 
 
-def backward_last(blocks, news, second, modulation, cond_cut, time_slope):
-    many = len(blocks)
+def row_cuts(rows):
+    half = (rows // 2 + 15) // 16 * 16
+    return [(0, half), (half, rows - half)]
+
+
+def scatter_items(parts, outs, scratch):
+    items, at = [], 0
+    for part, out in zip(parts, outs):
+        for start, count in row_cuts(part.shape[1]):
+            rows = pl.ds(start, count)
+            refs = scratch[at]
+            items.append(scatter_owners(part.at[:, rows], out.at[:, rows], *refs[:5], refs[5:]))
+            at += 1
+    return items
+
+
+def scatter_items_scratch(blocks):
+    scratch = []
+    for block in blocks:
+        for _, count in row_cuts(block.shape[1]):
+            scratch += scatter_owners_scratch(count, block.shape[2])
+    return scratch
+
+
+def backward_attention(g_up, g_down, my_d_attn, mlp_part, qkv, w_out, logs, units):
+    length = qkv.shape[0]
+    heads = qkv.shape[1] // (3 * HD)
+    span = heads * HD
+    rows, width = my_d_attn.shape
+
+    def kernel(*refs):
+        groups = takes(refs, 7, 5, 7, 7, 3, *[14] * 4)
+        args, outs, scratch, sum_scratch, token_sems = groups[:5]
+        d_mixed, head_rows, d_head, d_keys, d_values, up_all, _ = scratch
+        greet(True, True)
+
+        def attention():
+            yield from gather_ranks(args[2], outs[2], token_sems)
+            for part in range(4):
+                d_mixed[part * rows : (part + 1) * rows] = low_dot(outs[2][part], args[5][...], (1, 1)).astype(LOW)
+            yield
+            yield from attend_heads_back(
+                args[4], args[6], d_mixed, outs[4], head_rows, d_head, d_keys, d_values, heads
+            )
+
+        run_all(
+            scatter_items(args[:2], (up_all, outs[1]), groups[5:])
+            + [attention(), scatter_ranks(args[3], outs[3], *sum_scratch[:4], sum_scratch[4:])]
+        )
+        owners = up_all.shape[2] // units
+
+        def assemble(at):
+            for part in range(4):
+                for owner in range(owners):
+                    to = (owner * 4 + part) * units
+                    outs[0][at, to : to + units] = up_all[part, at, owner * units : (owner + 1) * units]
+
+        by_rows(up_all.shape[1], assemble)
+
+    return call(
+        kernel,
+        9,
+        (g_up, g_down, my_d_attn, mlp_part, qkv, w_out, logs),
+        [HBM, HBM, VMEM, HBM, VMEM, VMEM, VMEM],
+        [
+            shape((g_up.shape[1], 4 * g_up.shape[2]), LOW),
+            shape((4,) + g_down.shape[1:], LOW),
+            shape((4,) + my_d_attn.shape, LOW),
+            shape(my_d_attn.shape, F32),
+            shape(qkv.shape, LOW),
+        ],
+        [VMEM, HBM, VMEM, VMEM, VMEM],
+        [
+            pltpu.VMEM((length, span), LOW),
+            pltpu.VMEM((3, length, HD), LOW),
+            pltpu.VMEM((length, HD), LOW),
+            pltpu.VMEM((length, HD), F32),
+            pltpu.VMEM((length, HD), F32),
+            pltpu.VMEM((4,) + g_up.shape[1:], LOW),
+            pltpu.VMEM((8, 128), F32),
+        ]
+        + scatter_ranks_scratch(rows, width)
+        + GATHER_RANKS_SEMS
+        + scatter_items_scratch([g_up, g_down]),
+        "backward_attention",
+    )
+
+
+def backward_last(g_io, news, second, modulation, cond_cut, time_slope):
     rows, width = second.shape
+    span = g_io.shape[2] // 4
 
     def kernel(*refs):
-        groups = takes(refs, many + 5, many + 4, 5, 12, *[14] * many)
-        args, outs, scratch, sems = groups[:4]
+        groups = takes(refs, 6, 6, 5, 12, 1, *[14] * 2)
+        args, outs, scratch, sems, (io_all,) = groups[:5]
         greet(True, True)
         run_all(
-            [condition_backward(*args[many:], outs[many:], scratch, sems)]
-            + [
-                scatter_owners(args[at], outs[at], *groups[4 + at][:5], groups[4 + at][5:])
-                for at in range(many)
-            ]
-        )
-
-    scratch = [
-        pltpu.VMEM((4,) + news.shape, F32),
-        pltpu.VMEM(news.shape, F32),
-        pltpu.VMEM((8, 8, rows), F32),
-        pltpu.VMEM((8, 8, rows), F32),
-        pltpu.VMEM((8, 8, rows), F32),
-        DMA((3,)),
-        DMA((4,)),
-    ] + SWAP_SEMS * 5
-    for block in blocks:
-        scratch += scatter_owners_scratch(*block.shape[1:])
+            [condition_backward(*args[1:], outs[2:], scratch, sems)] + scatter_items(args[:1], (io_all,), groups[5:])
+        )
+
+        def assemble(at):
+            for part in range(4):
+                for block in range(3):
+                    to = (block * 4 + part) * span
+                    outs[0][at, to : to + span] = io_all[part, at, block * span : (block + 1) * span]
+                outs[1][at, part * span : (part + 1) * span] = io_all[part, at, 3 * span :]
+
+        by_rows(rows, assemble)
+
     return call(
         kernel,
         8,
-        tuple(blocks) + (news, second, modulation, cond_cut, time_slope),
-        [HBM] * many + [VMEM] * 5,
-        [shape((4,) + block.shape[1:], LOW) for block in blocks]
-        + [
+        (g_io, news, second, modulation, cond_cut, time_slope),
+        [HBM] + [VMEM] * 5,
+        [
+            shape((rows, 12 * span), LOW),
+            shape((rows, 4 * span), LOW),
             shape(news.shape, F32),
             shape((8, width), F32),
             shape((8, 8, rows), F32),
             shape((8, 1, modulation.shape[1]), F32),
         ],
-        [HBM] * many + [VMEM] * 4,
-        scratch,
+        [VMEM] * 6,
+        [
+            pltpu.VMEM((4,) + news.shape, F32),
+            pltpu.VMEM(news.shape, F32),
+            pltpu.VMEM((8, 8, rows), F32),
+            pltpu.VMEM((8, 8, rows), F32),
+            pltpu.VMEM((8, 8, rows), F32),
+            DMA((3,)),
+            DMA((4,)),
+        ]
+        + SWAP_SEMS * 5
+        + [pltpu.VMEM((4,) + g_io.shape[1:], LOW)]
+        + scatter_items_scratch([g_io]),
         "backward_last",
     )
+
+
+def pick_weights(attend_in, attend_out, expand, rank, span, units):
+    rows = attend_in.shape[0]
+    owners = expand.shape[1] // (4 * units)
+    if not fast():
+        w_in = pick(attend_in.reshape(rows, 3, 4, span), rank, 2).astype(LOW).reshape(rows, 3 * span)
+        w_up = pick(expand.reshape(rows, owners, 4, units), rank, 2).astype(LOW).reshape(rows, owners * units)
+        return jnp.concatenate([w_in, mine(attend_out, 1, 4, rank).astype(LOW)], axis=1), w_up
+
+    def kernel(in_ref, out_ref, up_ref, io, up):
+        here = lax.axis_index("seq")
+        for part in range(4):
+
+            @pl.when(here == part)
+            def _(part=part):
+                def one(at):
+                    for block in range(3):
+                        start = (block * 4 + part) * span
+                        io[at, block * span : (block + 1) * span] = in_ref[at, start : start + span].astype(LOW)
+                    io[at, 3 * span :] = out_ref[at, part * span : (part + 1) * span].astype(LOW)
+                    for owner in range(owners):
+                        start = (owner * 4 + part) * units
+                        up[at, owner * units : (owner + 1) * units] = up_ref[at, start : start + units].astype(LOW)
+
+                by_rows(rows, one)
+
+    return pl.pallas_call(
+        kernel,
+        out_shape=[shape((rows, 4 * span), LOW), shape((rows, owners * units), LOW)],
+        in_specs=[VMEM] * 3,
+        out_specs=[VMEM] * 2,
+        compiler_params=pltpu.CompilerParams(vmem_limit_bytes=32 * 1024 * 1024),
+        name="pick_weights",
+    )(attend_in, attend_out, expand)
 
 
 def sum_owners(number, value, name):
@@ -744,7 +971,7 @@
     return (master, moment_next, square_next)
 
 
-def condition_start(latent_tokens, w_in, w_out, biases, timesteps, labels, time_first, time_second, class_table, modulation):
+def condition_start(latent_tokens, w_io, biases, timesteps, labels, time_first, time_second, class_table, modulation):
     owners, owner = lax.axis_size("fsdp"), lax.axis_index("fsdp")
     share = biases.shape[0]
     width = time_first.shape[1]
@@ -763,8 +990,8 @@
             ],
             axis=1,
         )[:, None]
-        w_in_all, w_out_all, tokens, notes, act, slope, cond_cut, cond, mod = forward_first(
-            w_in, w_out, latent_tokens, note, first, second, table, modulation_low
+        w_io_all, tokens, notes, act, slope, cond_cut, cond, mod = forward_first(
+            w_io, latent_tokens, note, first, second, table, modulation_low
         )
         notes = notes[:, 0]
         all_bias = notes[:, :share].reshape(owners * share)
@@ -772,9 +999,8 @@
         all_labels = notes[:, share + units]
         mod_values = mod.reshape(owners * mod.shape[2])
         state = (first, second, modulation_low, my_features, all_labels, act, slope, cond_cut, cond)
-        return w_in_all, w_out_all, tokens, all_bias, mod_values, state
-    w_in_all, w_out_part = lax.all_gather(w_in, "fsdp", axis=0), lax.all_gather(w_out, "fsdp", axis=0)
-    w_out_all = lax.all_gather(w_out_part, "seq", axis=0)
+        return w_io_all, tokens, all_bias, mod_values, state
+    w_io_all = lax.all_gather(w_io, "fsdp", axis=0)
     tokens = lax.all_gather(latent_tokens, "seq", axis=0)
     note = jnp.concatenate([bias_low, features[0].astype(F32), labels.astype(F32)])
     notes = lax.all_gather(note, "fsdp", axis=0)
@@ -792,10 +1018,15 @@
     mod_part = mixed_dot("bd,de->be", silu_parts(cond)[0].astype(LOW), modulation_low)
     mod_values = pick(lax.all_gather(mod_part, "fsdp", axis=0), owner, 1).reshape(owners * mod_part.shape[1])
     state = (first, second, modulation_low, my_features, all_labels, act.astype(F32), slope, None, cond)
-    return w_in_all, w_out_all, tokens, all_bias, mod_values, state
-
-
-def condition_end(state, blocks, my_d_mod, tail, share):
+    return w_io_all, tokens, all_bias, mod_values, state
+
+
+def owner_sums(blocks):
+    summed = [lax.psum_scatter(block.astype(F32), "fsdp", scatter_dimension=0, tiled=False) for block in blocks]
+    return [lax.all_gather(block.astype(LOW), "seq", axis=0) for block in summed]
+
+
+def condition_end(state, g_io, my_d_mod, tail, share):
     first, second, modulation_low, my_features, all_labels, act, slope, cond_cut, cond = state
     owners, owner, rank = lax.axis_size("fsdp"), lax.axis_index("fsdp"), lax.axis_index("seq")
     wide, width = modulation_low.shape[1], cond.shape[1]
@@ -805,7 +1036,7 @@
         news = jnp.concatenate(
             [my_d_mod.reshape(owners, wide), jnp.zeros((owners, pad), F32), tails], axis=1
         )[:, None]
-        *grads, by_latent, d_cond, d_hid, sums = backward_last(blocks, news, second, modulation_low, cond_cut, slope)
+        grad_in, grad_out, by_latent, d_cond, d_hid, sums = backward_last(g_io, news, second, modulation_low, cond_cut, slope)
         d_mod = by_latent[:, 0, :wide]
         my_tail = jnp.sum(by_latent[:, 0, wide + pad :], axis=0)
         d_hidden = d_hid.transpose(1, 0, 2).reshape(owners, width)
@@ -815,8 +1046,10 @@
             owner < count, pick(front.reshape(count, share), jnp.minimum(owner, count - 1)), my_tail
         )
     else:
-        summed = [lax.psum_scatter(block.astype(F32), "fsdp", scatter_dimension=0, tiled=False) for block in blocks]
-        grads = [lax.all_gather(block.astype(LOW), "seq", axis=0) for block in summed]
+        (grad_io,) = owner_sums([g_io])
+        rows, span = grad_io.shape[1], grad_io.shape[2] // 4
+        grad_in = grad_io[:, :, : 3 * span].reshape(4, rows, 3, span).transpose(1, 2, 0, 3).reshape(rows, 12 * span)
+        grad_out = grad_io[:, :, 3 * span :].transpose(1, 0, 2).reshape(rows, 4 * span)
         all_d_mod = lax.all_gather(lax.psum(my_d_mod, "seq"), "fsdp", axis=0)
         d_mod = mine(all_d_mod, 1, owners, owner)
         part = high_dot(d_mod, modulation_low.astype(F32).T)
@@ -835,7 +1068,7 @@
     grad_second = high_dot(act.T, d_cond)
     grad_first = high_dot(my_features.T, d_hidden)
     condition_gradient = lax.dynamic_slice_in_dim(d_cond, owner, 1, 0)
-    return grads, (grad_first, grad_second, grad_class, grad_mod), grad_bias, condition_gradient
+    return grad_in, grad_out, (grad_first, grad_second, grad_class, grad_mod), grad_bias, condition_gradient
 
 
 def per_device(latents, timesteps, labels, upstream, *state):
@@ -854,19 +1087,14 @@
     unit = hidden // (owners * ranks)
     hid_here = owners * unit
 
-    my_in = pick(attend_in.reshape(rows, 3, ranks, span), rank, 2).astype(LOW).reshape(rows, 3 * span)
-    my_out = mine(attend_out, 1, ranks, rank).astype(LOW)
-    my_up = pick(expand.reshape(rows, owners, ranks, unit), rank, 2).astype(LOW).reshape(rows, hid_here)
+    my_io, my_up = pick_weights(attend_in, attend_out, expand, rank, span, unit)
     my_down = mine(contract, 0, ranks, rank).astype(LOW)
-    w_in, w_out, tokens, all_bias, mod_values, kept = condition_start(
-        latents[0], my_in, my_out, biases, timesteps, labels, time_first, time_second, class_table, modulation
-    )
-    w_in = w_in.reshape(width, 3 * span)
-    w_out = w_out.transpose(1, 2, 0, 3).reshape(width, width)
+    w_io, tokens, all_bias, mod_values, kept = condition_start(
+        latents[0], my_io, biases, timesteps, labels, time_first, time_second, class_table, modulation
+    )
+    w_io = w_io.reshape(width, 4 * span)
+    w_in = w_io[:, : 3 * span]
     inputs_low = tokens.reshape(length, width)
-    w_up, w_down, d_out_low = gathers(2, [my_up, my_down], [upstream[0]], "forward_second")
-    w_up, w_down = w_up.reshape(width, hid_here), w_down.reshape(hid_here, width)
-    d_out_low = d_out_low.reshape(length, width)
 
     b_t1, b_t2, b_mod, b_q, b_v, b_out, b_up, b_down = split_biases(all_bias, width, hidden)
     mod_values = (mod_values + b_mod).reshape(6, 1, width)
@@ -879,9 +1107,19 @@
     qkv_bias = jnp.concatenate([my_b_q, jnp.zeros_like(my_b_q), my_b_v])
     qkv = (mixed_dot("td,de->te", h_attn, w_in) + qkv_bias).astype(LOW)
     head_shape = (length, heads_here, HD)
-    query, keys, values = [qkv[:, part * span : (part + 1) * span].reshape(head_shape) for part in range(3)]
-    mixed_heads, log_total = attend(query, keys, values)
-    (mixed,) = gathers(3, [], [mixed_heads.reshape(length, span)], "gather_mixed")
+    if fast():
+        w_up, w_down, d_out_low, w_out, mixed, logs = forward_attention(
+            qkv, my_up, my_down, upstream[0], w_io[:, 3 * span :]
+        )
+    else:
+        query, keys, values = [qkv[:, part * span : (part + 1) * span].reshape(head_shape) for part in range(3)]
+        mixed_heads, logs = attend(query, keys, values)
+        w_up, w_down, d_out_low, w_out, mixed = gathers(
+            2, [my_up, my_down], [upstream[0], w_io[:, 3 * span :], mixed_heads.reshape(length, span)], "gathers"
+        )
+    w_up, w_down = w_up.reshape(width, hid_here), w_down.reshape(hid_here, width)
+    d_out_low = d_out_low.reshape(length, width)
+    w_out = w_out.transpose(1, 0, 2).reshape(width, width)
     mixed = mixed.transpose(1, 0, 2).reshape(length, width)
     attn_out = mixed_dot("td,de->te", mixed, w_out) + b_out
     middle = inputs + gate1 * attn_out
@@ -900,7 +1138,7 @@
     d_act = mixed_dot("td,fd->tf", d_mlp, w_down)
     d_pre = gelu_pull(d_act)[0].astype(LOW)
     d_hmlp_part = mixed_dot("tf,df->td", d_pre, w_up).astype(LOW).reshape(by_rank)
-    d_hmlp, mlp_sum = rank_sums(4, [d_hmlp_part, mlp_part], "sum_feed")
+    (d_hmlp,) = rank_sums(4, [d_hmlp_part], "sum_feed")
     g_down = by_owner(mixed_dot("tf,td->fd", act, d_mlp))
     g_up = by_owner(mixed_dot("td,tf->df", h_mlp, d_pre))
     gb_up = jnp.sum(d_pre.astype(F32), axis=0)
@@ -909,20 +1147,37 @@
     own = lambda array: mine(array, 0, ranks, rank)
     my_attn_out, my_middle, my_norm_two, my_inverse_two = own(attn_out), own(middle), own(norm_two), own(inverse_two)
     my_d_out = upstream[0].astype(F32)
-    mlp_out = mlp_sum + b_down
-    output = (my_middle + gate2 * mlp_out).astype(LOW)
-    d_gate2 = jnp.sum(my_d_out * mlp_out, axis=0)
     d_shift2 = jnp.sum(d_hmlp, axis=0)
     d_scale2 = jnp.sum(d_hmlp * my_norm_two, axis=0)
     d_middle = my_d_out + layer_norm_back(my_norm_two, my_inverse_two, d_hmlp * (1.0 + scale2))
     d_gate1 = jnp.sum(d_middle * my_attn_out, axis=0)
     my_d_attn = (d_middle * gate1).astype(LOW)
-    (d_attn,) = gathers(5, [], [my_d_attn], "gather_d_attn")
-    d_attn = d_attn.reshape(length, width)
-    d_mixed = mixed_dot("te,de->td", d_attn, mine(w_out, 0, ranks, rank)).astype(LOW)
-    g_out = by_owner(mixed_dot("td,te->de", mixed, mine(d_attn, 1, ranks, rank)))
-    d_qkv = attend_back(query, keys, values, d_mixed.reshape(head_shape), log_total)
-    g_in = by_owner(mixed_dot("td,te->de", h_attn, d_qkv))
+    my_w_out = mine(w_out, 0, ranks, rank)
+    if fast():
+        grad_up, grad_down, d_attn, mlp_sum, d_qkv = backward_attention(
+            g_up, g_down, my_d_attn, mlp_part, qkv, my_w_out, logs, unit
+        )
+        d_attn = d_attn.reshape(length, width)
+    else:
+        (mlp_sum,) = rank_sums(5, [mlp_part], "sums")
+        (d_attn,) = gathers(5, [], [my_d_attn], "gathers")
+        d_attn = d_attn.reshape(length, width)
+        d_mixed = mixed_dot("te,de->td", d_attn, my_w_out).astype(LOW)
+        d_qkv = attend_back(query, keys, values, d_mixed.reshape(head_shape), logs)
+        grad_up, grad_down = owner_sums([g_up, g_down])
+        grad_up = grad_up.reshape(ranks, rows, owners, unit).transpose(1, 2, 0, 3).reshape(rows, hidden)
+    mlp_out = mlp_sum + b_down
+    output = (my_middle + gate2 * mlp_out).astype(LOW)
+    d_gate2 = jnp.sum(my_d_out * mlp_out, axis=0)
+    g_io = by_owner(
+        jnp.concatenate(
+            [
+                mixed_dot("td,te->de", h_attn, d_qkv).astype(LOW),
+                mixed_dot("td,te->de", mixed, mine(d_attn, 1, ranks, rank)).astype(LOW),
+            ],
+            axis=1,
+        )
+    )
     d_hattn_part = mixed_dot("te,de->td", d_qkv, w_in).astype(LOW).reshape(by_rank)
     (d_hattn,) = rank_sums(6, [d_hattn_part], "sum_attend")
     my_inputs = latents[0].astype(F32)
@@ -946,13 +1201,10 @@
             jnp.where(rank == 0, gb_down, 0.0),
         ]
     )
-    grads, small_grads, grad_bias, condition_gradient = condition_end(
-        kept, [g_down, g_up, g_out, g_in], my_d_mod, gb_tail, biases.shape[0]
-    )
-    grad_down, grad_up, grad_out, grad_in = [grad.astype(F32) for grad in grads]
-    grad_in = grad_in.reshape(ranks, rows, 3, span).transpose(1, 2, 0, 3).reshape(rows, 3 * width)
-    grad_out = grad_out.transpose(1, 0, 2).reshape(rows, width)
-    grad_up = grad_up.reshape(ranks, rows, owners, unit).transpose(1, 2, 0, 3).reshape(rows, hidden)
+    grad_in, grad_out, small_grads, grad_bias, condition_gradient = condition_end(
+        kept, g_io, my_d_mod, gb_tail, biases.shape[0]
+    )
+    grad_in, grad_out, grad_up, grad_down = [grad.astype(F32) for grad in (grad_in, grad_out, grad_up, grad_down)]
     grad_down = grad_down.reshape(contract.shape)
     gradients = small_grads + (grad_in, grad_out, grad_up, grad_down, grad_bias)
     local_sum = sum(jnp.sum(gradient * gradient) for gradient in gradients)

time: 773 us -> 593 us (0.77)
  Pallas kernels: 425 us -> 354 us
  local copies, waits for them, and re-layouts: 119 us -> 60.2 us
  matrix products: 112 us -> 66.2 us
  other arithmetic: 98.1 us -> 90.3 us
    pallas_call x8 -> x7, Pallas kernels: 425 us -> 354 us  [call(): pl.pallas_call(kernel, out_shape=outs, in_specs=in_specs, out_specs=out_s...]
    dot_general x24 -> x11, matrix products: 102 us -> 54.7 us  [mixed_dot(): return jnp.einsum(form, left, right, preferred_element_type=jnp.float32)]
    reshape x7 -> x0, local copies, waits for them, and re-layouts: 29.2 us -> none  [the longest x1 6.56 us: per_device(): grad_up.reshape(ranks, rows, owners, unit).transpose(1, 2, 0, 3)]
    transpose x6 -> x1, local copies, waits for them, and re-layouts: 23.7 us -> 4.96 us  [per_device(): w_out = w_out.transpose(1, 0, 2).reshape(width, width)]
    convert_element_type x5 -> x0, local copies, waits for them, and re-layouts: 10.7 us -> none  [the longest x2 6.77 us: per_device(): block.astype(LOW).reshape((owners, -1) + block.shape[1:])]
    unnamed x183 -> x155, local copies, waits for them, and re-layouts: 18.9 us -> 20.8 us
where the time goes in v3:
time: 593 us; the launch traced here: 582 us
  Pallas kernels  354 us (60%)
  other arithmetic  90.3 us (15%)
  matrix products  66.2 us (11%)
  local copies, waits for them, and re-layouts  60.2 us (10%)
  between operations  11.1 us (2%)
    pallas_call x7, Pallas kernels, call(): pl.pallas_call(kernel, out_shape=outs, in_specs=in_specs, out_specs=out_s...  354 us
    dot_general x11, matrix products, mixed_dot(): return jnp.einsum(form, left, right, preferred_element_type=jnp.float32)  54.7 us
    sub x9, other arithmetic, adam_step(): weight - learn_rate * (moment_hat / (jnp.sqrt(square_hat) + adam_eps) + w...  33.7 us
    unnamed x155, local copies, waits for them, and re-layouts  20.8 us

profile of v3, /device:TPU:0, one launch (start us, length us, event | category | flops | bytes accessed | tf_op | source)
XLA Modules:
  0.0 582.2 jit_solution(10851416972472448715)
XLA Ops:
  10.6 2.0 copy.85.refs_5_
  12.5 1.9 dynamic-slice_convert_fusion.refs_2_
  14.4 1.9 convert_element_type.158.refs_4_.refs_2_
  20.2 4.6 copy.84.refs_6_.refs_3_
  24.7 51.9 %forward_first.1 = (bf16[8,144,1152]{2,1,0:T(8,128)(2,1)}, bf16[4,256,1152]{2,1,0:T(8,128)(2,1)}, f32[8,1,2432]{2,1,0:T(1,128)}, f32[8,144]{1,0:T(8,128)}, f32[8...) custom-call(bf16[144,1152]{1,0:T(8,128)(2,1)} %copy-done.5, ...), custom_call_target="tpu_custom_call" | custom-call | tf_op jit(solution)/shard_map/forward_first/pallas_call | solution.py:493
  77.5 2.2 convert_reduce_fusion
  89.1 2.5 slice.111.refs_4_
  91.6 2.8 fusion.13
  95.7 3.9 add_convert_fusion.1.refs_0_.refs_4_
  99.6 71.8 %forward_attention.1 = (bf16[8,144,1152]{2,1,0:T(8,128)(2,1)}, bf16[8,144,1152]{2,1,0:T(8,128)(2,1)}, bf16[4,256,1152]{2,1,0:T(8,128)(2,1)}, bf16[4,1152,288]{2,...) custom-call(bf16[1024,864]{1,0:T(8,128)(2,1)} %add_convert_fusion.1.refs_0_.refs_4_, ...), custom_call_target="tpu_custom_call" | custom-call | tf_op jit(solution)/shard_map/forward_attention/pallas_call | solution.py:493
  171.4 4.5 copy.87
  175.8 5.0 copy.88
  180.8 2.6 constant_dynamic-slice_fusion.1
  183.4 2.3 copy.95.refs_5_
  185.7 3.7 fusion.7
  191.1 3.5 fusion.70
  194.7 5.3 fusion.67
  203.5 5.7 convert_reduce_fusion.2
  209.2 5.4 convolution_convert_fusion.3
  214.6 4.7 convolution_convert_fusion.4
  220.2 19.5 %sum_feed.1 = f32[256,1152]{1,0:T(8,128)} custom-call(bf16[4,256,1152]{2,1,0:T(8,128)(2,1)} %bitcast.94), custom_call_target="tpu_custom_call" | custom-call | tf_op jit(solution)/shard_map/sum_feed/pallas_call | solution.py:493
  239.8 2.8 multiply_reduce_fusion.5
  242.6 8.0 %convolution_convert_fusion.1 = bf16[1152,1152]{1,0:T(8,128)(2,1)} fusion(bf16[1024,1152]{1,0:T(8,128)(2,1)} %copy-done.67, f32[1024,1152]{1,0:T(8,128)} %copy-done.12, f32[1152]{0:T(1024)S(1)} %copy-done.60, f32[1152]{0:T(1024)S(1)} %copy-done.44), kind=kOutput, calls=%fused_computation.1 | convolution fusion | flops 2722775040 | bytes 9741312 | tf_op jit(solution)/shard_map/td,tf->df/dot_general | solution.py:69
  250.7 3.1 convert_reduce_fusion.5
  253.8 5.2 convolution_convert_fusion
  259.0 90.8 %backward_attention.1 = (bf16[144,4608]{1,0:T(8,128)(2,1)}, bf16[4,144,1152]{2,1,0:T(8,128)(2,1)}, bf16[4,256,1152]{2,1,0:T(8,128)(2,1)}, f32[256,1152]{1,0:T(8,128)}, bf16[1024,864]{1,0:T(8,128)(2,1)}) custom-call(bf16[8,144,1152]{2,1,0:T(8,128)(2,1)} %bitcast.92, bf16[8,144,1152]{2,1,0:T(8,128)(2,1)} %bitcast.93, ...), custom_call_target="tpu_custom_call" | custom-call | tf_op jit(solution)/shard_map/backward_attention/pallas_call | solution.py:493
  349.9 6.1 %convolution_convert_fusion.5 = bf16[1152,864]{0,1:T(8,128)(2,1)} fusion(bf16[1024,1152]{1,0:T(8,128)(2,1)} %copy-done.25, bf16[1024,864]{1,0:T(8,128)(2,1)} %get-tuple-element.80), kind=kOutput, calls=%fused_computation.44 | convolution fusion | flops 2039427072 | bytes 6119424 | tf_op jit(solution)/shard_map/td,te->de/dot_general | solution.py:69
  356.0 4.2 convolution_convert_fusion.2
  361.5 19.3 %sum_attend.1 = f32[256,1152]{1,0:T(8,128)} custom-call(bf16[4,256,1152]{2,1,0:T(8,128)(2,1)} %bitcast.96), custom_call_target="tpu_custom_call" | custom-call | tf_op jit(solution)/shard_map/sum_attend/pallas_call | solution.py:493
  380.9 3.5 fusion.35
  384.3 2.6 convolution_convert_fusion.6
  388.7 5.2 copy.90
  396.1 2.0 fusion.33
  400.8 3.7 multiply_reduce_fusion.6
  407.0 88.7 %backward_last.1 = (bf16[144,3456]{1,0:T(8,128)(2,1)}, bf16[144,1152]{1,0:T(8,128)(2,1)}, f32[8,1,3200]{2,1,0:T(1,128)}, f32[8,1152]{1,0:T(8,128)}, f32[8,8,144]{2,1,0:T(8,128)}, /*index=5*/f32[8,1,864]{2,1,0:T(1,128)}) custom-call(bf16[8,144,1152]{2,1,0:T(8,128)(2,1)} %bitcast.86, f32[8,1,3200]{2,1,0:T(1,128)} %broadcast_in_dim.64.refs_1_, ...), custom_call_target="tpu_custom_call" | custom-call | tf_op jit(solution)/shard_map/backward_last/pallas_call | solution.py:493
  504.7 2.7 multiply_reduce_fusion.12
  507.4 2.9 multiply_reduce_fusion.11
  512.3 2.6 multiply_reduce_fusion.10
  514.9 3.5 multiply_reduce_fusion.4
  518.4 2.7 multiply_reduce_fusion.3
  521.1 4.3 multiply_reduce_fusion.1
  529.9 11.5 %sum_squares.1 = f32[8,128]{1,0:T(8,128)} custom-call(f32[8,128]{1,0:T(8,128)} %broadcast_in_dim.65.src), custom_call_target="tpu_custom_call" | custom-call | tf_op jit(solution)/shard_map/sum_squares/pallas_call | solution.py:493
  544.1 1.9 multiply_subtract_fusion.7
  546.0 3.2 multiply_subtract_fusion.6
  554.5 3.8 multiply_subtract_fusion.3
  560.0 4.6 multiply_subtract_fusion.2
  564.6 8.4 %multiply_subtract_fusion.1 = (f32[576,1152]{1,0:T(8,128)}, f32[576,1152]{1,0:T(8,128)}, f32[576,1152]{1,0:T(8,128)}, f32[576,1152]{1,0:T(8,128)}) fusion(f32[576,1152]{1,0:T(8,128)} %param.42, f32[]{:T(128)S(6)} %div.181, f32[576,1152]{1,0:T(8,128)} %param.51, f32[576,1152]{1,0:T(8,128)} %param.60, bf16[4,144,1152]{2,1,0:T(8,128)(2,1)S(1)} %copy-done.17), kind=kLoop, calls=%fused_computation.49 | loop fusion | flops 11280384 | bytes 19906564 | tf_op jit(solution)/shard_map/sub | solution.py:968
  573.1 7.8 %multiply_subtract_fusion = (f32[1152,864]{0,1:T(8,128)}, f32[1152,864]{0,1:T(8,128)}, f32[1152,864]{0,1:T(8,128)}) fusion(f32[1152,864]{0,1:T(8,128)S(1)} %copy-done.9, f32[1152,864]{0,1:T(8,128)S(1)} %copy-done.10, f32[]{:T(128)S(6)} %div.181, f32[1152,864]{0,1:T(8,128)} %param.47, f32[1152,864]{0,1:T(8,128)} %param.56), kind=kLoop, calls=%fused_computation.36 | loop fusion | flops 15925248 | bytes 27869188 | tf_op jit(solution)/shard_map/sub | solution.py:968
  (240 shorter events, 58.4 us)
Async XLA Ops:
  0.7 15.5 %copy-start = (f32[144,4608]{1,0:T(8,128)S(1)}, f32[144,4608]{1,0:T(8,128)}, u32[]{:S(2)}) copy-start(f32[144,4608]{1,0:T(8,128)} %up_ref.1) | copy-start | bytes 7962628
  0.7 15.5 %copy-start.3 = (f32[144,1152]{1,0:T(8,128)S(1)}, f32[144,1152]{1,0:T(8,128)}, u32[]{:S(2)}) copy-start(f32[144,1152]{1,0:T(8,128)} %out_ref.1) | copy-start | bytes 1990660
  77.5 4.2 copy-start.43
  91.6 4.2 copy-start.39
  91.6 4.2 copy-start.63
  180.8 4.9 copy-start.41
  185.7 3.7 copy-start.14
  191.1 3.6 copy-start.61
  203.5 5.7 copy-start.12
  209.2 5.4 copy-start.66
  209.2 5.4 copy-start.67
  220.2 22.3 %copy-start.60 = (f32[1152]{0:T(1024)S(1)}, f32[1152]{0:T(1024)}, u32[]{:S(2)}) copy-start(f32[1152]{0:T(1024)} %get-tuple-element.156) | copy-start | bytes 13828
  239.8 14.0 %slice-start = ((s8[4718592]{0:T(1024)(128)(4,1)}), s8[4194304]{0:T(1024)(128)(4,1)S(1)}, s32[]{:S(2)}) async-start(s8[4718592]{0:T(1024)(128)(4,1)} %bitcast.115), calls=%async_computation | async-start | bytes 8388608
  242.6 8.1 %copy-start.11 = (f32[256,1152]{1,0:T(8,128)S(1)}, f32[256,1152]{1,0:T(8,128)}, u32[]{:S(2)}) copy-start(f32[256,1152]{1,0:T(8,128)} %sum_feed.1) | copy-start | bytes 3538948
  242.6 8.1 %copy-start.18 = (bf16[1,256,1152]{2,1,0:T(8,128)(2,1)S(1)}, bf16[1,256,1152]{2,1,0:T(8,128)(2,1)}, u32[]{:S(2)}) copy-start(bf16[1,256,1152]{2,1,0:T(8,128)(2,1)} %param.34) | copy-start | bytes 1769476
  242.6 8.1 %copy-start.49 = (f32[1152]{0:T(1024)S(1)}, f32[1152]{0:T(1024)}, u32[]{:S(2)}) copy-start(f32[1152]{0:T(1024)} %get-tuple-element.160) | copy-start | bytes 13828
  242.6 8.0 %copy-start.62 = (f32[256]{0:T(256)S(1)}, f32[256]{0:T(256)}, u32[]{:S(2)}) copy-start(f32[256]{0:T(256)} %dynamic-slice.3) | copy-start | bytes 3076
  242.6 11.2 %slice-start.1 = ((s8[4718592]{0:T(1024)(128)(4,1)}), s8[524288]{0:T(1024)(128)(4,1)S(1)}, s32[]{:S(2)}) async-start(s8[4718592]{0:T(1024)(128)(4,1)} %bitcast.115), calls=%async_computation.1 | async-start | bytes 1048576
  349.9 6.2 %copy-start.32 = (bf16[1024,864]{1,0:T(8,128)(2,1)S(1)}, bf16[1024,864]{1,0:T(8,128)(2,1)}, u32[]{:S(2)}) copy-start(bf16[1024,864]{1,0:T(8,128)(2,1)} %get-tuple-element.80) | copy-start | bytes 5308420
  349.9 6.2 %copy-start.40 = (bf16[8,144,1152]{2,1,0:T(8,128)(2,1)S(1)}, bf16[8,144,1152]{2,1,0:T(8,128)(2,1)}, u32[]{:S(2)}) copy-start(bf16[8,144,1152]{2,1,0:T(8,128)(2,1)} %get-tuple-element.71) | copy-start | bytes 7962628
  356.0 4.2 copy-start.16
  360.2 20.6 %copy-start.54 = (f32[1152]{0:T(1024)S(1)}, f32[1152]{0:T(1024)}, u32[]{:S(2)}) copy-start(f32[1152]{0:T(1024)} %get-tuple-element.151) | copy-start | bytes 13828
  388.7 7.4 %copy-start.42 = (f32[4608]{0:T(1024)S(1)}, f32[4608]{0:T(1024)}, u32[]{:S(2)}) copy-start(f32[4608]{0:T(1024)} %reshape.330) | copy-start | bytes 55300
  388.7 7.4 %copy-start.50 = (f32[1152]{0:T(1024)S(1)}, f32[1152]{0:T(1024)}, u32[]{:S(2)}) copy-start(f32[1152]{0:T(1024)} %get-tuple-element.138) | copy-start | bytes 13828
  400.8 3.7 copy-start.55
  400.8 3.7 copy-start.52
  400.8 3.8 copy-start.51
  400.8 3.8 copy-start.53
  407.0 100.4 %copy-start.58 = (f32[8,144]{1,0:T(8,128)S(1)}, f32[8,144]{1,0:T(8,128)}, u32[]{:S(2)}) copy-start(f32[8,144]{1,0:T(8,128)} %get-tuple-element.86) | copy-start | bytes 13828
  502.2 41.2 %copy-start.46 = (f32[2304]{0:T(1024)}, f32[2304]{0:T(1024)S(1)}, u32[]{:S(2)}) copy-start(f32[2304]{0:T(1024)S(1)} %get-tuple-element.131) | copy-start | bytes 27652
  512.3 6.2 %copy-start.33 = (bf16[144,4608]{1,0:T(8,128)(2,1)S(1)}, bf16[144,4608]{1,0:T(8,128)(2,1)}, u32[]{:S(2)}) copy-start(bf16[144,4608]{1,0:T(8,128)(2,1)} %get-tuple-element.91) | copy-start | bytes 3981316
  521.1 22.2 %copy-start.45 = (f32[2304]{0:T(1024)S(1)}, f32[2304]{0:T(1024)}, u32[]{:S(2)}) copy-start(f32[2304]{0:T(1024)} %param.43) | copy-start | bytes 27652
  521.1 22.3 %copy-start.56 = (f32[2304]{0:T(1024)S(1)}, f32[2304]{0:T(1024)}, u32[]{:S(2)}) copy-start(f32[2304]{0:T(1024)} %param.52) | copy-start | bytes 27652
  521.1 22.3 %copy-start.57 = (f32[2304]{0:T(1024)S(1)}, f32[2304]{0:T(1024)}, u32[]{:S(2)}) copy-start(f32[2304]{0:T(1024)} %param.61) | copy-start | bytes 27652
  521.1 22.9 %copy-start.38 = (f32[32,1152]{1,0:T(8,128)S(1)}, f32[32,1152]{1,0:T(8,128)}, u32[]{:S(2)}) copy-start(f32[32,1152]{1,0:T(8,128)} %param.35) | copy-start | bytes 442372
  543.4 5.8 copy-start.21
  543.4 5.8 copy-start.34
  543.4 5.8 copy-start.35
  546.0 4.9 copy-start.36
  546.0 4.9 copy-start.37
  549.2 4.0 copy-start.30
  550.9 3.6 copy-start.15
  554.5 3.8 copy-start.13
  554.5 4.5 copy-start.23
  554.5 5.5 copy-start.24
  560.0 4.6 copy-start.17
  564.6 8.4 %copy-start.9 = (f32[1152,864]{0,1:T(8,128)S(1)}, f32[1152,864]{0,1:T(8,128)}, u32[]{:S(2)}) copy-start(f32[1152,864]{0,1:T(8,128)} %param.38) | copy-start | bytes 11943940
  564.6 8.4 %copy-start.10 = (f32[1152,864]{0,1:T(8,128)S(1)}, f32[1152,864]{0,1:T(8,128)}, u32[]{:S(2)}) copy-start(f32[1152,864]{0,1:T(8,128)} %get-tuple-element.172) | copy-start | bytes 11943940
  (22 other events, 50.4 us)

commit v4 on v3

--- a/solution.py
+++ b/solution.py
@@ -174,7 +174,7 @@
                 remote(out.at[block], out.at[block], sent.at[at, 0], landed.at[block], fsdp=owner - sign * 2), here & on
             )
             sends.start(remote(out.at[block], out.at[block], sent.at[at, 2], landed.at[block], fsdp=mate), here)
-            yield
+        yield
     for step in range(4):
         block = step * 2 + 1 - y
         arrived(out.at[block], landed.at[block], fsdp=mate)
@@ -489,7 +489,7 @@
     return groups
 
 
-def call(kernel, number, args, in_specs, outs, out_specs, scratch, name):
+def call(kernel, number, args, in_specs, outs, out_specs, scratch, name, room):
     return pl.pallas_call(
         kernel,
         out_shape=outs,
@@ -497,7 +497,7 @@
         out_specs=out_specs,
         scratch_shapes=scratch,
         compiler_params=pltpu.CompilerParams(
-            collective_id=number, has_side_effects=True, vmem_limit_bytes=60 * 1024 * 1024
+            collective_id=number, has_side_effects=True, vmem_limit_bytes=room * 1024 * 1024
         ),
         name=name,
     )(*args)
@@ -549,6 +549,7 @@
         + GATHER_OWNERS_SEMS
         + GATHER_RANKS_SEMS,
         "forward_first",
+        20,
     )
 
 
@@ -615,48 +616,75 @@
         yield
 
 
-def forward_attention(qkv, w_up, w_down, upstream, w_out):
+def beside(blocks, out):
+    columns = blocks.shape[2]
+
+    def one(at):
+        for part in range(4):
+            out[at, part * columns : (part + 1) * columns] = blocks[part, at]
+
+    by_rows(out.shape[0], one)
+
+
+def forward_attention(qkv, w_up, w_down, upstream, w_io):
     length = qkv.shape[0]
     heads = qkv.shape[1] // (3 * HD)
     span = heads * HD
+    width = w_io.shape[0]
 
     def kernel(*refs):
-        args, outs, scratch, up_sems, down_sems, token_sems, out_sems, mixed_sems = takes(refs, 5, 6, 2, 3, 3, 3, 3, 3)
-        mixed_here, head_rows = scratch
+        args, outs, scratch, up_sems, down_sems, token_sems, out_sems, mixed_sems = takes(refs, 5, 6, 5, 3, 3, 3, 3, 3)
+        mixed_here, head_rows, mixed_all, out_here, out_all = scratch
         greet(True, True)
 
         def attention():
-            yield from attend_heads(args[0], mixed_here, outs[5], head_rows, heads)
-            yield from gather_ranks(mixed_here, outs[4], mixed_sems)
+            steps = attend_heads(args[0], mixed_here, outs[5], head_rows, heads)
+            for index, _ in enumerate(steps):
+                if 0 < index < heads - 1:
+                    yield
+            yield from gather_ranks(mixed_here, mixed_all, mixed_sems)
+
+        def out_weight():
+            out_here[...] = args[4][:, 3 * span :]
+            yield from gather_ranks(out_here, out_all, out_sems)
+            beside(out_all, outs[3])
 
         run_all(
             [
                 gather_owners(args[1], outs[0], up_sems),
                 gather_owners(args[2], outs[1], down_sems),
-                gather_ranks(args[4], outs[3], out_sems),
+                out_weight(),
                 attention(),
                 gather_ranks(args[3], outs[2], token_sems),
             ]
         )
+        beside(mixed_all, outs[4])
 
     return call(
         kernel,
         2,
-        (qkv, w_up, w_down, upstream, w_out),
+        (qkv, w_up, w_down, upstream, w_io),
         [VMEM] * 5,
         [
             shape((8,) + w_up.shape, LOW),
             shape((8,) + w_down.shape, LOW),
             shape((4,) + upstream.shape, LOW),
-            shape((4,) + w_out.shape, LOW),
-            shape((4, length, span), LOW),
+            shape((width, 4 * span), LOW),
+            shape((length, 4 * span), LOW),
             shape((heads, length // QUERIES, 1, QUERIES), F32),
         ],
-        [HBM] * 5 + [VMEM],
-        [pltpu.VMEM((length, span), LOW), pltpu.VMEM((3, length, HD), LOW)]
+        [HBM] * 3 + [VMEM] * 3,
+        [
+            pltpu.VMEM((length, span), LOW),
+            pltpu.VMEM((3, length, HD), LOW),
+            pltpu.VMEM((4, length, span), LOW),
+            pltpu.VMEM((width, span), LOW),
+            pltpu.VMEM((4, width, span), LOW),
+        ]
         + GATHER_OWNERS_SEMS * 2
         + GATHER_RANKS_SEMS * 3,
         "forward_attention",
+        40,
     )
 
 
@@ -686,6 +714,7 @@
         [HBM] * len(blocks),
         GATHER_OWNERS_SEMS * many + GATHER_RANKS_SEMS * few,
         name,
+        16,
     )
 
 
@@ -716,29 +745,45 @@
         [VMEM] * many,
         scratch,
         name,
-    )
-
-
-def row_cuts(rows):
-    half = (rows // 2 + 15) // 16 * 16
-    return [(0, half), (half, rows - half)]
-
-
-def scatter_items(parts, outs, scratch):
+        16,
+    )
+
+
+def row_cuts(rows, cuts):
+    step = (rows // cuts + 15) // 16 * 16
+    return [(start, min(step, rows - start)) for start in range(0, rows, step)]
+
+
+def together(parts, first):
+    parts = list(parts)
+    for _ in range(first):
+        for part in parts:
+            next(part)
+    yield
+    while parts:
+        for part in list(parts):
+            try:
+                next(part)
+            except StopIteration:
+                parts.remove(part)
+        yield
+
+
+def scatter_items(parts, outs, scratch, cuts):
     items, at = [], 0
     for part, out in zip(parts, outs):
-        for start, count in row_cuts(part.shape[1]):
+        for start, count in row_cuts(part.shape[1], cuts):
             rows = pl.ds(start, count)
             refs = scratch[at]
             items.append(scatter_owners(part.at[:, rows], out.at[:, rows], *refs[:5], refs[5:]))
             at += 1
-    return items
-
-
-def scatter_items_scratch(blocks):
+    return [together(items, 4)]
+
+
+def scatter_items_scratch(blocks, cuts):
     scratch = []
     for block in blocks:
-        for _, count in row_cuts(block.shape[1]):
+        for _, count in row_cuts(block.shape[1], cuts):
             scratch += scatter_owners_scratch(count, block.shape[2])
     return scratch
 
@@ -750,22 +795,26 @@
     rows, width = my_d_attn.shape
 
     def kernel(*refs):
-        groups = takes(refs, 7, 5, 7, 7, 3, *[14] * 4)
+        groups = takes(refs, 7, 5, 6, 7, 3, *[14] * 6)
         args, outs, scratch, sum_scratch, token_sems = groups[:5]
-        d_mixed, head_rows, d_head, d_keys, d_values, up_all, _ = scratch
+        d_mixed, head_rows, d_head, d_keys, d_values, up_all = scratch
         greet(True, True)
 
         def attention():
-            yield from gather_ranks(args[2], outs[2], token_sems)
+            tokens = gather_ranks(args[2], outs[2], token_sems)
+            next(tokens)
+            yield
+            for _ in tokens:
+                pass
+            w_rows = args[5][pl.ds(pl.multiple_of(lax.axis_index("seq") * span, 16), span)]
             for part in range(4):
-                d_mixed[part * rows : (part + 1) * rows] = low_dot(outs[2][part], args[5][...], (1, 1)).astype(LOW)
-            yield
+                d_mixed[part * rows : (part + 1) * rows] = low_dot(outs[2][part], w_rows, (1, 1)).astype(LOW)
             yield from attend_heads_back(
                 args[4], args[6], d_mixed, outs[4], head_rows, d_head, d_keys, d_values, heads
             )
 
         run_all(
-            scatter_items(args[:2], (up_all, outs[1]), groups[5:])
+            scatter_items(args[:2], (up_all, outs[1]), groups[5:], 3)
             + [attention(), scatter_ranks(args[3], outs[3], *sum_scratch[:4], sum_scratch[4:])]
         )
         owners = up_all.shape[2] // units
@@ -798,50 +847,76 @@
             pltpu.VMEM((length, HD), F32),
             pltpu.VMEM((length, HD), F32),
             pltpu.VMEM((4,) + g_up.shape[1:], LOW),
-            pltpu.VMEM((8, 128), F32),
         ]
         + scatter_ranks_scratch(rows, width)
         + GATHER_RANKS_SEMS
-        + scatter_items_scratch([g_up, g_down]),
+        + scatter_items_scratch([g_up, g_down], 3),
         "backward_attention",
-    )
-
-
-def backward_last(g_io, news, second, modulation, cond_cut, time_slope):
+        50,
+    )
+
+
+def backward_last(g_in, g_out, d_tokens, tokens, scale, d_middle, news, second, modulation, cond_cut, time_slope):
     rows, width = second.shape
-    span = g_io.shape[2] // 4
+    span = g_out.shape[2]
+    tok_rows = tokens.shape[0]
+    wide = modulation.shape[1]
 
     def kernel(*refs):
-        groups = takes(refs, 6, 6, 5, 12, 1, *[14] * 2)
-        args, outs, scratch, sems, (io_all,) = groups[:5]
+        groups = takes(refs, 11, 7, 5, 12, 7, 5, *[14] * 4)
+        args, outs, scratch, sems, sum_scratch, (in_all, out_all, d_sum, edge, news_here) = groups[:6]
         greet(True, True)
-        run_all(
-            [condition_backward(*args[1:], outs[2:], scratch, sems)] + scatter_items(args[:1], (io_all,), groups[5:])
-        )
+
+        def condition():
+            yield from scatter_ranks(args[2], d_sum, *sum_scratch[:4], sum_scratch[4:])
+            edge[...] = jnp.zeros_like(edge)
+
+            def one(at):
+                value = args[3][at].astype(F32)
+                norm, inverse = layer_norm(value)
+                grad = d_sum[at]
+                edge[0] += jnp.sum(grad.reshape(2, 8, width), axis=0)
+                edge[1] += jnp.sum((grad * norm).reshape(2, 8, width), axis=0)
+                outs[2][at] = args[5][at] + layer_norm_back(norm, inverse, grad * (1.0 + args[4][...]))
+
+            by_rows(tok_rows, one)
+            news_here[...] = args[6][...]
+            line = jnp.concatenate(
+                [jnp.sum(edge[0], axis=0, keepdims=True), jnp.sum(edge[1], axis=0, keepdims=True)], axis=1
+            )
+            at = 0
+            while at * wide < 2 * width:
+                end = min((at + 1) * wide, 2 * width)
+                news_here[at, :, : end - at * wide] = line[:, at * wide : end]
+                at += 1
+            yield from condition_backward(news_here, *args[7:], outs[3:], scratch, sems)
+
+        run_all([condition()] + scatter_items(args[:2], (in_all, out_all), groups[6:], 2))
 
         def assemble(at):
             for part in range(4):
                 for block in range(3):
                     to = (block * 4 + part) * span
-                    outs[0][at, to : to + span] = io_all[part, at, block * span : (block + 1) * span]
-                outs[1][at, part * span : (part + 1) * span] = io_all[part, at, 3 * span :]
+                    outs[0][at, to : to + span] = in_all[part, at, block * span : (block + 1) * span]
+                outs[1][at, part * span : (part + 1) * span] = out_all[part, at]
 
         by_rows(rows, assemble)
 
     return call(
         kernel,
         8,
-        (g_io, news, second, modulation, cond_cut, time_slope),
-        [HBM] + [VMEM] * 5,
+        (g_in, g_out, d_tokens, tokens, scale, d_middle, news, second, modulation, cond_cut, time_slope),
+        [HBM] * 3 + [VMEM] * 8,
         [
             shape((rows, 12 * span), LOW),
             shape((rows, 4 * span), LOW),
+            shape(tokens.shape, F32),
             shape(news.shape, F32),
             shape((8, width), F32),
             shape((8, 8, rows), F32),
-            shape((8, 1, modulation.shape[1]), F32),
+            shape((8, 1, wide), F32),
         ],
-        [VMEM] * 6,
+        [VMEM] * 7,
         [
             pltpu.VMEM((4,) + news.shape, F32),
             pltpu.VMEM(news.shape, F32),
@@ -852,9 +927,17 @@
             DMA((4,)),
         ]
         + SWAP_SEMS * 5
-        + [pltpu.VMEM((4,) + g_io.shape[1:], LOW)]
-        + scatter_items_scratch([g_io]),
+        + scatter_ranks_scratch(tok_rows, width)
+        + [
+            pltpu.VMEM((4,) + g_in.shape[1:], LOW),
+            pltpu.VMEM((4,) + g_out.shape[1:], LOW),
+            pltpu.VMEM((tok_rows, width), F32),
+            pltpu.VMEM((2, 8, width), F32),
+            pltpu.VMEM(news.shape, F32),
+        ]
+        + scatter_items_scratch([g_in, g_out], 2),
         "backward_last",
+        36,
     )
 
 
@@ -912,7 +995,7 @@
 
     block = jnp.full((8, 128), value, F32)
     total = call(
-        kernel, number, (block,), [VMEM], shape((8, 128), F32), VMEM, [pltpu.VMEM((8, 8, 128), F32)] + SWAP_SEMS, name
+        kernel, number, (block,), [VMEM], shape((8, 128), F32), VMEM, [pltpu.VMEM((8, 8, 128), F32)] + SWAP_SEMS, name, 4
     )
     return total[0, 0]
 
@@ -1026,17 +1109,20 @@
     return [lax.all_gather(block.astype(LOW), "seq", axis=0) for block in summed]
 
 
-def condition_end(state, g_io, my_d_mod, tail, share):
+def condition_end(state, g_in, g_out, d_tokens, tokens, scale1, d_middle, d_mod_rest, tail, share):
     first, second, modulation_low, my_features, all_labels, act, slope, cond_cut, cond = state
     owners, owner, rank = lax.axis_size("fsdp"), lax.axis_index("fsdp"), lax.axis_index("seq")
     wide, width = modulation_low.shape[1], cond.shape[1]
+    blank = jnp.zeros((2 * width,), F32)
     if fast():
         pad = -wide % 128
         tails = jnp.concatenate([jnp.zeros((owners * share - tail.shape[0],), F32), tail]).reshape(owners, share)
         news = jnp.concatenate(
-            [my_d_mod.reshape(owners, wide), jnp.zeros((owners, pad), F32), tails], axis=1
+            [jnp.concatenate([blank, d_mod_rest]).reshape(owners, wide), jnp.zeros((owners, pad), F32), tails], axis=1
         )[:, None]
-        grad_in, grad_out, by_latent, d_cond, d_hid, sums = backward_last(g_io, news, second, modulation_low, cond_cut, slope)
+        grad_in, grad_out, input_gradient, by_latent, d_cond, d_hid, sums = backward_last(
+            g_in, g_out, d_tokens, tokens, scale1, d_middle, news, second, modulation_low, cond_cut, slope
+        )
         d_mod = by_latent[:, 0, :wide]
         my_tail = jnp.sum(by_latent[:, 0, wide + pad :], axis=0)
         d_hidden = d_hid.transpose(1, 0, 2).reshape(owners, width)
@@ -1046,10 +1132,14 @@
             owner < count, pick(front.reshape(count, share), jnp.minimum(owner, count - 1)), my_tail
         )
     else:
-        (grad_io,) = owner_sums([g_io])
-        rows, span = grad_io.shape[1], grad_io.shape[2] // 4
-        grad_in = grad_io[:, :, : 3 * span].reshape(4, rows, 3, span).transpose(1, 2, 0, 3).reshape(rows, 12 * span)
-        grad_out = grad_io[:, :, 3 * span :].transpose(1, 0, 2).reshape(rows, 4 * span)
+        (d_hattn,) = rank_sums(6, [d_tokens], "sums")
+        norm, inverse = layer_norm(tokens.astype(F32))
+        input_gradient = d_middle + layer_norm_back(norm, inverse, d_hattn * (1.0 + scale1))
+        my_d_mod = jnp.concatenate([jnp.sum(d_hattn, axis=0), jnp.sum(d_hattn * norm, axis=0), d_mod_rest])
+        grad_in, grad_out = owner_sums([g_in, g_out])
+        rows, span = grad_out.shape[1], grad_out.shape[2]
+        grad_in = grad_in.reshape(4, rows, 3, span).transpose(1, 2, 0, 3).reshape(rows, 12 * span)
+        grad_out = grad_out.transpose(1, 0, 2).reshape(rows, 4 * span)
         all_d_mod = lax.all_gather(lax.psum(my_d_mod, "seq"), "fsdp", axis=0)
         d_mod = mine(all_d_mod, 1, owners, owner)
         part = high_dot(d_mod, modulation_low.astype(F32).T)
@@ -1068,7 +1158,7 @@
     grad_second = high_dot(act.T, d_cond)
     grad_first = high_dot(my_features.T, d_hidden)
     condition_gradient = lax.dynamic_slice_in_dim(d_cond, owner, 1, 0)
-    return grad_in, grad_out, (grad_first, grad_second, grad_class, grad_mod), grad_bias, condition_gradient
+    return grad_in, grad_out, input_gradient, (grad_first, grad_second, grad_class, grad_mod), grad_bias, condition_gradient
 
 
 def per_device(latents, timesteps, labels, upstream, *state):
@@ -1109,7 +1199,7 @@
     head_shape = (length, heads_here, HD)
     if fast():
         w_up, w_down, d_out_low, w_out, mixed, logs = forward_attention(
-            qkv, my_up, my_down, upstream[0], w_io[:, 3 * span :]
+            qkv, my_up, my_down, upstream[0], w_io
         )
     else:
         query, keys, values = [qkv[:, part * span : (part + 1) * span].reshape(head_shape) for part in range(3)]
@@ -1117,10 +1207,10 @@
         w_up, w_down, d_out_low, w_out, mixed = gathers(
             2, [my_up, my_down], [upstream[0], w_io[:, 3 * span :], mixed_heads.reshape(length, span)], "gathers"
         )
+        w_out = w_out.transpose(1, 0, 2).reshape(width, width)
+        mixed = mixed.transpose(1, 0, 2).reshape(length, width)
     w_up, w_down = w_up.reshape(width, hid_here), w_down.reshape(hid_here, width)
     d_out_low = d_out_low.reshape(length, width)
-    w_out = w_out.transpose(1, 0, 2).reshape(width, width)
-    mixed = mixed.transpose(1, 0, 2).reshape(length, width)
     attn_out = mixed_dot("td,de->te", mixed, w_out) + b_out
     middle = inputs + gate1 * attn_out
     norm_two, inverse_two = layer_norm(middle)
@@ -1152,41 +1242,26 @@
     d_middle = my_d_out + layer_norm_back(my_norm_two, my_inverse_two, d_hmlp * (1.0 + scale2))
     d_gate1 = jnp.sum(d_middle * my_attn_out, axis=0)
     my_d_attn = (d_middle * gate1).astype(LOW)
-    my_w_out = mine(w_out, 0, ranks, rank)
     if fast():
         grad_up, grad_down, d_attn, mlp_sum, d_qkv = backward_attention(
-            g_up, g_down, my_d_attn, mlp_part, qkv, my_w_out, logs, unit
+            g_up, g_down, my_d_attn, mlp_part, qkv, w_out, logs, unit
         )
         d_attn = d_attn.reshape(length, width)
     else:
         (mlp_sum,) = rank_sums(5, [mlp_part], "sums")
         (d_attn,) = gathers(5, [], [my_d_attn], "gathers")
         d_attn = d_attn.reshape(length, width)
-        d_mixed = mixed_dot("te,de->td", d_attn, my_w_out).astype(LOW)
+        d_mixed = mixed_dot("te,de->td", d_attn, mine(w_out, 0, ranks, rank)).astype(LOW)
         d_qkv = attend_back(query, keys, values, d_mixed.reshape(head_shape), logs)
         grad_up, grad_down = owner_sums([g_up, g_down])
         grad_up = grad_up.reshape(ranks, rows, owners, unit).transpose(1, 2, 0, 3).reshape(rows, hidden)
     mlp_out = mlp_sum + b_down
     output = (my_middle + gate2 * mlp_out).astype(LOW)
     d_gate2 = jnp.sum(my_d_out * mlp_out, axis=0)
-    g_io = by_owner(
-        jnp.concatenate(
-            [
-                mixed_dot("td,te->de", h_attn, d_qkv).astype(LOW),
-                mixed_dot("td,te->de", mixed, mine(d_attn, 1, ranks, rank)).astype(LOW),
-            ],
-            axis=1,
-        )
-    )
+    g_in = by_owner(mixed_dot("td,te->de", h_attn, d_qkv))
+    g_out = by_owner(mixed_dot("td,te->de", mixed, mine(d_attn, 1, ranks, rank)))
     d_hattn_part = mixed_dot("te,de->td", d_qkv, w_in).astype(LOW).reshape(by_rank)
-    (d_hattn,) = rank_sums(6, [d_hattn_part], "sum_attend")
-    my_inputs = latents[0].astype(F32)
-    my_norm_one, my_inverse_one = layer_norm(my_inputs)
-    d_shift1 = jnp.sum(d_hattn, axis=0)
-    d_scale1 = jnp.sum(d_hattn * my_norm_one, axis=0)
-    input_gradient = d_middle + layer_norm_back(my_norm_one, my_inverse_one, d_hattn * (1.0 + scale1))
-
-    my_d_mod = jnp.concatenate([d_shift1, d_scale1, d_gate1, d_shift2, d_scale2, d_gate2])
+    d_mod_rest = jnp.concatenate([d_gate1, d_shift2, d_scale2, d_gate2])
     gb_qv = jnp.sum(d_qkv.astype(F32), axis=0)
     wide = lambda part, size: lax.dynamic_update_slice(jnp.zeros((size,), F32), part, (rank * part.shape[0],))
     gb_up_wide = lax.dynamic_update_slice(
@@ -1201,8 +1276,8 @@
             jnp.where(rank == 0, gb_down, 0.0),
         ]
     )
-    grad_in, grad_out, small_grads, grad_bias, condition_gradient = condition_end(
-        kept, g_io, my_d_mod, gb_tail, biases.shape[0]
+    grad_in, grad_out, input_gradient, small_grads, grad_bias, condition_gradient = condition_end(
+        kept, g_in, g_out, d_hattn_part, latents[0], scale1, d_middle, d_mod_rest, gb_tail, biases.shape[0]
     )
     grad_in, grad_out, grad_up, grad_down = [grad.astype(F32) for grad in (grad_in, grad_out, grad_up, grad_down)]
     grad_down = grad_down.reshape(contract.shape)

time: 593 us -> 504 us (0.85)
  Pallas kernels: 354 us -> 309 us
  other arithmetic: 90.3 us -> 61.5 us
  local copies, waits for them, and re-layouts: 60.2 us -> 50.2 us
    pallas_call x7 -> x6, Pallas kernels: 354 us -> 308 us  [call(): pl.pallas_call(kernel, out_shape=outs, in_specs=in_specs, out_specs=out_s...]
    unnamed x155 -> x186, local copies, waits for them, and re-layouts: 20.8 us -> 37 us
    transpose x2 -> x0, local copies, waits for them, and re-layouts: 9.41 us -> none  [the longest x1 4.96 us: per_device(): w_out = w_out.transpose(1, 0, 2).reshape(width, width)]
    convert_element_type x0 -> x2, local copies, waits for them, and re-layouts: none -> 6.53 us  [per_device(): block.astype(LOW).reshape((owners, -1) + block.shape[1:])]
where the time goes in v4:
time: 504 us; the launch traced here: 494 us
  Pallas kernels  309 us (61%)
  matrix products  62.4 us (12%)
  other arithmetic  61.5 us (12%)
  local copies, waits for them, and re-layouts  50.2 us (10%)
  between operations  11.3 us (2%)
    pallas_call x6, Pallas kernels, call(): pl.pallas_call(kernel, out_shape=outs, in_specs=in_specs, out_specs=out_s...  308 us
    dot_general x11, matrix products, mixed_dot(): return jnp.einsum(form, left, right, preferred_element_type=jnp.float32)  52.4 us
    unnamed x186, local copies, waits for them, and re-layouts  37 us
    sub x9, other arithmetic, adam_step(): weight - learn_rate * (moment_hat / (jnp.sqrt(square_hat) + adam_eps) + w...  33.8 us

profile of v4, /device:TPU:0, one launch (start us, length us, event | category | flops | bytes accessed | tf_op | source)
XLA Modules:
  0.0 494.0 jit_solution(12190678630763208363)
XLA Ops:
  3.8 1.6 convert_element_type.154.refs_3_
  7.3 1.9 dynamic-slice_convert_fusion.refs_2_
  10.3 1.5 copy-done.5
  15.3 4.6 copy.82.refs_6_.refs_8_
  20.0 1.6 copy-done
  23.6 44.7 %forward_first.1 = (bf16[8,144,1152]{2,1,0:T(8,128)(2,1)S(1)}, bf16[4,256,1152]{2,1,0:T(8,128)(2,1)S(1)}, f32[8,1,2432]{2,1,0:T(1,128)S(1)}, f32[8,144]{1,0:T(8,...) custom-call(bf16[144,1152]{1,0:T(8,128)(2,1)S(1)} %copy-done.32, ...), custom_call_target="tpu_custom_call" | custom-call | tf_op jit(solution)/shard_map/forward_first/pallas_call | solution.py:493
  68.3 1.5 copy-done.13
  76.9 2.8 add_convert_fusion.1.refs_0_.refs_4_
  79.7 71.8 %forward_attention.1 = (bf16[8,144,1152]{2,1,0:T(8,128)(2,1)S(1)}, bf16[8,144,1152]{2,1,0:T(8,128)(2,1)S(1)}, bf16[4,256,1152]{2,1,0:T(8,128)(2,1)S(1)}, bf16[11...) custom-call(bf16[1024,864]{1,0:T(8,128)(2,1)S(1)} %add_convert_fusion.1.refs_0_.refs_4_, ...), custom_call_target="tpu_custom_call" | custom-call | tf_op jit(solution)/shard_map/forward_attention/pallas_call | solution.py:493
  151.5 2.2 fusion.7
  154.4 3.5 fusion.58
  157.9 5.3 %fusion.55 = (f32[1024]{0:T(1024)S(1)}, f32[1024,1152]{1,0:T(8,128)S(1)}, f32[1024,1152]{1,0:T(8,128)}) fusion(f32[1152]{0:T(1024)S(1)} %get-tuple-element.157, bf16[4,256,1152]{2,1,0:T(8,128)(2,1)S(1)} %get-tuple-element.69, f32[1152]{0:T(1024)S(1)} %get-tuple-element.148, bf16[1024,1152]{1,0:T(8,128)(2,1)S(1)} %get-tuple-element.74, ...), kind=kOutput, calls=%fused_computation.152 | convolution fusion | flops 2723806208 | bytes 16823296 | tf_op jit(solution)/shard_map/td,de->te/dot_general | solution.py:69
  165.4 5.7 %convert_reduce_fusion.2 = (f32[1152]{0:T(1024)S(1)}, bf16[1024,1152]{1,0:T(8,128)(2,1)S(1)}, f32[1024,1152]{1,0:T(8,128)S(1)}) fusion(f32[1024,1152]{1,0:T(8,128)S(1)} %fusion.58, f32[1152]{0:T(1024)S(1)} %add.305, bf16[1152,1152]{1,0:T(8,128)(2,1)S(1)} %bitcast.88, f32[1024,1152]{1,0:T(8,128)S(1)} %subtract_multiply_fusion, ...), kind=kOutput, calls=%fused_computation.25 | convolution fusion | flops 2748578816 | bytes 19187712 | tf_op jit(solution)/shard_map/td,df->tf/dot_general | solution.py:69
  171.1 5.6 %convolution_convert_fusion.3 = bf16[1024,1152]{1,0:T(8,128)(2,1)} fusion(bf16[1152,1152]{1,0:T(8,128)(2,1)S(1)} %bitcast.91, f32[1024,1152]{1,0:T(8,128)S(1)} %get-tuple-element.161), kind=kOutput, calls=%fused_computation.40 | convolution fusion | flops 2729705472 | bytes 9732096 | tf_op jit(solution)/shard_map/tf,fd->td/dot_general | solution.py:69
  176.7 3.7 convolution_convert_fusion.4
  180.7 18.3 %sum_feed.1 = f32[256,1152]{1,0:T(8,128)S(1)} custom-call(bf16[4,256,1152]{2,1,0:T(8,128)(2,1)S(1)} %bitcast.84), custom_call_target="tpu_custom_call" | custom-call | tf_op jit(solution)/shard_map/sum_feed/pallas_call | solution.py:493
  199.0 1.8 multiply_reduce_fusion.5
  200.9 6.5 %convolution_convert_fusion.1 = bf16[1152,1152]{1,0:T(8,128)(2,1)} fusion(bf16[1024,1152]{1,0:T(8,128)(2,1)} %copy-done.83, f32[1024,1152]{1,0:T(8,128)S(1)} %copy-done.49, f32[1152]{0:T(1024)S(1)} %get-tuple-element.153, f32[1152]{0:T(1024)S(1)} %get-tuple-element.154), kind=kOutput, calls=%fused_computation.1 | convolution fusion | flops 2722775040 | bytes 9741312 | tf_op jit(solution)/shard_map/td,tf->df/dot_general | solution.py:69
  207.9 1.6 multiply_reduce_fusion.6
  209.6 5.2 %convolution_convert_fusion = bf16[1152,1152]{1,0:T(8,128)(2,1)} fusion(bf16[1024,1152]{1,0:T(8,128)(2,1)S(1)} %copy-done.65, f32[1024,1152]{1,0:T(8,128)S(1)} %bitcast.104), kind=kOutput, calls=%fused_computation | convolution fusion | flops 2729852928 | bytes 9732096 | tf_op jit(solution)/shard_map/tf,td->fd/dot_general | solution.py:69
  214.8 84.7 %backward_attention.1 = (bf16[144,4608]{1,0:T(8,128)(2,1)S(1)}, bf16[4,144,1152]{2,1,0:T(8,128)(2,1)}, bf16[4,256,1152]{2,1,0:T(8,128)(2,1)}, f32[256,1152]{1,0:T(8,128)S(1)}, bf16[1024,864]{1,0:T(8,128)(2,1)}) custom-call(bf16[8,144,1152]{2,1,0:T(8,128)(2,1)} %bitcast.92, bf16[8,144,1152]{2,1,0:T(8,128)(2,1)} %bitcast.93, ...), custom_call_target="tpu_custom_call" | custom-call | tf_op jit(solution)/shard_map/backward_attention/pallas_call | solution.py:493
  299.5 5.8 %convolution_convert_fusion.5 = bf16[1152,864]{0,1:T(8,128)(2,1)} fusion(bf16[1024,1152]{1,0:T(8,128)(2,1)S(1)} %copy-done.64, bf16[1024,864]{1,0:T(8,128)(2,1)} %get-tuple-element.81), kind=kOutput, calls=%fused_computation.44 | convolution fusion | flops 2039427072 | bytes 6119424 | tf_op jit(solution)/shard_map/td,te->de/dot_general | solution.py:69
  305.4 4.1 convolution_convert_fusion.2
  309.5 1.3 multiply_reduce_fusion.2
  310.8 2.3 fusion.23
  313.2 4.1 convolution_convert_fusion.6
  318.2 4.2 copy.85
  322.5 2.3 copy.86
  324.8 1.6 copy-done.4
  326.3 1.2 copy-done.10
  329.6 1.7 copy-done.20
  333.4 79.1 %backward_last.1 = (bf16[144,3456]{1,0:T(8,128)(2,1)S(1)}, bf16[144,1152]{1,0:T(8,128)(2,1)S(1)}, f32[256,1152]{1,0:T(8,128)S(1)}, f32[8,1,3200]{2,1,0:T(1,128)S...) custom-call(bf16[8,144,864]{2,1,0:T(8,128)(2,1)S(1)} %bitcast.76, ...), custom_call_target="tpu_custom_call" | custom-call | tf_op jit(solution)/shard_map/backward_last/pallas_call | solution.py:493
  418.4 1.6 multiply_reduce_fusion.12
  420.0 2.0 multiply_reduce_fusion.11
  422.0 2.1 multiply_reduce_fusion.10
  426.0 2.5 multiply_reduce_fusion.9
  428.5 2.3 multiply_reduce_fusion.4
  430.8 2.7 multiply_reduce_fusion.3
  433.6 4.3 multiply_reduce_fusion.1
  441.9 9.2 %sum_squares.1 = f32[8,128]{1,0:T(8,128)S(1)} custom-call(f32[8,128]{1,0:T(8,128)S(1)} %broadcast_in_dim.65.src), custom_call_target="tpu_custom_call" | custom-call | tf_op jit(solution)/shard_map/sum_squares/pallas_call | solution.py:493
  453.0 1.8 multiply_subtract_fusion.7
  454.8 2.8 multiply_subtract_fusion.6
  457.7 1.6 multiply_subtract_fusion.4
  459.4 1.6 multiply_subtract_fusion.5
  463.0 3.7 multiply_subtract_fusion.3
  469.2 4.7 multiply_subtract_fusion.2
  474.0 9.4 %multiply_subtract_fusion.1 = (f32[576,1152]{1,0:T(8,128)}, f32[576,1152]{1,0:T(8,128)}, f32[576,1152]{1,0:T(8,128)}, f32[576,1152]{1,0:T(8,128)}) fusion(f32[576,1152]{1,0:T(8,128)} %param.42, f32[]{:T(128)S(6)} %div.165, f32[576,1152]{1,0:T(8,128)} %param.51, f32[576,1152]{1,0:T(8,128)} %param.60, bf16[4,144,1152]{2,1,0:T(8,128)(2,1)S(1)} %copy-done.53), kind=kLoop, calls=%fused_computation.48 | loop fusion | flops 11280384 | bytes 19906564 | tf_op jit(solution)/shard_map/sub | solution.py:1051
  484.1 7.4 %multiply_subtract_fusion = (f32[1152,864]{0,1:T(8,128)}, f32[1152,864]{0,1:T(8,128)}, f32[1152,864]{0,1:T(8,128)}) fusion(f32[1152,864]{0,1:T(8,128)S(1)} %copy-done.46, f32[1152,864]{0,1:T(8,128)S(1)} %copy-done.47, f32[]{:T(128)S(6)} %div.165, f32[1152,864]{0,1:T(8,128)S(1)} %copy-done.54, f32[1152,864]{0,1:T(8,128)} %param.56), kind=kLoop, calls=%fused_computation.36 | loop fusion | flops 15925248 | bytes 27869188 | tf_op jit(solution)/shard_map/sub | solution.py:1051
  (260 shorter events, 39.1 us)
Async XLA Ops:
  0.7 9.6 %copy-start.2 = (f32[144,4608]{1,0:T(8,128)S(1)}, f32[144,4608]{1,0:T(8,128)}, u32[]{:S(2)}) copy-start(f32[144,4608]{1,0:T(8,128)} %up_ref.1) | copy-start | bytes 7962628
  13.0 7.0 %copy-start.11 = (bf16[144,1152]{1,0:T(8,128)(2,1)}, bf16[144,1152]{1,0:T(8,128)(2,1)S(1)}, u32[]{:S(2)}) copy-start(bf16[144,1152]{1,0:T(8,128)(2,1)S(1)} %convert_element_type.155.refs_4_.refs_7_) | copy-start | bytes 995332
  15.3 4.6 copy-start.33
  15.3 4.6 copy-start.34
  79.7 71.8 %copy-start.7 = (bf16[1024,864]{1,0:T(8,128)(2,1)}, bf16[1024,864]{1,0:T(8,128)(2,1)S(1)}, u32[]{:S(2)}) copy-start(bf16[1024,864]{1,0:T(8,128)(2,1)S(1)} %add_convert_fusion.1.refs_0_.refs_4_) | copy-start | bytes 5308420
  151.5 6.4 %copy-start.44 = (bf16[1024,1152]{1,0:T(8,128)(2,1)}, bf16[1024,1152]{1,0:T(8,128)(2,1)S(1)}, u32[]{:S(2)}) copy-start(bf16[1024,1152]{1,0:T(8,128)(2,1)S(1)} %get-tuple-element.74) | copy-start | bytes 7077892
  165.4 5.7 %copy-start.48 = (f32[1024,1152]{1,0:T(8,128)}, f32[1024,1152]{1,0:T(8,128)S(1)}, u32[]{:S(2)}) copy-start(f32[1024,1152]{1,0:T(8,128)S(1)} %subtract_multiply_fusion) | copy-start | bytes 14155780
  171.1 5.6 %copy-start.82 = (f32[1024,1152]{1,0:T(8,128)}, f32[1024,1152]{1,0:T(8,128)S(1)}, u32[]{:S(2)}) copy-start(f32[1024,1152]{1,0:T(8,128)S(1)} %get-tuple-element.161) | copy-start | bytes 14155780
  171.1 5.6 %copy-start.83 = (bf16[1024,1152]{1,0:T(8,128)(2,1)}, bf16[1024,1152]{1,0:T(8,128)(2,1)S(1)}, u32[]{:S(2)}) copy-start(bf16[1024,1152]{1,0:T(8,128)(2,1)S(1)} %get-tuple-element.139) | copy-start | bytes 7077892
  180.7 20.1 %copy-start.49 = (f32[1024,1152]{1,0:T(8,128)S(1)}, f32[1024,1152]{1,0:T(8,128)}, u32[]{:S(2)}) copy-start(f32[1024,1152]{1,0:T(8,128)} %copy-done.48) | copy-start | bytes 14155780
  199.0 10.6 %slice-start = ((s8[4718592]{0:T(1024)(128)(4,1)}), s8[4194304]{0:T(1024)(128)(4,1)S(1)}, s32[]{:S(2)}) async-start(s8[4718592]{0:T(1024)(128)(4,1)} %bitcast.103), calls=%async_computation | async-start | bytes 8388608
  200.9 6.6 %copy-start.9 = (bf16[1,256,1152]{2,1,0:T(8,128)(2,1)S(1)}, bf16[1,256,1152]{2,1,0:T(8,128)(2,1)}, u32[]{:S(2)}) copy-start(bf16[1,256,1152]{2,1,0:T(8,128)(2,1)} %param.34) | copy-start | bytes 1769476
  200.9 8.7 %slice-start.1 = ((s8[4718592]{0:T(1024)(128)(4,1)}), s8[524288]{0:T(1024)(128)(4,1)S(1)}, s32[]{:S(2)}) async-start(s8[4718592]{0:T(1024)(128)(4,1)} %bitcast.103), calls=%async_computation.1 | async-start | bytes 1048576
  214.8 84.8 %copy-start.64 = (bf16[1024,1152]{1,0:T(8,128)(2,1)S(1)}, bf16[1024,1152]{1,0:T(8,128)(2,1)}, u32[]{:S(2)}) copy-start(bf16[1024,1152]{1,0:T(8,128)(2,1)} %copy-done.63) | copy-start | bytes 7077892
  299.5 5.8 %copy-start.21 = (bf16[144,4608]{1,0:T(8,128)(2,1)}, bf16[144,4608]{1,0:T(8,128)(2,1)S(1)}, u32[]{:S(2)}) copy-start(bf16[144,4608]{1,0:T(8,128)(2,1)S(1)} %get-tuple-element.93) | copy-start | bytes 3981316
  299.5 5.8 %copy-start.15 = (bf16[8,144,1152]{2,1,0:T(8,128)(2,1)S(1)}, bf16[8,144,1152]{2,1,0:T(8,128)(2,1)}, u32[]{:S(2)}) copy-start(bf16[8,144,1152]{2,1,0:T(8,128)(2,1)} %copy-done.13) | copy-start | bytes 7962628
  299.5 5.8 %copy-start.68 = (bf16[1024,864]{1,0:T(8,128)(2,1)S(1)}, bf16[1024,864]{1,0:T(8,128)(2,1)}, u32[]{:S(2)}) copy-start(bf16[1024,864]{1,0:T(8,128)(2,1)} %get-tuple-element.81) | copy-start | bytes 5308420
  305.4 4.1 copy-start.52
  313.1 4.2 copy-start.69
  313.2 4.8 copy-start.77
  318.2 6.5 %copy-start.1 = (bf16[1152,864]{1,0:T(8,128)(2,1)S(1)}, bf16[1152,864]{1,0:T(8,128)(2,1)}, u32[]{:S(2)}) copy-start(bf16[1152,864]{1,0:T(8,128)(2,1)} %copy.82.refs_6_.refs_8_) | copy-start | bytes 5971972
  415.9 12.6 %copy-start.27 = (bf16[144,3456]{1,0:T(8,128)(2,1)S(1)}, bf16[144,3456]{1,0:T(8,128)(2,1)}, u32[]{:S(2)}) copy-start(bf16[144,3456]{1,0:T(8,128)(2,1)} %copy-done.26) | copy-start | bytes 2985988
  418.3 34.1 %copy-start.79 = (f32[2304]{0:T(1024)}, f32[2304]{0:T(1024)S(1)}, u32[]{:S(2)}) copy-start(f32[2304]{0:T(1024)S(1)} %get-tuple-element.224) | copy-start | bytes 27652
  420.0 33.0 %copy-start.75 = (f32[32,1152]{1,0:T(8,128)}, f32[32,1152]{1,0:T(8,128)S(1)}, u32[]{:S(2)}) copy-start(f32[32,1152]{1,0:T(8,128)S(1)} %get-tuple-element.216) | copy-start | bytes 442372
  420.0 10.8 %copy-start.22 = (bf16[144,4608]{1,0:T(8,128)(2,1)S(1)}, bf16[144,4608]{1,0:T(8,128)(2,1)}, u32[]{:S(2)}) copy-start(bf16[144,4608]{1,0:T(8,128)(2,1)} %copy-done.21) | copy-start | bytes 3981316
  424.0 35.3 %copy-start.55 = (f32[144,1152]{1,0:T(8,128)}, f32[144,1152]{1,0:T(8,128)S(1)}, u32[]{:S(2)}) copy-start(f32[144,1152]{1,0:T(8,128)S(1)} %get-tuple-element.217) | copy-start | bytes 1990660
  433.5 18.8 %copy-start.78 = (f32[2304]{0:T(1024)S(1)}, f32[2304]{0:T(1024)}, u32[]{:S(2)}) copy-start(f32[2304]{0:T(1024)} %param.43) | copy-start | bytes 27652
  433.5 18.8 %copy-start.80 = (f32[2304]{0:T(1024)S(1)}, f32[2304]{0:T(1024)}, u32[]{:S(2)}) copy-start(f32[2304]{0:T(1024)} %param.52) | copy-start | bytes 27652
  433.5 18.8 %copy-start.81 = (f32[2304]{0:T(1024)S(1)}, f32[2304]{0:T(1024)}, u32[]{:S(2)}) copy-start(f32[2304]{0:T(1024)} %param.61) | copy-start | bytes 27652
  433.6 19.5 %copy-start.74 = (f32[32,1152]{1,0:T(8,128)S(1)}, f32[32,1152]{1,0:T(8,128)}, u32[]{:S(2)}) copy-start(f32[32,1152]{1,0:T(8,128)} %param.35) | copy-start | bytes 442372
  433.6 21.3 %copy-start.61 = (f32[1000,144]{0,1:T(8,128)S(1)}, f32[1000,144]{0,1:T(8,128)}, u32[]{:S(2)}) copy-start(f32[1000,144]{0,1:T(8,128)} %param.37) | copy-start | bytes 1728004
  433.6 21.3 %copy-start.62 = (f32[1000,144]{0,1:T(8,128)S(1)}, f32[1000,144]{0,1:T(8,128)}, u32[]{:S(2)}) copy-start(f32[1000,144]{0,1:T(8,128)} %get-tuple-element.218) | copy-start | bytes 1728004
  437.9 19.8 %copy-start.17 = (f32[144,1152]{1,0:T(8,128)S(1)}, f32[144,1152]{1,0:T(8,128)}, u32[]{:S(2)}) copy-start(f32[144,1152]{1,0:T(8,128)} %out_ref.1) | copy-start | bytes 1990660
  437.9 19.8 %copy-start.56 = (f32[144,1152]{1,0:T(8,128)S(1)}, f32[144,1152]{1,0:T(8,128)}, u32[]{:S(2)}) copy-start(f32[144,1152]{1,0:T(8,128)} %get-tuple-element.221) | copy-start | bytes 1990660
  452.4 5.4 %copy-start.70 = (f32[144,1152]{1,0:T(8,128)S(1)}, f32[144,1152]{1,0:T(8,128)}, u32[]{:S(2)}) copy-start(f32[144,1152]{1,0:T(8,128)} %param.49) | copy-start | bytes 1990660
  452.4 5.4 %copy-start.71 = (f32[144,1152]{1,0:T(8,128)S(1)}, f32[144,1152]{1,0:T(8,128)}, u32[]{:S(2)}) copy-start(f32[144,1152]{1,0:T(8,128)} %param.58) | copy-start | bytes 1990660
  454.8 4.5 copy-start.73
  457.7 4.0 copy-start.67
  459.3 3.6 copy-start.51
  463.0 3.8 copy-start.3
  463.0 4.7 copy-start.50
  463.0 5.5 %copy-start.59 = (f32[144,4608]{1,0:T(8,128)S(1)}, f32[144,4608]{1,0:T(8,128)}, u32[]{:S(2)}) copy-start(f32[144,4608]{1,0:T(8,128)} %param.50) | copy-start | bytes 7962628
  463.0 6.3 %copy-start.60 = (f32[144,4608]{1,0:T(8,128)S(1)}, f32[144,4608]{1,0:T(8,128)}, u32[]{:S(2)}) copy-start(f32[144,4608]{1,0:T(8,128)} %param.59) | copy-start | bytes 7962628
  469.2 4.7 copy-start.53
  474.0 9.5 %copy-start.46 = (f32[1152,864]{0,1:T(8,128)S(1)}, f32[1152,864]{0,1:T(8,128)}, u32[]{:S(2)}) copy-start(f32[1152,864]{0,1:T(8,128)} %param.38) | copy-start | bytes 11943940
  474.0 9.5 %copy-start.47 = (f32[1152,864]{0,1:T(8,128)S(1)}, f32[1152,864]{0,1:T(8,128)}, u32[]{:S(2)}) copy-start(f32[1152,864]{0,1:T(8,128)} %get-tuple-element.219) | copy-start | bytes 11943940
  474.0 10.1 %copy-start.54 = (f32[1152,864]{0,1:T(8,128)S(1)}, f32[1152,864]{0,1:T(8,128)}, u32[]{:S(2)}) copy-start(f32[1152,864]{0,1:T(8,128)} %param.47) | copy-start | bytes 11943940
  484.1 7.4 %copy-start.25 = (f32[256,1152]{1,0:T(8,128)S(1)}, f32[256,1152]{1,0:T(8,128)}, u32[]{:S(2)}) copy-start(f32[256,1152]{1,0:T(8,128)} %copy-done.24) | copy-start | bytes 3538948
  (38 other events, 59.5 us)

commit v5 on v4

--- a/solution.py
+++ b/solution.py
@@ -272,8 +272,8 @@
     sends = Sends()
     loads = {}
     for to in (3, 0, 2, 1):
-        sends.start(remote(parts.at[to * 2 + 1 - y], mail.at[to], y_sent.at[to], y_landed.at[to], fsdp=mate))
-        loads[to] = pltpu.make_async_copy(parts.at[to * 2 + y], own.at[to], own_sem.at[to])
+        sends.start(remote(parts(to * 2 + 1 - y), mail.at[to], y_sent.at[to], y_landed.at[to], fsdp=mate))
+        loads[to] = pltpu.make_async_copy(parts(to * 2 + y), own.at[to], own_sem.at[to])
         loads[to].start()
         yield
     for to, up in ((3, True), (0, False), (2, True), (1, False), (1, True), (2, False)):
@@ -393,9 +393,9 @@
     hid_in[owner] = send_cut[0, owner]
     swap_start(sends, lambda to: send_cut.at[0, to], hid_in, *sems[2:4])
     yield
-    classes = lax.broadcasted_iota(jnp.int32, (8, table.shape[0]), 1).astype(F32)
+    classes = lax.broadcasted_iota(jnp.int32, (8, table.shape[1]), 1).astype(F32)
     onehot = (label == classes).astype(F32).astype(LOW)
-    from_class = low_dot(onehot, table[...], (1, 0))
+    from_class = low_dot(onehot, table[...], (1, 1))
     swap_wait(hid_in, sems[3])
     hidden_cut = bias_cut[0, owner] + jnp.zeros((8, cut), F32)
     for of in range(8):
@@ -421,7 +421,7 @@
     for of in range(8):
         cond_out[:, of * cut : (of + 1) * cut] = cond_cut[of]
     cond_act = silu_parts(cond_out[...])[0].astype(LOW)
-    values = low_dot(cond_act, modulation[...], (1, 0))
+    values = low_dot(cond_act, modulation[...], (1, 1))
     for to in range(8):
         mod_cut[to] = values[to : to + 1]
     mod[owner] = mod_cut[owner]
@@ -436,7 +436,7 @@
     rank_news, owner_news, d_cut, d_in, d_cond_cut = scratch
     owner, rank, *_ = places()
     cut = second.shape[0]
-    wide = modulation.shape[1]
+    wide = modulation.shape[0]
     sends = Sends()
     for step in range(1, 4):
         to = lax.rem(rank + step, 4)
@@ -453,7 +453,7 @@
     yield
     swap_wait(by_latent, sems[3])
     d_mod = stack_rows(by_latent)[:, :wide]
-    part = fine_dot(d_mod, modulation[...], (1, 1))
+    part = fine_dot(d_mod, modulation[...], (1, 0))
     for to in range(8):
         d_cut[to] = part[:, to * cut : (to + 1) * cut]
     d_in[owner] = d_cut[owner]
@@ -509,7 +509,7 @@
 
 def forward_first(w_io, tokens, note, first, second, table, modulation):
     rows, width = second.shape
-    wide = modulation.shape[1]
+    wide = modulation.shape[0]
 
     def kernel(*refs):
         args, outs, scratch, cond_sems, io_sems, token_sems = takes(refs, 7, 8, 5, 10, 3, 3)
@@ -749,6 +749,44 @@
     )
 
 
+def columns_product(left, right, out, first=0):
+    count = left.shape[1] // 128
+
+    def one(index, carry):
+        at = pl.ds(pl.multiple_of(lax.rem(index + first, count) * 128, 128), 128)
+        out[at] = low_dot(left[:, at], right[...], (0, 0)).astype(LOW)
+        return carry
+
+    lax.fori_loop(0, count, one, 0)
+
+
+def sum_feed(part, pairs):
+    many = len(pairs)
+
+    def kernel(*refs):
+        args, outs, scratch = takes(refs, 1 + 2 * many, 1 + many, 7)
+        greet(False, True)
+
+        def products():
+            for at in range(many):
+                columns_product(args[1 + 2 * at], args[2 + 2 * at], outs[1 + at])
+                yield
+
+        run_all([scatter_ranks(args[0], outs[0], *scratch[:4], scratch[4:]), products()])
+
+    return call(
+        kernel,
+        4,
+        (part,) + tuple(array for pair in pairs for array in pair),
+        [HBM] + [VMEM] * (2 * many),
+        [shape(part.shape[1:], F32)] + [shape((left.shape[1], right.shape[1]), LOW) for left, right in pairs],
+        [VMEM] * (1 + many),
+        scatter_ranks_scratch(*part.shape[1:]),
+        "sum_feed",
+        36,
+    )
+
+
 def row_cuts(rows, cuts):
     step = (rows // cuts + 15) // 16 * 16
     return [(start, min(step, rows - start)) for start in range(0, rows, step)]
@@ -772,19 +810,25 @@
 def scatter_items(parts, outs, scratch, cuts):
     items, at = [], 0
     for part, out in zip(parts, outs):
-        for start, count in row_cuts(part.shape[1], cuts):
-            rows = pl.ds(start, count)
+        height = out.shape[1]
+        for start, count in row_cuts(height, cuts):
             refs = scratch[at]
-            items.append(scatter_owners(part.at[:, rows], out.at[:, rows], *refs[:5], refs[5:]))
+
+            def block(owner, part=part, start=start, count=count):
+                if len(part.shape) == 3:
+                    return part.at[owner, pl.ds(start, count)]
+                return part.at[pl.ds(pl.multiple_of(owner * height + start, 16), count)]
+
+            items.append(scatter_owners(block, out.at[:, pl.ds(start, count)], *refs[:5], refs[5:]))
             at += 1
     return [together(items, 4)]
 
 
-def scatter_items_scratch(blocks, cuts):
+def scatter_items_scratch(shapes, cuts):
     scratch = []
-    for block in blocks:
-        for _, count in row_cuts(block.shape[1], cuts):
-            scratch += scatter_owners_scratch(count, block.shape[2])
+    for height, columns in shapes:
+        for _, count in row_cuts(height, cuts):
+            scratch += scatter_owners_scratch(count, columns)
     return scratch
 
 
@@ -795,7 +839,7 @@
     rows, width = my_d_attn.shape
 
     def kernel(*refs):
-        groups = takes(refs, 7, 5, 6, 7, 3, *[14] * 6)
+        groups = takes(refs, 7, 6, 6, 7, 3, *[14] * 6)
         args, outs, scratch, sum_scratch, token_sems = groups[:5]
         d_mixed, head_rows, d_head, d_keys, d_values, up_all = scratch
         greet(True, True)
@@ -818,12 +862,14 @@
             + [attention(), scatter_ranks(args[3], outs[3], *sum_scratch[:4], sum_scratch[4:])]
         )
         owners = up_all.shape[2] // units
+        outs[5][...] = jnp.zeros_like(outs[5])
 
         def assemble(at):
             for part in range(4):
                 for owner in range(owners):
                     to = (owner * 4 + part) * units
                     outs[0][at, to : to + units] = up_all[part, at, owner * units : (owner + 1) * units]
+            add_squares(outs[0][at], outs[5])
 
         by_rows(up_all.shape[1], assemble)
 
@@ -838,8 +884,9 @@
             shape((4,) + my_d_attn.shape, LOW),
             shape(my_d_attn.shape, F32),
             shape(qkv.shape, LOW),
+            shape((1, 4 * g_up.shape[2]), F32),
         ],
-        [VMEM, HBM, VMEM, VMEM, VMEM],
+        [VMEM, HBM, VMEM, VMEM, VMEM, VMEM],
         [
             pltpu.VMEM((length, span), LOW),
             pltpu.VMEM((3, length, HD), LOW),
@@ -850,21 +897,29 @@
         ]
         + scatter_ranks_scratch(rows, width)
         + GATHER_RANKS_SEMS
-        + scatter_items_scratch([g_up, g_down], 3),
+        + scatter_items_scratch([g_up.shape[1:], g_down.shape[1:]], 3),
         "backward_attention",
         50,
     )
 
 
-def backward_last(g_in, g_out, d_tokens, tokens, scale, d_middle, news, second, modulation, cond_cut, time_slope):
+def add_squares(values, box):
+    values = values.astype(F32)
+    box[...] += jnp.sum(values * values, axis=0, keepdims=True)
+
+
+def backward_last(h_attn, d_qkv, mixed, d_part, d_tokens, tokens, scale, d_middle, news, second, modulation, cond_cut, time_slope):
     rows, width = second.shape
-    span = g_out.shape[2]
+    span = d_part.shape[1]
     tok_rows = tokens.shape[0]
-    wide = modulation.shape[1]
+    wide = modulation.shape[0]
 
     def kernel(*refs):
-        groups = takes(refs, 11, 7, 5, 12, 7, 5, *[14] * 4)
-        args, outs, scratch, sems, sum_scratch, (in_all, out_all, d_sum, edge, news_here) = groups[:6]
+        groups = takes(refs, 13, 9, 5, 12, 7, 7, *[14] * 4)
+        args, outs, scratch, sems, sum_scratch = groups[:5]
+        in_all, out_all, d_sum, edge, news_here, g_in, g_out = groups[5]
+        squares, outs = outs[7:], outs[:7]
+        products, args = args[:4], args[2:]
         greet(True, True)
 
         def condition():
@@ -891,7 +946,15 @@
                 at += 1
             yield from condition_backward(news_here, *args[7:], outs[3:], scratch, sems)
 
-        run_all([condition()] + scatter_items(args[:2], (in_all, out_all), groups[6:], 2))
+        def gradients():
+            columns_product(products[2], products[3], g_out, 5)
+            yield
+            columns_product(products[0], products[1], g_in, 5)
+            yield from scatter_items((g_in, g_out), (in_all, out_all), groups[6:], 2)[0]
+
+        run_all([condition(), gradients()])
+        for box in squares:
+            box[...] = jnp.zeros_like(box)
 
         def assemble(at):
             for part in range(4):
@@ -899,14 +962,16 @@
                     to = (block * 4 + part) * span
                     outs[0][at, to : to + span] = in_all[part, at, block * span : (block + 1) * span]
                 outs[1][at, part * span : (part + 1) * span] = out_all[part, at]
+            add_squares(outs[0][at], squares[0])
+            add_squares(outs[1][at], squares[1])
 
         by_rows(rows, assemble)
 
     return call(
         kernel,
         8,
-        (g_in, g_out, d_tokens, tokens, scale, d_middle, news, second, modulation, cond_cut, time_slope),
-        [HBM] * 3 + [VMEM] * 8,
+        (h_attn, d_qkv, mixed, d_part, d_tokens, tokens, scale, d_middle, news, second, modulation, cond_cut, time_slope),
+        [VMEM] * 4 + [HBM] + [VMEM] * 8,
         [
             shape((rows, 12 * span), LOW),
             shape((rows, 4 * span), LOW),
@@ -915,8 +980,10 @@
             shape((8, width), F32),
             shape((8, 8, rows), F32),
             shape((8, 1, wide), F32),
+            shape((1, 12 * span), F32),
+            shape((1, 4 * span), F32),
         ],
-        [VMEM] * 7,
+        [VMEM] * 9,
         [
             pltpu.VMEM((4,) + news.shape, F32),
             pltpu.VMEM(news.shape, F32),
@@ -929,15 +996,17 @@
         + SWAP_SEMS * 5
         + scatter_ranks_scratch(tok_rows, width)
         + [
-            pltpu.VMEM((4,) + g_in.shape[1:], LOW),
-            pltpu.VMEM((4,) + g_out.shape[1:], LOW),
+            pltpu.VMEM((4, rows, 3 * span), LOW),
+            pltpu.VMEM((4, rows, span), LOW),
             pltpu.VMEM((tok_rows, width), F32),
             pltpu.VMEM((2, 8, width), F32),
             pltpu.VMEM(news.shape, F32),
+            pltpu.VMEM((width, 3 * span), LOW),
+            pltpu.VMEM((width, span), LOW),
         ]
-        + scatter_items_scratch([g_in, g_out], 2),
+        + scatter_items_scratch([(rows, 3 * span), (rows, span)], 2),
         "backward_last",
-        36,
+        52,
     )
 
 
@@ -1074,7 +1143,7 @@
             axis=1,
         )[:, None]
         w_io_all, tokens, notes, act, slope, cond_cut, cond, mod = forward_first(
-            w_io, latent_tokens, note, first, second, table, modulation_low
+            w_io, latent_tokens, note, first, second, table.T, modulation_low.T
         )
         notes = notes[:, 0]
         all_bias = notes[:, :share].reshape(owners * share)
@@ -1109,7 +1178,7 @@
     return [lax.all_gather(block.astype(LOW), "seq", axis=0) for block in summed]
 
 
-def condition_end(state, g_in, g_out, d_tokens, tokens, scale1, d_middle, d_mod_rest, tail, share):
+def condition_end(state, h_attn, d_qkv, mixed, d_part, d_tokens, tokens, scale1, d_middle, d_mod_rest, tail, share):
     first, second, modulation_low, my_features, all_labels, act, slope, cond_cut, cond = state
     owners, owner, rank = lax.axis_size("fsdp"), lax.axis_index("fsdp"), lax.axis_index("seq")
     wide, width = modulation_low.shape[1], cond.shape[1]
@@ -1120,8 +1189,8 @@
         news = jnp.concatenate(
             [jnp.concatenate([blank, d_mod_rest]).reshape(owners, wide), jnp.zeros((owners, pad), F32), tails], axis=1
         )[:, None]
-        grad_in, grad_out, input_gradient, by_latent, d_cond, d_hid, sums = backward_last(
-            g_in, g_out, d_tokens, tokens, scale1, d_middle, news, second, modulation_low, cond_cut, slope
+        grad_in, grad_out, input_gradient, by_latent, d_cond, d_hid, sums, *squares = backward_last(
+            h_attn, d_qkv, mixed, d_part, d_tokens, tokens, scale1, d_middle, news, second, modulation_low.T, cond_cut, slope
         )
         d_mod = by_latent[:, 0, :wide]
         my_tail = jnp.sum(by_latent[:, 0, wide + pad :], axis=0)
@@ -1136,10 +1205,14 @@
         norm, inverse = layer_norm(tokens.astype(F32))
         input_gradient = d_middle + layer_norm_back(norm, inverse, d_hattn * (1.0 + scale1))
         my_d_mod = jnp.concatenate([jnp.sum(d_hattn, axis=0), jnp.sum(d_hattn * norm, axis=0), d_mod_rest])
-        grad_in, grad_out = owner_sums([g_in, g_out])
+        by_owner = lambda block: block.astype(LOW).reshape((owners, -1) + block.shape[1:])
+        grad_in, grad_out = owner_sums(
+            [by_owner(mixed_dot("td,te->de", h_attn, d_qkv)), by_owner(mixed_dot("td,te->de", mixed, d_part))]
+        )
         rows, span = grad_out.shape[1], grad_out.shape[2]
         grad_in = grad_in.reshape(4, rows, 3, span).transpose(1, 2, 0, 3).reshape(rows, 12 * span)
         grad_out = grad_out.transpose(1, 0, 2).reshape(rows, 4 * span)
+        squares = [grad.astype(F32) * grad.astype(F32) for grad in (grad_in, grad_out)]
         all_d_mod = lax.all_gather(lax.psum(my_d_mod, "seq"), "fsdp", axis=0)
         d_mod = mine(all_d_mod, 1, owners, owner)
         part = high_dot(d_mod, modulation_low.astype(F32).T)
@@ -1158,7 +1231,7 @@
     grad_second = high_dot(act.T, d_cond)
     grad_first = high_dot(my_features.T, d_hidden)
     condition_gradient = lax.dynamic_slice_in_dim(d_cond, owner, 1, 0)
-    return grad_in, grad_out, input_gradient, (grad_first, grad_second, grad_class, grad_mod), grad_bias, condition_gradient
+    return grad_in, grad_out, squares, input_gradient, (grad_first, grad_second, grad_class, grad_mod), grad_bias, condition_gradient
 
 
 def per_device(latents, timesteps, labels, upstream, *state):
@@ -1228,9 +1301,13 @@
     d_act = mixed_dot("td,fd->tf", d_mlp, w_down)
     d_pre = gelu_pull(d_act)[0].astype(LOW)
     d_hmlp_part = mixed_dot("tf,df->td", d_pre, w_up).astype(LOW).reshape(by_rank)
-    (d_hmlp,) = rank_sums(4, [d_hmlp_part], "sum_feed")
-    g_down = by_owner(mixed_dot("tf,td->fd", act, d_mlp))
-    g_up = by_owner(mixed_dot("td,tf->df", h_mlp, d_pre))
+    if fast():
+        d_hmlp, g_down, g_up = sum_feed(d_hmlp_part, [(act, d_mlp), (h_mlp, d_pre)])
+        g_down, g_up = by_owner(g_down), by_owner(g_up)
+    else:
+        (d_hmlp,) = rank_sums(4, [d_hmlp_part], "sums")
+        g_down = by_owner(mixed_dot("tf,td->fd", act, d_mlp))
+        g_up = by_owner(mixed_dot("td,tf->df", h_mlp, d_pre))
     gb_up = jnp.sum(d_pre.astype(F32), axis=0)
     gb_down = jnp.sum(d_mlp.astype(F32), axis=0)
 
@@ -1243,7 +1320,7 @@
     d_gate1 = jnp.sum(d_middle * my_attn_out, axis=0)
     my_d_attn = (d_middle * gate1).astype(LOW)
     if fast():
-        grad_up, grad_down, d_attn, mlp_sum, d_qkv = backward_attention(
+        grad_up, grad_down, d_attn, mlp_sum, d_qkv, up_squares = backward_attention(
             g_up, g_down, my_d_attn, mlp_part, qkv, w_out, logs, unit
         )
         d_attn = d_attn.reshape(length, width)
@@ -1255,11 +1332,11 @@
         d_qkv = attend_back(query, keys, values, d_mixed.reshape(head_shape), logs)
         grad_up, grad_down = owner_sums([g_up, g_down])
         grad_up = grad_up.reshape(ranks, rows, owners, unit).transpose(1, 2, 0, 3).reshape(rows, hidden)
+        up_squares = grad_up.astype(F32) * grad_up.astype(F32)
     mlp_out = mlp_sum + b_down
     output = (my_middle + gate2 * mlp_out).astype(LOW)
     d_gate2 = jnp.sum(my_d_out * mlp_out, axis=0)
-    g_in = by_owner(mixed_dot("td,te->de", h_attn, d_qkv))
-    g_out = by_owner(mixed_dot("td,te->de", mixed, mine(d_attn, 1, ranks, rank)))
+    d_part = mine(d_attn, 1, ranks, rank)
     d_hattn_part = mixed_dot("te,de->td", d_qkv, w_in).astype(LOW).reshape(by_rank)
     d_mod_rest = jnp.concatenate([d_gate1, d_shift2, d_scale2, d_gate2])
     gb_qv = jnp.sum(d_qkv.astype(F32), axis=0)
@@ -1276,13 +1353,14 @@
             jnp.where(rank == 0, gb_down, 0.0),
         ]
     )
-    grad_in, grad_out, input_gradient, small_grads, grad_bias, condition_gradient = condition_end(
-        kept, g_in, g_out, d_hattn_part, latents[0], scale1, d_middle, d_mod_rest, gb_tail, biases.shape[0]
+    grad_in, grad_out, squares_io, input_gradient, small_grads, grad_bias, condition_gradient = condition_end(
+        kept, h_attn, d_qkv, mixed, d_part, d_hattn_part, latents[0], scale1, d_middle, d_mod_rest, gb_tail, biases.shape[0]
     )
     grad_in, grad_out, grad_up, grad_down = [grad.astype(F32) for grad in (grad_in, grad_out, grad_up, grad_down)]
     grad_down = grad_down.reshape(contract.shape)
     gradients = small_grads + (grad_in, grad_out, grad_up, grad_down, grad_bias)
-    local_sum = sum(jnp.sum(gradient * gradient) for gradient in gradients)
+    local_sum = sum(jnp.sum(gradient * gradient) for gradient in small_grads + (grad_down, grad_bias))
+    local_sum = local_sum + sum(jnp.sum(box) for box in [up_squares] + list(squares_io))
     norm_before = jnp.sqrt(sum_owners(7, local_sum, "sum_squares"))
     factor = clip_limit / jnp.maximum(norm_before, clip_limit)
     results = [

time: 504 us -> 481 us (0.954)
  local copies, waits for them, and re-layouts: 50.2 us -> 28.3 us
  matrix products: 62.4 us -> 43.2 us
  Pallas kernels: 309 us -> 326 us
    dot_general x11 -> x7, matrix products: 52.4 us -> 34 us  [mixed_dot(): return jnp.einsum(form, left, right, preferred_element_type=jnp.float32)]
    pallas_call x6, Pallas kernels: 308 us -> 325 us  [call(): pl.pallas_call(kernel, out_shape=outs, in_specs=in_specs, out_specs=out_s...]
    unnamed x186 -> x133, local copies, waits for them, and re-layouts: 37 us -> 20.1 us
    convert_element_type x3 -> x0, local copies, waits for them, and re-layouts: 6.73 us -> none  [the longest x2 6.53 us: per_device(): block.astype(LOW).reshape((owners, -1) + block.shape[1:])]
    reduce_sum x5, other arithmetic: 9.43 us -> 3.76 us  [the longest x2 1.89 us: per_device(): jnp.sum(gradient * gradient)]
where the time goes in v5:
time: 481 us; the launch traced here: 472 us
  Pallas kernels  326 us (68%)
  other arithmetic  62.8 us (13%)
  matrix products  43.2 us (9%)
  local copies, waits for them, and re-layouts  28.3 us (6%)
  between operations  11.3 us (2%)
    pallas_call x6, Pallas kernels, call(): pl.pallas_call(kernel, out_shape=outs, in_specs=in_specs, out_specs=out_s...  325 us
    sub x9, other arithmetic, adam_step(): weight - learn_rate * (moment_hat / (jnp.sqrt(square_hat) + adam_eps) + w...  35.1 us
    dot_general x7, matrix products, mixed_dot(): return jnp.einsum(form, left, right, preferred_element_type=jnp.float32)  34 us
    unnamed x133, local copies, waits for them, and re-layouts  20.1 us

profile of v5, /device:TPU:0, one launch (start us, length us, event | category | flops | bytes accessed | tf_op | source)
XLA Modules:
  0.0 471.6 jit_solution(2941288260839610666)
XLA Ops:
  3.8 1.0 convert_element_type.140.refs_3_
  5.4 1.1 convert_bitcast_fusion.1.refs_5_
  6.5 1.9 dynamic-slice_convert_fusion.refs_2_
  8.4 1.1 convert_element_type.141.refs_4_.refs_9_
  9.5 1.5 copy-done.4
  12.0 1.3 copy-done.28
  14.4 44.9 %forward_first.1 = (bf16[8,144,1152]{2,1,0:T(8,128)(2,1)S(1)}, bf16[4,256,1152]{2,1,0:T(8,128)(2,1)S(1)}, f32[8,1,2432]{2,1,0:T(1,128)S(1)}, f32[8,144]{1,0:T(8,...) custom-call(bf16[144,1152]{1,0:T(8,128)(2,1)S(1)} %get-tuple-element, ...), custom_call_target="tpu_custom_call" | custom-call | tf_op jit(solution)/shard_map/forward_first/pallas_call | solution.py:493
  59.3 1.3 copy-done
  60.5 1.5 copy-done.8
  66.6 2.8 add_convert_fusion.1.refs_0_.refs_4_
  69.5 71.8 %forward_attention.1 = (bf16[8,144,1152]{2,1,0:T(8,128)(2,1)S(1)}, bf16[8,144,1152]{2,1,0:T(8,128)(2,1)S(1)}, bf16[4,256,1152]{2,1,0:T(8,128)(2,1)S(1)}, bf16[11...) custom-call(bf16[1024,864]{1,0:T(8,128)(2,1)S(1)} %add_convert_fusion.1.refs_0_.refs_4_, ...), custom_call_target="tpu_custom_call" | custom-call | tf_op jit(solution)/shard_map/forward_attention/pallas_call | solution.py:493
  141.3 2.2 fusion.7.refs_2_
  144.2 3.5 fusion.56
  147.7 5.3 %fusion.53 = (f32[1024]{0:T(1024)S(1)}, f32[1024,1152]{1,0:T(8,128)S(1)}, f32[1024,1152]{1,0:T(8,128)}) fusion(f32[1152]{0:T(1024)S(1)} %get-tuple-element.169, bf16[4,256,1152]{2,1,0:T(8,128)(2,1)S(1)} %get-tuple-element.75, f32[1152]{0:T(1024)S(1)} %get-tuple-element.160, bf16[1024,1152]{1,0:T(8,128)(2,1)S(1)} %get-tuple-element.80.refs_2_, ...), kind=kOutput, calls=%fused_computation.146 | convolution fusion | flops 2723806208 | bytes 16823296 | tf_op jit(solution)/shard_map/td,de->te/dot_general | solution.py:69
  153.8 3.1 add_convert_fusion
  156.9 6.5 %convert_reduce_fusion.2 = (f32[1152]{0:T(1024)S(1)}, bf16[1024,1152]{1,0:T(8,128)(2,1)S(1)}, bf16[1024,1152]{1,0:T(8,128)(2,1)S(1)}) fusion(f32[1024,1152]{1,0:T(8,128)S(1)} %fusion.56, f32[1152]{0:T(1024)S(1)} %add.305, bf16[1024,1152]{1,0:T(8,128)(2,1)S(1)} %get-tuple-element.152.refs_3_, bf16[1152,1152]{1,0:T(8,128)(2,1)S(1)} %bitcast.85), kind=kOutput, calls=%fused_computation.23 | convolution fusion | flops 2747399168 | bytes 14459904 | tf_op jit(solution)/shard_map/td,df->tf/dot_general | solution.py:69
  163.4 4.8 %convolution_convert_fusion.1 = bf16[1024,1152]{1,0:T(8,128)(2,1)} fusion(bf16[1024,1152]{1,0:T(8,128)(2,1)S(1)} %get-tuple-element.156.refs_1_, bf16[1152,1152]{1,0:T(8,128)(2,1)S(1)} %bitcast.88), kind=kOutput, calls=%fused_computation.38 | convolution fusion | flops 2719088640 | bytes 7372800 | tf_op jit(solution)/shard_map/tf,fd->td/dot_general | solution.py:69
  168.2 4.8 %convolution_convert_fusion.2 = bf16[1024,1152]{1,0:T(8,128)(2,1)} fusion(bf16[1024,1152]{1,0:T(8,128)(2,1)S(1)} %get-tuple-element.148.refs_4_, bf16[1152,1152]{1,0:T(8,128)(2,1)S(1)} %bitcast.86), kind=kOutput, calls=%fused_computation.39 | convolution fusion | flops 2719088640 | bytes 7372800 | tf_op jit(solution)/shard_map/tf,df->td/dot_general | solution.py:69
  173.3 1.7 copy-done.3
  174.9 1.7 copy-done.19
  176.6 1.7 copy-done.21
  178.3 1.7 copy-done.22
  179.9 21.8 %sum_feed.1 = (f32[256,1152]{1,0:T(8,128)S(1)}, bf16[1152,1152]{1,0:T(8,128)(2,1)S(1)}, bf16[1152,1152]{1,0:T(8,128)(2,1)S(1)}) custom-call(bf16[4,256,1152]{2,1,0:T(8,128)(2,1)S(1)} %bitcast.83, bf16[1024,1152]{1,0:T(8,128)(2,1)S(1)} %copy-done.21, bf16[1024,1152]{1,0:T(8,128)(2,1)S(1)} %copy-done.3, bf16[1024,1152]{1,0:T(8,128)(2,1)S(1)} %get-tuple-element.152.refs_3_, ...), custom_call_target="tpu_custom_call" | custom-call | tf_op jit(solution)/shard_map/sum_feed/pallas_call | solution.py:493
  201.8 2.6 multiply_reduce_fusion.3
  204.4 1.7 convert_reduce_fusion.4
  206.2 1.8 multiply_reduce_fusion.4
  208.1 85.1 %backward_attention.1 = (bf16[144,4608]{1,0:T(8,128)(2,1)S(1)}, bf16[4,144,1152]{2,1,0:T(8,128)(2,1)}, bf16[4,256,1152]{2,1,0:T(8,128)(2,1)}, f32[256,1152]{1,0:...) custom-call(bf16[8,144,1152]{2,1,0:T(8,128)(2,1)} %bitcast.80, bf16[8,144,1152]{2,1,0:T(8,128)(2,1)} %bitcast.79, ...), custom_call_target="tpu_custom_call" | custom-call | tf_op jit(solution)/shard_map/backward_attention/pallas_call | solution.py:493
  293.2 6.2 %convolution_convert_fusion = bf16[1024,1152]{1,0:T(8,128)(2,1)} fusion(bf16[1024,864]{1,0:T(8,128)(2,1)} %get-tuple-element.90.refs_1_, bf16[1152,1152]{1,0:T(8,128)(2,1)S(1)} %bitcast.78), kind=kOutput, calls=%fused_computation.37 | convolution fusion | flops 2039611392 | bytes 6193152 | tf_op jit(solution)/shard_map/te,de->td/dot_general | solution.py:69
  299.4 1.3 multiply_reduce_fusion.2
  301.4 2.7 fusion.23
  304.2 2.5 constant_dynamic-slice_fusion.1.refs_3_
  306.7 1.8 convert_reduce_fusion.3
  309.1 94.6 %backward_last.1 = (bf16[144,3456]{1,0:T(8,128)(2,1)}, bf16[144,1152]{1,0:T(8,128)(2,1)S(1)}, f32[256,1152]{1,0:T(8,128)}, f32[8,1,3200]{2,1,0:T(1,128)S(1)}, f3...) custom-call(bf16[1024,1152]{1,0:T(8,128)(2,1)} %copy-done.32, ...), custom_call_target="tpu_custom_call" | custom-call | tf_op jit(solution)/shard_map/backward_last/pallas_call | solution.py:493
  408.6 1.6 multiply_reduce_fusion.9
  410.3 2.0 multiply_reduce_fusion.8
  412.3 1.4 multiply_reduce_fusion.7
  415.7 4.3 multiply_reduce_fusion.1
  422.0 6.8 %sum_squares.1 = f32[8,128]{1,0:T(8,128)S(1)} custom-call(f32[8,128]{1,0:T(8,128)S(1)} %broadcast_in_dim.65.src), custom_call_target="tpu_custom_call" | custom-call | tf_op jit(solution)/shard_map/sum_squares/pallas_call | solution.py:493
  430.8 1.8 multiply_subtract_fusion.7
  432.6 3.0 multiply_subtract_fusion.6
  435.6 2.9 multiply_subtract_fusion.5
  438.5 1.7 multiply_subtract_fusion.4
  441.8 4.5 multiply_subtract_fusion.3
  446.3 1.3 copy-done.36
  448.3 4.8 %multiply_subtract_fusion.1 = (f32[576,1152]{1,0:T(8,128)}, f32[576,1152]{1,0:T(8,128)}, f32[576,1152]{1,0:T(8,128)}, f32[576,1152]{1,0:T(8,128)}) fusion(f32[576,1152]{1,0:T(8,128)S(1)} %copy-done.35, f32[]{:T(128)S(6)} %div.165, f32[576,1152]{1,0:T(8,128)S(1)} %copy-done.36, f32[576,1152]{1,0:T(8,128)S(1)} %copy-done.37, ...), kind=kLoop, calls=%fused_computation.45 | loop fusion | flops 11280384 | bytes 19906564 | tf_op jit(solution)/shard_map/sub | solution.py:1120
  453.2 7.9 %multiply_subtract_fusion.2 = (f32[144,4608]{1,0:T(8,128)}, f32[144,4608]{1,0:T(8,128)}, f32[144,4608]{1,0:T(8,128)}, f32[144,4608]{1,0:T(8,128)}) fusion(f32[144,4608]{1,0:T(8,128)S(1)} %copy-done.2, f32[]{:T(128)S(6)} %div.165, f32[144,4608]{1,0:T(8,128)} %param.50, f32[144,4608]{1,0:T(8,128)} %param.59, bf16[144,4608]{1,0:T(8,128)(2,1)S(1)} %get-tuple-element.107), kind=kLoop, calls=%fused_computation.47 | loop fusion | flops 11280384 | bytes 19906564 | tf_op jit(solution)/shard_map/sub | solution.py:1120
  461.1 7.9 %multiply_subtract_fusion = (f32[1152,864]{0,1:T(8,128)}, f32[1152,864]{0,1:T(8,128)}, f32[1152,864]{0,1:T(8,128)}) fusion(f32[1152,864]{0,1:T(8,128)S(1)} %copy-done.29, f32[1152,864]{0,1:T(8,128)S(1)} %copy-done.30, f32[]{:T(128)S(6)} %div.165, f32[1152,864]{0,1:T(8,128)} %param.47, f32[1152,864]{0,1:T(8,128)} %param.56), kind=kLoop, calls=%fused_computation.34 | loop fusion | flops 15925248 | bytes 27869188 | tf_op jit(solution)/shard_map/sub | solution.py:1120
  469.0 1.0 copy.107
  (201 shorter events, 18.2 us)
Async XLA Ops:
  0.7 8.8 %copy-start.1 = (f32[144,4608]{1,0:T(8,128)S(1)}, f32[144,4608]{1,0:T(8,128)}, u32[]{:S(2)}) copy-start(f32[144,4608]{1,0:T(8,128)} %up_ref.1) | copy-start | bytes 7962628
  3.7 5.8 %copy-start.13 = (f32[144,1152]{1,0:T(8,128)S(1)}, f32[144,1152]{1,0:T(8,128)}, u32[]{:S(2)}) copy-start(f32[144,1152]{1,0:T(8,128)} %out_ref.1) | copy-start | bytes 1990660
  11.1 2.2 copy-start.28
  66.6 2.8 copy-start.32
  66.6 2.8 copy-start.7
  66.6 2.8 copy-start.23
  66.6 2.8 copy-start.26
  69.4 71.8 %copy-start.6 = (bf16[1024,864]{1,0:T(8,128)(2,1)}, bf16[1024,864]{1,0:T(8,128)(2,1)S(1)}, u32[]{:S(2)}) copy-start(bf16[1024,864]{1,0:T(8,128)(2,1)S(1)} %add_convert_fusion.1.refs_0_.refs_4_) | copy-start | bytes 5308420
  141.2 6.4 %copy-start.17 = (bf16[1024,1152]{1,0:T(8,128)(2,1)}, bf16[1024,1152]{1,0:T(8,128)(2,1)S(1)}, u32[]{:S(2)}) copy-start(bf16[1024,1152]{1,0:T(8,128)(2,1)S(1)} %get-tuple-element.80.refs_2_) | copy-start | bytes 7077892
  144.2 3.6 copy-start.39
  153.1 3.8 copy-start.27
  163.4 4.8 %copy-start.20 = (bf16[1024,1152]{1,0:T(8,128)(2,1)}, bf16[1024,1152]{1,0:T(8,128)(2,1)S(1)}, u32[]{:S(2)}) copy-start(bf16[1024,1152]{1,0:T(8,128)(2,1)S(1)} %get-tuple-element.156.refs_1_) | copy-start | bytes 7077892
  163.4 4.8 %copy-start.18 = (bf16[1024,1152]{1,0:T(8,128)(2,1)}, bf16[1024,1152]{1,0:T(8,128)(2,1)S(1)}, u32[]{:S(2)}) copy-start(bf16[1024,1152]{1,0:T(8,128)(2,1)S(1)} %get-tuple-element.148.refs_4_) | copy-start | bytes 7077892
  201.7 4.4 copy-start.11
  201.8 4.4 copy-start.12
  204.4 3.6 copy-start.56
  206.1 1.9 copy-start.31
  208.0 85.1 %copy-start.10 = (bf16[8,144,1152]{2,1,0:T(8,128)(2,1)S(1)}, bf16[8,144,1152]{2,1,0:T(8,128)(2,1)}, u32[]{:S(2)}) copy-start(bf16[8,144,1152]{2,1,0:T(8,128)(2,1)} %copy-done.8) | copy-start | bytes 7962628
  293.2 6.3 %copy-start.24 = (f32[256,1152]{1,0:T(8,128)}, f32[256,1152]{1,0:T(8,128)S(1)}, u32[]{:S(2)}) copy-start(f32[256,1152]{1,0:T(8,128)S(1)} %get-tuple-element.89) | copy-start | bytes 3538948
  293.2 6.2 %copy-start.33 = (bf16[4,144,1152]{2,1,0:T(8,128)(2,1)S(1)}, bf16[4,144,1152]{2,1,0:T(8,128)(2,1)}, u32[]{:S(2)}) copy-start(bf16[4,144,1152]{2,1,0:T(8,128)(2,1)} %get-tuple-element.100) | copy-start | bytes 3981316
  301.3 7.4 %copy-start.52 = (f32[18432]{0:T(1024)S(1)}, f32[18432]{0:T(1024)}, u32[]{:S(2)}) copy-start(f32[18432]{0:T(1024)} %broadcast_dynamic-update-slice_fusion) | copy-start | bytes 221188
  304.1 5.0 %copy-start.16 = (bf16[1,256,1152]{2,1,0:T(8,128)(2,1)S(1)}, bf16[1,256,1152]{2,1,0:T(8,128)(2,1)}, u32[]{:S(2)}) copy-start(bf16[1,256,1152]{2,1,0:T(8,128)(2,1)} %param.31) | copy-start | bytes 1769476
  309.1 101.2 %copy-start.59 = (f32[8]{0:T(128)S(1)}, f32[8]{0:T(128)}, u32[]{:S(2)}) copy-start(f32[8]{0:T(128)} %slice_reduce_fusion.1) | copy-start | bytes 100
  408.5 21.5 %copy-start.54 = (f32[2304]{0:T(1024)}, f32[2304]{0:T(1024)S(1)}, u32[]{:S(2)}) copy-start(f32[2304]{0:T(1024)S(1)} %get-tuple-element.235) | copy-start | bytes 27652
  410.3 20.5 %copy-start.50 = (f32[32,1152]{1,0:T(8,128)}, f32[32,1152]{1,0:T(8,128)S(1)}, u32[]{:S(2)}) copy-start(f32[32,1152]{1,0:T(8,128)S(1)} %get-tuple-element.227) | copy-start | bytes 442372
  410.3 19.8 %copy-start.53 = (f32[2304]{0:T(1024)S(1)}, f32[2304]{0:T(1024)}, u32[]{:S(2)}) copy-start(f32[2304]{0:T(1024)} %param.43) | copy-start | bytes 27652
  410.3 19.8 %copy-start.57 = (f32[2304]{0:T(1024)S(1)}, f32[2304]{0:T(1024)}, u32[]{:S(2)}) copy-start(f32[2304]{0:T(1024)} %param.52) | copy-start | bytes 27652
  410.3 19.8 %copy-start.58 = (f32[2304]{0:T(1024)S(1)}, f32[2304]{0:T(1024)}, u32[]{:S(2)}) copy-start(f32[2304]{0:T(1024)} %param.61) | copy-start | bytes 27652
  410.3 20.5 %copy-start.49 = (f32[32,1152]{1,0:T(8,128)S(1)}, f32[32,1152]{1,0:T(8,128)}, u32[]{:S(2)}) copy-start(f32[32,1152]{1,0:T(8,128)} %param.35) | copy-start | bytes 442372
  413.7 21.9 %copy-start.38 = (f32[144,1152]{1,0:T(8,128)}, f32[144,1152]{1,0:T(8,128)S(1)}, u32[]{:S(2)}) copy-start(f32[144,1152]{1,0:T(8,128)S(1)} %get-tuple-element.228) | copy-start | bytes 1990660
  413.7 18.9 %copy-start.40 = (f32[1000,144]{0,1:T(8,128)S(1)}, f32[1000,144]{0,1:T(8,128)}, u32[]{:S(2)}) copy-start(f32[1000,144]{0,1:T(8,128)} %param.37) | copy-start | bytes 1728004
  430.1 5.4 %copy-start.45 = (f32[144,1152]{1,0:T(8,128)S(1)}, f32[144,1152]{1,0:T(8,128)}, u32[]{:S(2)}) copy-start(f32[144,1152]{1,0:T(8,128)} %param.45) | copy-start | bytes 1990660
  430.1 5.4 %copy-start.46 = (f32[144,1152]{1,0:T(8,128)S(1)}, f32[144,1152]{1,0:T(8,128)}, u32[]{:S(2)}) copy-start(f32[144,1152]{1,0:T(8,128)} %param.54) | copy-start | bytes 1990660
  435.5 2.9 copy-start.14
  435.5 2.9 copy-start.47
  435.5 2.9 copy-start.48
  435.6 4.6 copy-start.42
  438.4 2.5 copy-start.5
  438.4 3.1 copy-start.41
  438.4 3.4 copy-start.44
  441.8 4.5 copy-start.34
  441.8 4.5 copy-start.35
  441.8 5.8 %copy-start.36 = (f32[576,1152]{1,0:T(8,128)S(1)}, f32[576,1152]{1,0:T(8,128)}, u32[]{:S(2)}) copy-start(f32[576,1152]{1,0:T(8,128)} %param.51) | copy-start | bytes 7962628
  441.8 6.5 %copy-start.37 = (f32[576,1152]{1,0:T(8,128)S(1)}, f32[576,1152]{1,0:T(8,128)}, u32[]{:S(2)}) copy-start(f32[576,1152]{1,0:T(8,128)} %param.60) | copy-start | bytes 7962628
  448.3 4.8 %copy-start.2 = (f32[144,4608]{1,0:T(8,128)S(1)}, f32[144,4608]{1,0:T(8,128)}, u32[]{:S(2)}) copy-start(f32[144,4608]{1,0:T(8,128)} %up_ref.1) | copy-start | bytes 7962628
  453.2 7.9 %copy-start.29 = (f32[1152,864]{0,1:T(8,128)S(1)}, f32[1152,864]{0,1:T(8,128)}, u32[]{:S(2)}) copy-start(f32[1152,864]{0,1:T(8,128)} %param.38) | copy-start | bytes 11943940
  453.2 7.9 %copy-start.30 = (f32[1152,864]{0,1:T(8,128)S(1)}, f32[1152,864]{0,1:T(8,128)}, u32[]{:S(2)}) copy-start(f32[1152,864]{0,1:T(8,128)} %get-tuple-element.230) | copy-start | bytes 11943940
  461.1 7.9 %copy-start.43 = (f32[256,1152]{1,0:T(8,128)S(1)}, f32[256,1152]{1,0:T(8,128)}, u32[]{:S(2)}) copy-start(f32[256,1152]{1,0:T(8,128)} %get-tuple-element.94) | copy-start | bytes 3538948
  (12 other events, 17.4 us)

commit v6 on v5

--- a/solution.py
+++ b/solution.py
@@ -915,7 +915,7 @@
     wide = modulation.shape[0]
 
     def kernel(*refs):
-        groups = takes(refs, 13, 9, 5, 12, 7, 7, *[14] * 4)
+        groups = takes(refs, 13, 9, 5, 12, 7, 7, *[14] * 6)
         args, outs, scratch, sems, sum_scratch = groups[:5]
         in_all, out_all, d_sum, edge, news_here, g_in, g_out = groups[5]
         squares, outs = outs[7:], outs[:7]
@@ -950,7 +950,7 @@
             columns_product(products[2], products[3], g_out, 5)
             yield
             columns_product(products[0], products[1], g_in, 5)
-            yield from scatter_items((g_in, g_out), (in_all, out_all), groups[6:], 2)[0]
+            yield from scatter_items((g_in, g_out), (in_all, out_all), groups[6:], 3)[0]
 
         run_all([condition(), gradients()])
         for box in squares:
@@ -1004,7 +1004,7 @@
             pltpu.VMEM((width, 3 * span), LOW),
             pltpu.VMEM((width, span), LOW),
         ]
-        + scatter_items_scratch([(rows, 3 * span), (rows, span)], 2),
+        + scatter_items_scratch([(rows, 3 * span), (rows, span)], 3),
         "backward_last",
         52,
     )

time: 481 us -> 480 us (level)
  no operation moved by 1% of the time
where the time goes in v6:
time: 480 us; the launch traced here: 471 us
  Pallas kernels  325 us (68%)
  other arithmetic  62.8 us (13%)
  matrix products  43.2 us (9%)
  local copies, waits for them, and re-layouts  28.3 us (6%)
  between operations  11.3 us (2%)
    pallas_call x6, Pallas kernels, call(): pl.pallas_call(kernel, out_shape=outs, in_specs=in_specs, out_specs=out_s...  324 us
    sub x9, other arithmetic, adam_step(): weight - learn_rate * (moment_hat / (jnp.sqrt(square_hat) + adam_eps) + w...  35.1 us
    dot_general x7, matrix products, mixed_dot(): return jnp.einsum(form, left, right, preferred_element_type=jnp.float32)  34 us
    unnamed x133, local copies, waits for them, and re-layouts  20.1 us

profile of v6, /device:TPU:0, one launch (start us, length us, event | category | flops | bytes accessed | tf_op | source)
XLA Modules:
  0.0 470.9 jit_solution(16090026490007599290)
XLA Ops:
  3.8 1.0 convert_element_type.140.refs_3_
  5.4 1.1 convert_bitcast_fusion.1.refs_5_
  6.5 1.9 dynamic-slice_convert_fusion.refs_2_
  8.4 1.1 convert_element_type.141.refs_4_.refs_9_
  9.5 1.5 copy-done.4
  12.0 1.3 copy-done.28
  14.4 44.9 %forward_first.1 = (bf16[8,144,1152]{2,1,0:T(8,128)(2,1)S(1)}, bf16[4,256,1152]{2,1,0:T(8,128)(2,1)S(1)}, f32[8,1,2432]{2,1,0:T(1,128)S(1)}, f32[8,144]{1,0:T(8,...) custom-call(bf16[144,1152]{1,0:T(8,128)(2,1)S(1)} %get-tuple-element, ...), custom_call_target="tpu_custom_call" | custom-call | tf_op jit(solution)/shard_map/forward_first/pallas_call | solution.py:493
  59.3 1.3 copy-done
  60.5 1.5 copy-done.8
  66.6 2.8 add_convert_fusion.1.refs_0_.refs_4_
  69.5 71.8 %forward_attention.1 = (bf16[8,144,1152]{2,1,0:T(8,128)(2,1)S(1)}, bf16[8,144,1152]{2,1,0:T(8,128)(2,1)S(1)}, bf16[4,256,1152]{2,1,0:T(8,128)(2,1)S(1)}, bf16[11...) custom-call(bf16[1024,864]{1,0:T(8,128)(2,1)S(1)} %add_convert_fusion.1.refs_0_.refs_4_, ...), custom_call_target="tpu_custom_call" | custom-call | tf_op jit(solution)/shard_map/forward_attention/pallas_call | solution.py:493
  141.3 2.2 fusion.7.refs_2_
  144.2 3.5 fusion.56
  147.7 5.3 %fusion.53 = (f32[1024]{0:T(1024)S(1)}, f32[1024,1152]{1,0:T(8,128)S(1)}, f32[1024,1152]{1,0:T(8,128)}) fusion(f32[1152]{0:T(1024)S(1)} %get-tuple-element.169, bf16[4,256,1152]{2,1,0:T(8,128)(2,1)S(1)} %get-tuple-element.75, f32[1152]{0:T(1024)S(1)} %get-tuple-element.160, bf16[1024,1152]{1,0:T(8,128)(2,1)S(1)} %get-tuple-element.80.refs_2_, ...), kind=kOutput, calls=%fused_computation.146 | convolution fusion | flops 2723806208 | bytes 16823296 | tf_op jit(solution)/shard_map/td,de->te/dot_general | solution.py:69
  153.8 3.1 add_convert_fusion
  156.9 6.5 %convert_reduce_fusion.2 = (f32[1152]{0:T(1024)S(1)}, bf16[1024,1152]{1,0:T(8,128)(2,1)S(1)}, bf16[1024,1152]{1,0:T(8,128)(2,1)S(1)}) fusion(f32[1024,1152]{1,0:T(8,128)S(1)} %fusion.56, f32[1152]{0:T(1024)S(1)} %add.305, bf16[1024,1152]{1,0:T(8,128)(2,1)S(1)} %get-tuple-element.152.refs_3_, bf16[1152,1152]{1,0:T(8,128)(2,1)S(1)} %bitcast.85), kind=kOutput, calls=%fused_computation.23 | convolution fusion | flops 2747399168 | bytes 14459904 | tf_op jit(solution)/shard_map/td,df->tf/dot_general | solution.py:69
  163.4 4.8 %convolution_convert_fusion.1 = bf16[1024,1152]{1,0:T(8,128)(2,1)} fusion(bf16[1024,1152]{1,0:T(8,128)(2,1)S(1)} %get-tuple-element.156.refs_1_, bf16[1152,1152]{1,0:T(8,128)(2,1)S(1)} %bitcast.88), kind=kOutput, calls=%fused_computation.38 | convolution fusion | flops 2719088640 | bytes 7372800 | tf_op jit(solution)/shard_map/tf,fd->td/dot_general | solution.py:69
  168.2 4.8 %convolution_convert_fusion.2 = bf16[1024,1152]{1,0:T(8,128)(2,1)} fusion(bf16[1024,1152]{1,0:T(8,128)(2,1)S(1)} %get-tuple-element.148.refs_4_, bf16[1152,1152]{1,0:T(8,128)(2,1)S(1)} %bitcast.86), kind=kOutput, calls=%fused_computation.39 | convolution fusion | flops 2719088640 | bytes 7372800 | tf_op jit(solution)/shard_map/tf,df->td/dot_general | solution.py:69
  173.3 1.7 copy-done.3
  174.9 1.7 copy-done.19
  176.6 1.7 copy-done.21
  178.3 1.7 copy-done.22
  179.9 21.8 %sum_feed.1 = (f32[256,1152]{1,0:T(8,128)S(1)}, bf16[1152,1152]{1,0:T(8,128)(2,1)S(1)}, bf16[1152,1152]{1,0:T(8,128)(2,1)S(1)}) custom-call(bf16[4,256,1152]{2,1,0:T(8,128)(2,1)S(1)} %bitcast.83, bf16[1024,1152]{1,0:T(8,128)(2,1)S(1)} %copy-done.21, bf16[1024,1152]{1,0:T(8,128)(2,1)S(1)} %copy-done.3, bf16[1024,1152]{1,0:T(8,128)(2,1)S(1)} %get-tuple-element.152.refs_3_, ...), custom_call_target="tpu_custom_call" | custom-call | tf_op jit(solution)/shard_map/sum_feed/pallas_call | solution.py:493
  201.8 2.6 multiply_reduce_fusion.3
  204.4 1.7 convert_reduce_fusion.4
  206.2 1.8 multiply_reduce_fusion.4
  208.1 85.1 %backward_attention.1 = (bf16[144,4608]{1,0:T(8,128)(2,1)S(1)}, bf16[4,144,1152]{2,1,0:T(8,128)(2,1)}, bf16[4,256,1152]{2,1,0:T(8,128)(2,1)}, f32[256,1152]{1,0:...) custom-call(bf16[8,144,1152]{2,1,0:T(8,128)(2,1)} %bitcast.80, bf16[8,144,1152]{2,1,0:T(8,128)(2,1)} %bitcast.79, ...), custom_call_target="tpu_custom_call" | custom-call | tf_op jit(solution)/shard_map/backward_attention/pallas_call | solution.py:493
  293.2 6.2 %convolution_convert_fusion = bf16[1024,1152]{1,0:T(8,128)(2,1)} fusion(bf16[1024,864]{1,0:T(8,128)(2,1)} %get-tuple-element.90.refs_1_, bf16[1152,1152]{1,0:T(8,128)(2,1)S(1)} %bitcast.78), kind=kOutput, calls=%fused_computation.37 | convolution fusion | flops 2039611392 | bytes 6193152 | tf_op jit(solution)/shard_map/te,de->td/dot_general | solution.py:69
  299.4 1.3 multiply_reduce_fusion.2
  301.4 2.7 fusion.23
  304.2 2.5 constant_dynamic-slice_fusion.1.refs_3_
  306.7 1.8 convert_reduce_fusion.3
  309.1 94.0 %backward_last.1 = (bf16[144,3456]{1,0:T(8,128)(2,1)}, bf16[144,1152]{1,0:T(8,128)(2,1)S(1)}, f32[256,1152]{1,0:T(8,128)}, f32[8,1,3200]{2,1,0:T(1,128)S(1)}, f3...) custom-call(bf16[1024,1152]{1,0:T(8,128)(2,1)} %copy-done.32, ...), custom_call_target="tpu_custom_call" | custom-call | tf_op jit(solution)/shard_map/backward_last/pallas_call | solution.py:493
  408.0 1.6 multiply_reduce_fusion.9
  409.7 2.0 multiply_reduce_fusion.8
  411.7 1.4 multiply_reduce_fusion.7
  415.1 4.3 multiply_reduce_fusion.1
  421.4 6.8 %sum_squares.1 = f32[8,128]{1,0:T(8,128)S(1)} custom-call(f32[8,128]{1,0:T(8,128)S(1)} %broadcast_in_dim.65.src), custom_call_target="tpu_custom_call" | custom-call | tf_op jit(solution)/shard_map/sum_squares/pallas_call | solution.py:493
  430.2 1.8 multiply_subtract_fusion.7
  432.0 3.0 multiply_subtract_fusion.6
  435.0 2.9 multiply_subtract_fusion.5
  437.9 1.7 multiply_subtract_fusion.4
  441.2 4.5 multiply_subtract_fusion.3
  445.7 1.3 copy-done.36
  447.7 4.8 %multiply_subtract_fusion.1 = (f32[576,1152]{1,0:T(8,128)}, f32[576,1152]{1,0:T(8,128)}, f32[576,1152]{1,0:T(8,128)}, f32[576,1152]{1,0:T(8,128)}) fusion(f32[576,1152]{1,0:T(8,128)S(1)} %copy-done.35, f32[]{:T(128)S(6)} %div.165, f32[576,1152]{1,0:T(8,128)S(1)} %copy-done.36, f32[576,1152]{1,0:T(8,128)S(1)} %copy-done.37, ...), kind=kLoop, calls=%fused_computation.45 | loop fusion | flops 11280384 | bytes 19906564 | tf_op jit(solution)/shard_map/sub | solution.py:1120
  452.6 7.9 %multiply_subtract_fusion.2 = (f32[144,4608]{1,0:T(8,128)}, f32[144,4608]{1,0:T(8,128)}, f32[144,4608]{1,0:T(8,128)}, f32[144,4608]{1,0:T(8,128)}) fusion(f32[144,4608]{1,0:T(8,128)S(1)} %copy-done.2, f32[]{:T(128)S(6)} %div.165, f32[144,4608]{1,0:T(8,128)} %param.50, f32[144,4608]{1,0:T(8,128)} %param.59, bf16[144,4608]{1,0:T(8,128)(2,1)S(1)} %get-tuple-element.107), kind=kLoop, calls=%fused_computation.47 | loop fusion | flops 11280384 | bytes 19906564 | tf_op jit(solution)/shard_map/sub | solution.py:1120
  460.5 7.9 %multiply_subtract_fusion = (f32[1152,864]{0,1:T(8,128)}, f32[1152,864]{0,1:T(8,128)}, f32[1152,864]{0,1:T(8,128)}) fusion(f32[1152,864]{0,1:T(8,128)S(1)} %copy-done.29, f32[1152,864]{0,1:T(8,128)S(1)} %copy-done.30, f32[]{:T(128)S(6)} %div.165, f32[1152,864]{0,1:T(8,128)} %param.47, f32[1152,864]{0,1:T(8,128)} %param.56), kind=kLoop, calls=%fused_computation.34 | loop fusion | flops 15925248 | bytes 27869188 | tf_op jit(solution)/shard_map/sub | solution.py:1120
  468.4 1.0 copy.107
  (201 shorter events, 18.2 us)
Async XLA Ops:
  0.7 8.8 %copy-start.1 = (f32[144,4608]{1,0:T(8,128)S(1)}, f32[144,4608]{1,0:T(8,128)}, u32[]{:S(2)}) copy-start(f32[144,4608]{1,0:T(8,128)} %up_ref.1) | copy-start | bytes 7962628
  3.7 5.8 %copy-start.13 = (f32[144,1152]{1,0:T(8,128)S(1)}, f32[144,1152]{1,0:T(8,128)}, u32[]{:S(2)}) copy-start(f32[144,1152]{1,0:T(8,128)} %out_ref.1) | copy-start | bytes 1990660
  11.1 2.2 copy-start.28
  66.6 2.8 copy-start.32
  66.6 2.8 copy-start.7
  66.6 2.8 copy-start.23
  66.6 2.8 copy-start.26
  69.4 71.8 %copy-start.6 = (bf16[1024,864]{1,0:T(8,128)(2,1)}, bf16[1024,864]{1,0:T(8,128)(2,1)S(1)}, u32[]{:S(2)}) copy-start(bf16[1024,864]{1,0:T(8,128)(2,1)S(1)} %add_convert_fusion.1.refs_0_.refs_4_) | copy-start | bytes 5308420
  141.2 6.4 %copy-start.17 = (bf16[1024,1152]{1,0:T(8,128)(2,1)}, bf16[1024,1152]{1,0:T(8,128)(2,1)S(1)}, u32[]{:S(2)}) copy-start(bf16[1024,1152]{1,0:T(8,128)(2,1)S(1)} %get-tuple-element.80.refs_2_) | copy-start | bytes 7077892
  144.2 3.6 copy-start.39
  153.1 3.8 copy-start.27
  163.4 4.8 %copy-start.20 = (bf16[1024,1152]{1,0:T(8,128)(2,1)}, bf16[1024,1152]{1,0:T(8,128)(2,1)S(1)}, u32[]{:S(2)}) copy-start(bf16[1024,1152]{1,0:T(8,128)(2,1)S(1)} %get-tuple-element.156.refs_1_) | copy-start | bytes 7077892
  163.4 4.8 %copy-start.18 = (bf16[1024,1152]{1,0:T(8,128)(2,1)}, bf16[1024,1152]{1,0:T(8,128)(2,1)S(1)}, u32[]{:S(2)}) copy-start(bf16[1024,1152]{1,0:T(8,128)(2,1)S(1)} %get-tuple-element.148.refs_4_) | copy-start | bytes 7077892
  201.7 4.4 copy-start.11
  201.8 4.4 copy-start.12
  204.4 3.6 copy-start.56
  206.1 1.9 copy-start.31
  208.0 85.1 %copy-start.10 = (bf16[8,144,1152]{2,1,0:T(8,128)(2,1)S(1)}, bf16[8,144,1152]{2,1,0:T(8,128)(2,1)}, u32[]{:S(2)}) copy-start(bf16[8,144,1152]{2,1,0:T(8,128)(2,1)} %copy-done.8) | copy-start | bytes 7962628
  293.2 6.3 %copy-start.24 = (f32[256,1152]{1,0:T(8,128)}, f32[256,1152]{1,0:T(8,128)S(1)}, u32[]{:S(2)}) copy-start(f32[256,1152]{1,0:T(8,128)S(1)} %get-tuple-element.89) | copy-start | bytes 3538948
  293.2 6.2 %copy-start.33 = (bf16[4,144,1152]{2,1,0:T(8,128)(2,1)S(1)}, bf16[4,144,1152]{2,1,0:T(8,128)(2,1)}, u32[]{:S(2)}) copy-start(bf16[4,144,1152]{2,1,0:T(8,128)(2,1)} %get-tuple-element.100) | copy-start | bytes 3981316
  301.3 7.4 %copy-start.52 = (f32[18432]{0:T(1024)S(1)}, f32[18432]{0:T(1024)}, u32[]{:S(2)}) copy-start(f32[18432]{0:T(1024)} %broadcast_dynamic-update-slice_fusion) | copy-start | bytes 221188
  304.1 5.0 %copy-start.16 = (bf16[1,256,1152]{2,1,0:T(8,128)(2,1)S(1)}, bf16[1,256,1152]{2,1,0:T(8,128)(2,1)}, u32[]{:S(2)}) copy-start(bf16[1,256,1152]{2,1,0:T(8,128)(2,1)} %param.31) | copy-start | bytes 1769476
  309.1 100.6 %copy-start.59 = (f32[8]{0:T(128)S(1)}, f32[8]{0:T(128)}, u32[]{:S(2)}) copy-start(f32[8]{0:T(128)} %slice_reduce_fusion.1) | copy-start | bytes 100
  407.9 21.5 %copy-start.54 = (f32[2304]{0:T(1024)}, f32[2304]{0:T(1024)S(1)}, u32[]{:S(2)}) copy-start(f32[2304]{0:T(1024)S(1)} %get-tuple-element.235) | copy-start | bytes 27652
  409.7 20.5 %copy-start.50 = (f32[32,1152]{1,0:T(8,128)}, f32[32,1152]{1,0:T(8,128)S(1)}, u32[]{:S(2)}) copy-start(f32[32,1152]{1,0:T(8,128)S(1)} %get-tuple-element.227) | copy-start | bytes 442372
  409.7 19.8 %copy-start.53 = (f32[2304]{0:T(1024)S(1)}, f32[2304]{0:T(1024)}, u32[]{:S(2)}) copy-start(f32[2304]{0:T(1024)} %param.43) | copy-start | bytes 27652
  409.7 19.8 %copy-start.57 = (f32[2304]{0:T(1024)S(1)}, f32[2304]{0:T(1024)}, u32[]{:S(2)}) copy-start(f32[2304]{0:T(1024)} %param.52) | copy-start | bytes 27652
  409.7 19.8 %copy-start.58 = (f32[2304]{0:T(1024)S(1)}, f32[2304]{0:T(1024)}, u32[]{:S(2)}) copy-start(f32[2304]{0:T(1024)} %param.61) | copy-start | bytes 27652
  409.7 20.5 %copy-start.49 = (f32[32,1152]{1,0:T(8,128)S(1)}, f32[32,1152]{1,0:T(8,128)}, u32[]{:S(2)}) copy-start(f32[32,1152]{1,0:T(8,128)} %param.35) | copy-start | bytes 442372
  413.0 21.9 %copy-start.38 = (f32[144,1152]{1,0:T(8,128)}, f32[144,1152]{1,0:T(8,128)S(1)}, u32[]{:S(2)}) copy-start(f32[144,1152]{1,0:T(8,128)S(1)} %get-tuple-element.228) | copy-start | bytes 1990660
  413.0 18.9 %copy-start.40 = (f32[1000,144]{0,1:T(8,128)S(1)}, f32[1000,144]{0,1:T(8,128)}, u32[]{:S(2)}) copy-start(f32[1000,144]{0,1:T(8,128)} %param.37) | copy-start | bytes 1728004
  429.5 5.4 %copy-start.45 = (f32[144,1152]{1,0:T(8,128)S(1)}, f32[144,1152]{1,0:T(8,128)}, u32[]{:S(2)}) copy-start(f32[144,1152]{1,0:T(8,128)} %param.45) | copy-start | bytes 1990660
  429.5 5.4 %copy-start.46 = (f32[144,1152]{1,0:T(8,128)S(1)}, f32[144,1152]{1,0:T(8,128)}, u32[]{:S(2)}) copy-start(f32[144,1152]{1,0:T(8,128)} %param.54) | copy-start | bytes 1990660
  434.9 2.9 copy-start.14
  434.9 2.9 copy-start.47
  434.9 2.9 copy-start.48
  435.0 4.6 copy-start.42
  437.8 2.5 copy-start.5
  437.8 3.1 copy-start.41
  437.8 3.4 copy-start.44
  441.2 4.5 copy-start.34
  441.2 4.5 copy-start.35
  441.2 5.8 %copy-start.36 = (f32[576,1152]{1,0:T(8,128)S(1)}, f32[576,1152]{1,0:T(8,128)}, u32[]{:S(2)}) copy-start(f32[576,1152]{1,0:T(8,128)} %param.51) | copy-start | bytes 7962628
  441.2 6.5 %copy-start.37 = (f32[576,1152]{1,0:T(8,128)S(1)}, f32[576,1152]{1,0:T(8,128)}, u32[]{:S(2)}) copy-start(f32[576,1152]{1,0:T(8,128)} %param.60) | copy-start | bytes 7962628
  447.7 4.8 %copy-start.2 = (f32[144,4608]{1,0:T(8,128)S(1)}, f32[144,4608]{1,0:T(8,128)}, u32[]{:S(2)}) copy-start(f32[144,4608]{1,0:T(8,128)} %up_ref.1) | copy-start | bytes 7962628
  452.6 7.9 %copy-start.29 = (f32[1152,864]{0,1:T(8,128)S(1)}, f32[1152,864]{0,1:T(8,128)}, u32[]{:S(2)}) copy-start(f32[1152,864]{0,1:T(8,128)} %param.38) | copy-start | bytes 11943940
  452.6 7.9 %copy-start.30 = (f32[1152,864]{0,1:T(8,128)S(1)}, f32[1152,864]{0,1:T(8,128)}, u32[]{:S(2)}) copy-start(f32[1152,864]{0,1:T(8,128)} %get-tuple-element.230) | copy-start | bytes 11943940
  460.5 7.9 %copy-start.43 = (f32[256,1152]{1,0:T(8,128)S(1)}, f32[256,1152]{1,0:T(8,128)}, u32[]{:S(2)}) copy-start(f32[256,1152]{1,0:T(8,128)} %get-tuple-element.94) | copy-start | bytes 3538948
  (12 other events, 17.4 us)
